TPU v7x, 256 devices: a whole 4x4x8 slice. The times are simulated.
256 devices in a mesh: sec: 2 (over y_hi), row: 64 (over z, x, y_lo), col: 2 (over core).
Axes of the slice: x: 4, y: 4 (y_hi: 2, y_lo: 2; y = y_hi * 2 + y_lo), z: 8, core: 2. Of those that a mesh axis runs over, the one named last changes fastest.
Arguments:
- basis_matrix: bfloat16 [81920, 4096], P('row', 'col'), may hold values from -6 to 6
- operator_blocks: bfloat16 [640, 7, 128, 128], P('row', None, 'sec'), may hold values from -0.1875 to 0.1875
- neighbours: int32 [640, 7], P('row'), may hold values from 0 to 639, as said below
- neighbour_mask: int32 [640, 7], P('row'), may hold values from 0 to 1, as said below
Outputs:
- reduced: float32 [4096, 4096], P(('sec', 'row'), 'col')
Inputs may be any that keep to these rules, and one draw needn't show every extreme that they name: `neighbours`: slot 0 of row block b is b; slots 1 to 4 are b - 1, b + 1, b - 2, b + 2; slots 5 and 6 lie within 2 blocks of b; a slot whose mask is 0 holds b. `neighbour_mask`: 0 exactly where slots 1 to 4 fall outside the slab, and at random in slots 5 and 6 (also where they fall outside); slot 0 is always 1.
All inputs are finite; a program needn't handle non-finite values.
Results may differ from a plain program's by a relative error of at most 0.0029.
Values may be sent and summed in bfloat16 or wider, within the bound.
A program may use at most 192 MiB of HBM per device.

v0:
```python
import functools
import math

import jax
import jax.numpy as jnp
import numpy as np
from jax import lax
from jax.experimental import pallas as pl
from jax.experimental.pallas import tpu as pltpu
from jax.sharding import Mesh
from jax.sharding import PartitionSpec as P

REACH = 2
ROW_PARTS = (("z", 8), ("x", 4), ("y", 2))
ROW = tuple(name for name, _ in ROW_PARTS)
UNIT = 256
ORDERS = ((("z", "x", "y"), 4), (("x", "z", "y"), 4))
TILE_COLUMNS = 1024
STATIC_OFFSETS = (0, -1, 1, -2, 2)
WINDOW_SLOTS = tuple(range(len(STATIC_OFFSETS)))


def halo(shard, width):
    count = 1
    for _, size in ROW_PARTS:
        count *= size
    length = shard.shape[0]
    axes = ("sec",) + ROW

    def index(sec, row):
        return sec * count + row

    after_pairs, before_pairs = [], []
    for sec in range(2):
        for row in range(count):
            other = sec if row % 2 == 0 else 1 - sec
            if row + 1 < count:
                after_pairs.append((index(other, row + 1), index(sec, row)))
            other = 1 - sec if row % 2 == 0 else sec
            if row >= 1:
                before_pairs.append((index(other, row - 1), index(sec, row)))
    before = lax.ppermute(shard[length - width :], axes, before_pairs)
    after = lax.ppermute(shard[:width], axes, after_pairs)
    return jnp.concatenate([before, shard, after], axis=0)


def take_chunk(x, index, dim):
    return lax.dynamic_index_in_dim(x, index, axis=dim, keepdims=False)


def multi_ring_kernel(plan, *refs):
    count = len(plan)
    x_refs, o_refs = refs[:count], refs[count : 2 * count]
    scratch = refs[2 * count :]
    mesh = pl.DeviceIdType.MESH
    rings = []
    for index, (axis, n) in enumerate(plan):
        out_f, in_f, out_b, in_b, send_sem, recv_sem, credit_sem = scratch[7 * index : 7 * index + 7]
        p = lax.axis_index(axis)
        rings.append(
            dict(
                axis=axis, n=n, p=p, x=x_refs[index], o=o_refs[index],
                right=lax.rem(p + 1, n), left=lax.rem(p + n - 1, n),
                out_f=out_f, in_f=in_f, out_b=out_b, in_b=in_b,
                send=send_sem, recv=recv_sem, credit=credit_sem, copies=None,
            )
        )

    barrier = pltpu.get_barrier_semaphore()
    for ring in rings:
        for neighbour in (ring["left"], ring["right"]):
            pl.semaphore_signal(barrier, 1, device_id={ring["axis"]: neighbour}, device_id_type=mesh)
    pl.semaphore_wait(barrier, 2 * count)

    ticks = max(n - 1 for _, n in plan)
    for tick in range(ticks):
        for ring in rings:
            n = ring["n"]
            due = [step for step in range(n - 1) if (step * ticks) // (n - 1) == tick]
            for step in due:
                if ring["copies"] is not None:
                    for copy in ring["copies"]:
                        copy.wait()
                    ring["copies"] = None
                slot = step % 2
                p, x, half = ring["p"], ring["x"], ring["x"].shape[-1] // 2
                chunk_f = lax.rem(p - step - 1 + 2 * n, n)
                chunk_b = lax.rem(p + step + 1, n)
                if step == 0:
                    ring["out_f"][slot] = x[chunk_f, :, :half]
                    ring["out_b"][slot] = x[chunk_b, :, half:]
                else:
                    ring["out_f"][slot] = ring["in_f"][1 - slot] + x[chunk_f, :, :half]
                    ring["out_b"][slot] = ring["in_b"][1 - slot] + x[chunk_b, :, half:]
                    if step <= n - 3:
                        pl.semaphore_signal(
                            ring["credit"].at[0], 1, device_id={ring["axis"]: ring["left"]}, device_id_type=mesh
                        )
                        pl.semaphore_signal(
                            ring["credit"].at[1], 1, device_id={ring["axis"]: ring["right"]}, device_id_type=mesh
                        )
                if step >= 2:
                    pl.semaphore_wait(ring["credit"].at[0], 1)
                    pl.semaphore_wait(ring["credit"].at[1], 1)
                copy_f = pltpu.make_async_remote_copy(
                    src_ref=ring["out_f"].at[slot], dst_ref=ring["in_f"].at[slot],
                    send_sem=ring["send"].at[0, slot], recv_sem=ring["recv"].at[0, slot],
                    device_id={ring["axis"]: ring["right"]}, device_id_type=mesh,
                )
                copy_b = pltpu.make_async_remote_copy(
                    src_ref=ring["out_b"].at[slot], dst_ref=ring["in_b"].at[slot],
                    send_sem=ring["send"].at[1, slot], recv_sem=ring["recv"].at[1, slot],
                    device_id={ring["axis"]: ring["left"]}, device_id_type=mesh,
                )
                copy_f.start()
                copy_b.start()
                ring["copies"] = (copy_f, copy_b)
    for ring in rings:
        for copy in ring["copies"]:
            copy.wait()
        n, p, x = ring["n"], ring["p"], ring["x"]
        half = x.shape[-1] // 2
        last = (n - 2) % 2
        ring["o"][:, :half] = ring["in_f"][last] + x[p, :, :half]
        ring["o"][:, half:] = ring["in_b"][last] + x[p, :, half:]


def multi_ring_reduce(inputs, plan, collective_id):
    vmem = pltpu.VMEM
    scratch = []
    for x in inputs:
        _, rows, width = x.shape
        half = width // 2
        scratch += [vmem((2, rows, half), x.dtype) for _ in range(4)]
        scratch += [
            pltpu.SemaphoreType.DMA((2, 2)),
            pltpu.SemaphoreType.DMA((2, 2)),
            pltpu.SemaphoreType.REGULAR((2,)),
        ]
    return pl.pallas_call(
        functools.partial(multi_ring_kernel, tuple(plan)),
        out_shape=[jax.ShapeDtypeStruct(x.shape[1:], x.dtype) for x in inputs],
        in_specs=[pl.BlockSpec(memory_space=vmem) for _ in inputs],
        out_specs=[pl.BlockSpec(memory_space=vmem) for _ in inputs],
        scratch_shapes=scratch,
        compiler_params=pltpu.CompilerParams(
            collective_id=collective_id, has_side_effects=True, vmem_limit_bytes=60 * 1024 * 1024
        ),
    )(*inputs)


def ring_sum(x, dim, axis, n):
    p = lax.axis_index(axis)
    partner = [(0, 1), (1, 0)]
    got = lax.ppermute(take_chunk(x, 1 - p, dim), axis, partner)
    return got + take_chunk(x, p, dim)


def applied_kernel(offsets_ref, mask_ref, ops_ref, ext_ref, out_ref):
    block = pl.program_id(1)
    slot_count, block_rows = ops_ref.shape[1], ops_ref.shape[2]
    order = [slot for _, slot in sorted(zip(STATIC_OFFSETS, WINDOW_SLOTS))]
    lhs = jnp.concatenate(
        [
            jnp.where(mask_ref[block * slot_count + slot] != 0, ops_ref[0, slot], 0)
            for slot in order
        ],
        axis=1,
    )
    first = pl.multiple_of(block * block_rows, block_rows)
    acc = jnp.dot(
        lhs, ext_ref[pl.ds(first, len(order) * block_rows), :], preferred_element_type=jnp.float32
    )
    for slot in range(len(WINDOW_SLOTS), slot_count):
        tile_index = offsets_ref[block * slot_count + slot]
        start = pl.multiple_of(tile_index * block_rows, block_rows)
        tile = ext_ref[pl.ds(start, block_rows), :]
        product = jnp.dot(ops_ref[0, slot], tile, preferred_element_type=jnp.float32)
        live = mask_ref[block * slot_count + slot] != 0
        acc = acc + jnp.where(live, product, 0.0)
    out_ref[...] = acc.astype(out_ref.dtype)


def apply_operator(offsets, mask, full_ops, extended, column_start, column_count):
    block_count, slot_count, block_rows, _ = full_ops.shape
    ext_rows = extended.shape[0]
    tile = min(TILE_COLUMNS, column_count)
    skip = column_start // tile
    grid_spec = pltpu.PrefetchScalarGridSpec(
        num_scalar_prefetch=2,
        grid=(column_count // tile, block_count),
        in_specs=[
            pl.BlockSpec((1, slot_count, block_rows, block_rows), lambda j, b, *_: (b, 0, 0, 0)),
            pl.BlockSpec((ext_rows, tile), lambda j, b, *_: (0, j + skip)),
        ],
        out_specs=pl.BlockSpec((block_rows, tile), lambda j, b, *_: (b, j)),
    )
    flops = 2 * block_count * slot_count * block_rows * block_rows * column_count
    return pl.pallas_call(
        applied_kernel,
        grid_spec=grid_spec,
        out_shape=jax.ShapeDtypeStruct((block_count * block_rows, column_count), jnp.bfloat16),
        compiler_params=pltpu.CompilerParams(dimension_semantics=("arbitrary", "arbitrary")),
        cost_estimate=pl.CostEstimate(
            flops=flops, bytes_accessed=3 * ext_rows * column_count * 2, transcendentals=0
        ),
    )(offsets, mask, full_ops, extended)


def per_device(basis_matrix, operator_blocks, neighbours, neighbour_mask):
    local_rows, column_count = basis_matrix.shape
    block_count, slot_count, half_rows, block_rows = operator_blocks.shape
    sec = lax.axis_index("sec")
    col = lax.axis_index("col")
    row = 0
    for name, size in ROW_PARTS:
        row = row * size + lax.axis_index(name)

    share = block_count // 2
    mine = lax.dynamic_slice_in_dim(operator_blocks, col * share, share, 0)
    from_sec = lax.ppermute(mine, "sec", [(0, 1), (1, 0)])
    from_col = lax.ppermute(from_sec, "col", [(0, 1), (1, 0)])
    other_half = jnp.where(
        col == 0,
        jnp.concatenate([from_sec, from_col], axis=0),
        jnp.concatenate([from_col, from_sec], axis=0),
    )
    first = jnp.where(sec == 0, operator_blocks, other_half)
    second = jnp.where(sec == 0, other_half, operator_blocks)
    full_ops = jnp.concatenate([first, second], axis=2)

    other_basis = lax.ppermute(basis_matrix, "col", [(0, 1), (1, 0)])
    left_projector = jnp.where(sec == col, basis_matrix, other_basis)

    extended = halo(basis_matrix, REACH * block_rows)
    offsets = jnp.clip(neighbours - row * block_count + REACH, 0, block_count + 2 * REACH - 1)
    row_count = 1
    for _, size in ROW_PARTS:
        row_count *= size
    scaling = 1.0 / math.sqrt(local_rows * row_count)
    chunk_rows = left_projector.shape[1] // row_count
    sizes = dict(ROW_PARTS)
    parts, names, start = [], [], 0
    for order, units in ORDERS:
        width = units * UNIT
        applied = apply_operator(
            offsets.reshape(-1), neighbour_mask.reshape(-1), full_ops, extended, start, width
        )
        start += width
        part = scaling * lax.dot_general(
            left_projector, applied, (((0,), (0,)), ((), ())), preferred_element_type=jnp.float32
        )
        parts.append(part.reshape(tuple(size for _, size in ROW_PARTS) + (chunk_rows, width)))
        names.append(list(ROW))
    for stage in range(len(ROW_PARTS)):
        axes = [order[stage] for order, _ in ORDERS]
        if sizes[axes[0]] == 2:
            for index, axis in enumerate(axes):
                dim = names[index].index(axis)
                parts[index] = ring_sum(parts[index], dim, axis, 2)
                names[index].remove(axis)
            continue
        inputs, shapes = [], []
        for index, axis in enumerate(axes):
            dim = names[index].index(axis)
            x = parts[index]
            shapes.append(x.shape[:dim] + x.shape[dim + 1 :])
            inputs.append(jnp.moveaxis(x, dim, 0).reshape(sizes[axis], -1, x.shape[-1]))
            names[index].remove(axis)
        outs = multi_ring_reduce(inputs, [(axis, sizes[axis]) for axis in axes], stage)
        parts = [out.reshape(shape) for out, shape in zip(outs, shapes)]
    pieces = parts
    return jnp.concatenate(pieces, axis=-1)


def solution(mesh):
    sizes = [mesh.shape["sec"]] + [size for _, size in ROW_PARTS] + [mesh.shape["col"]]
    fine = Mesh(np.asarray(mesh.devices).reshape(sizes), ("sec",) + ROW + ("col",))
    return jax.shard_map(
        per_device,
        mesh=fine,
        in_specs=(P(ROW, "col"), P(ROW, None, "sec", None), P(ROW, None), P(ROW, None)),
        out_specs=P(("sec",) + ROW, "col"),
        check_vma=False,
    )
```

profile of v0, /device:TPU:8, one launch (start us, length us, event | category | flops | bytes accessed | tf_op | source)
XLA Modules:
  0.0 255.9 jit_solution(16680495269761113521)
XLA Ops:
  0.0 0.0 copy-start.3
  0.0 0.0 copy-start.2
  0.0 0.0 collective-permute-start
  0.0 2.7 %fusion = (bf16[256,2048]{1,0:T(8,128)(2,1)S(1)}, bf16[256,2048]{1,0:T(8,128)(2,1)}) fusion(bf16[1280,2048]{1,0:T(8,128)(2,1)} %param.4), kind=kLoop, calls=%fused_computation.17 | loop fusion | bytes 4194304 | tf_op jit(solution)/shard_map/slice | solution.py:43
  2.7 4.4 %collective-permute-start.3 = (bf16[256,2048]{1,0:T(8,128)(2,1)}, bf16[256,2048]{1,0:T(8,128)(2,1)S(1)}, u32[]{:S(2)}, u32[]{:S(2)}) collective-permute-start(bf16[256,2048]{1,0:T(8,128)(2,1)} %get-tuple-element.14), channel_id=1, source_target_pairs={{0,2},{130,4},{4,6},{134,8},{8,10},{138,12},{12,14},{142,16},{16,1... | collective-permute-start | bytes 3145736 | tf_op jit(solution)/shard_map/ppermute | solution.py:42
  7.2 1.9 constant_dynamic-slice_fusion
  9.1 0.9 collective-permute-start.1
  10.0 3.4 %collective-permute-start.4 = (bf16[256,2048]{1,0:T(8,128)(2,1)S(1)}, bf16[256,2048]{1,0:T(8,128)(2,1)S(1)}, u32[]{:S(2)}, u32[]{:S(2)}) collective-permute-start(bf16[256,2048]{1,0:T(8,128)(2,1)S(1)} %get-tuple-element.13), channel_id=1, source_target_pairs={{2,0},{132,2},{6,4},{136,6},{10,8},{140,10},{14,12},{144,14},{18,1... | collective-permute-start | bytes 3145736 | tf_op jit(solution)/shard_map/ppermute | solution.py:43
  13.5 0.0 copy-done.3
  13.5 0.1 copy.8
  13.6 0.6 reshape.20.offsets_ref
  14.2 0.0 copy-done.2
  14.2 0.1 copy.9
  14.3 0.6 reshape.21.mask_ref
  14.9 21.6 %collective-permute-done.1 = bf16[5,7,64,128]{3,2,1,0:T(8,128)(2,1)} collective-permute-done((bf16[5,7,64,128]{3,2,1,0:T(8,128)(2,1)}, bf16[5,7,64,128]{3,2,1,0:T(8,128)(2,1)}, u32[]{:S(2)}, u32[]{:S(2)}) %collective-permute-start.1) | collective-permute-done | bytes 573472 | tf_op jit(solution)/shard_map/ppermute | solution.py:221
  36.6 0.0 collective-permute-start.2
  36.6 0.0 collective-permute-done.3
  36.6 1.1 constant_dynamic-update-slice_fusion.2
  37.6 0.0 copy-start.1
  37.6 5.8 %constant_dynamic-update-slice_fusion.1 = bf16[1792,2048]{1,0:T(8,128)(2,1)} fusion(bf16[1792,2048]{1,0:T(8,128)(2,1)} %constant_dynamic-update-slice_fusion.2, bf16[1280,2048]{1,0:T(8,128)(2,1)} %param.4), kind=kLoop, calls=%fused_computation.13 | loop fusion | bytes 10485760
  43.4 7.9 %collective-permute-done.4 = bf16[256,2048]{1,0:T(8,128)(2,1)S(1)} collective-permute-done((bf16[256,2048]{1,0:T(8,128)(2,1)S(1)}, bf16[256,2048]{1,0:T(8,128)(2,1)S(1)}, u32[]{:S(2)}, u32[]{:S(2)}) %collective-permute-start.4) | collective-permute-done | bytes 1048608 | tf_op jit(solution)/shard_map/ppermute | solution.py:43
  51.3 1.1 constant_dynamic-update-slice_fusion.ext_ref
  52.3 0.0 collective-permute-done.2
  52.3 0.0 copy-done.1
  52.3 1.5 broadcast_select_fusion.4
  53.8 1.6 pad_maximum_fusion.ops_ref
  55.4 10.9 %shard_map.47 = bf16[1280,1024]{1,0:T(8,128)(2,1)} custom-call(s32[70]{0:T(128)} %reshape.20.offsets_ref, s32[70]{0:T(128)} %reshape.21.mask_ref, bf16[10,7,128,128]{3,2,1,0:T(8,128)(2,1)} %pad_maximum_fusion.ops_ref, bf16[1792,2048]{1,0:T(8,128)(2,1)} %constant_dynamic-update-slice_fusion.ext_ref), custom_call_target="tpu_custom_call" | custom-call | flops 2348810240 | bytes 11010048 | tf_op jit(solution)/shard_map/pallas_call | solution.py:199
  66.4 0.0 slice-start
  66.4 11.1 %shard_map.46 = bf16[1280,1024]{1,0:T(8,128)(2,1)} custom-call(s32[70]{0:T(128)} %reshape.20.offsets_ref, s32[70]{0:T(128)} %reshape.21.mask_ref, bf16[10,7,128,128]{3,2,1,0:T(8,128)(2,1)} %pad_maximum_fusion.ops_ref, bf16[1792,2048]{1,0:T(8,128)(2,1)} %constant_dynamic-update-slice_fusion.ext_ref), custom_call_target="tpu_custom_call" | custom-call | flops 2348810240 | bytes 11010048 | tf_op jit(solution)/shard_map/pallas_call | solution.py:199
  77.5 0.0 slice-start.1
  77.5 0.0 collective-permute-done
  77.5 9.0 %convolution_multiply_fusion = f32[2048,1024]{1,0:T(8,128)S(1)} fusion(bf16[1280,1024]{1,0:T(8,128)(2,1)} %shard_map.47, bf16[1280,2048]{1,0:T(8,128)(2,1)} %param.4, bf16[1280,2048]{1,0:T(8,128)(2,1)} %collective-permute-done, pred[]{:T(512)S(6)} %eq.10), kind=kOutput, calls=%fused_computation.1 | convolution fusion | flops 5373427712 | bytes 21495808 | tf_op jit(solution)/shard_map/dot_general | solution.py:250
  86.5 0.0 copy-start
  86.5 4.1 %copy.10 = f32[8,4,2,32,1024]{4,3,2,0,1:T(8,128)} copy(f32[8,4,2,32,1024]{4,3,2,1,0:T(8,128)S(1)} %bitcast.23) | data formatting | bytes 16777216 | tf_op jit(solution)/shard_map/reshape | solution.py:253
  90.6 0.0 slice-done
  90.6 0.0 slice-done.1
  90.6 0.0 copy-done
  90.6 8.3 %convolution_multiply_fusion.1 = f32[2048,1024]{1,0:T(8,128)} fusion(bf16[1280,1024]{1,0:T(8,128)(2,1)S(1)} %copy-done, bf16[1280,2048]{1,0:T(8,128)(2,1)S(1)} %bitcast.21, bf16[1280,2048]{1,0:T(8,128)(2,1)} %collective-permute-done, pred[]{:T(512)S(6)} %eq.10), kind=kOutput, calls=%fused_computation.2 | convolution fusion | flops 5373427712 | bytes 21495808 | tf_op jit(solution)/shard_map/dot_general | solution.py:250
  99.0 105.6 %shard_map.48 = (f32[256,1024]{1,0:T(8,128)}, f32[512,1024]{1,0:T(8,128)}) custom-call(f32[8,256,1024]{2,1,0:T(8,128)} %bitcast.22, f32[4,512,1024]{2,1,0:T(8,128)} %bitcast.19), custom_call_target="tpu_custom_call" | custom-call | tf_op jit(solution)/shard_map/pallas_call | solution.py:140
  204.6 40.1 %shard_map.49 = (f32[64,1024]{1,0:T(8,128)}, f32[64,1024]{1,0:T(8,128)}) custom-call(f32[4,64,1024]{2,1,0:T(8,128)} %bitcast.25, f32[8,64,1024]{2,1,0:T(8,128)} %bitcast.24), custom_call_target="tpu_custom_call" | custom-call | tf_op jit(solution)/shard_map/pallas_call | solution.py:140
  244.7 0.9 dynamic-slice_bitcast_fusion.1
  245.6 2.7 %collective-permute-start.5 = (f32[32,1024]{1,0:T(8,128)S(1)}, f32[32,1024]{1,0:T(8,128)S(1)}, u32[]{:S(2)}, u32[]{:S(2)}) collective-permute-start(f32[32,1024]{1,0:T(8,128)S(1)} %dynamic-slice_bitcast_fusion.1), channel_id=1, source_target_pairs={{0,2},{2,0},{1,3},{3,1},{4,6},{6,4},{5,7},{7,5},{8,10},{10,8},{9,1... | collective-permute-start | bytes 393224 | tf_op jit(solution)/shard_map/ppermute | solution.py:155
  248.3 0.9 dynamic-slice_bitcast_fusion
  249.2 0.1 collective-permute-start.6
  249.3 1.9 collective-permute-done.5
  251.2 0.9 bitcast_add_fusion.1
  252.2 2.1 collective-permute-done.6
  254.3 0.9 bitcast_add_fusion
  255.2 0.7 pad_maximum_fusion.1
  (2 shorter events, 0.0 us)
Async XLA Ops:
  0.0 13.5 %copy-start.3 = (s32[10,7]{0,1:T(8,128)S(1)}, s32[10,7]{0,1:T(8,128)}, u32[]{:S(2)}) copy-start(s32[10,7]{0,1:T(8,128)} %param.6) | copy-start | bytes 844
  0.0 14.2 %copy-start.2 = (s32[10,7]{0,1:T(8,128)S(1)}, s32[10,7]{0,1:T(8,128)}, u32[]{:S(2)}) copy-start(s32[10,7]{0,1:T(8,128)} %param.7) | copy-start | bytes 844
  0.0 77.5 %collective-permute-start = (bf16[1280,2048]{1,0:T(8,128)(2,1)}, bf16[1280,2048]{1,0:T(8,128)(2,1)}, u32[]{:S(2)}, u32[]{:S(2)}) collective-permute-start(bf16[1280,2048]{1,0:T(8,128)(2,1)} %param.4), channel_id=1, source_target_pairs={{0,1},{1,0},{2,3},{3,2},{4,5},{5,4},{6,7},{7,6},{8,9},{9,8},{10,11... | collective-permute-start | bytes 15728648 | tf_op jit(solution)/shard_map/ppermute | solution.py:232
  2.7 33.8 %collective-permute-start.3 = (bf16[256,2048]{1,0:T(8,128)(2,1)}, bf16[256,2048]{1,0:T(8,128)(2,1)S(1)}, u32[]{:S(2)}, u32[]{:S(2)}) collective-permute-start(bf16[256,2048]{1,0:T(8,128)(2,1)} %get-tuple-element.14), channel_id=1, source_target_pairs={{0,2},{130,4},{4,6},{134,8},{8,10},{138,12},{12,14},{142,16},{16,1... | collective-permute-start | bytes 3145736 | tf_op jit(solution)/shard_map/ppermute | solution.py:42
  9.1 27.5 %collective-permute-start.1 = (bf16[5,7,64,128]{3,2,1,0:T(8,128)(2,1)}, bf16[5,7,64,128]{3,2,1,0:T(8,128)(2,1)}, u32[]{:S(2)}, u32[]{:S(2)}) collective-permute-start(bf16[5,7,64,128]{3,2,1,0:T(8,128)(2,1)} %constant_dynamic-slice_fusion), channel_id=1, source_target_pairs={{0,128},{128,0},{1,129},{129,1},{2,130},{130,2},{3,131},{131,3},{4... | collective-permute-start | bytes 1720328 | tf_op jit(solution)/shard_map/ppermute | solution.py:221
  10.0 41.2 %collective-permute-start.4 = (bf16[256,2048]{1,0:T(8,128)(2,1)S(1)}, bf16[256,2048]{1,0:T(8,128)(2,1)S(1)}, u32[]{:S(2)}, u32[]{:S(2)}) collective-permute-start(bf16[256,2048]{1,0:T(8,128)(2,1)S(1)} %get-tuple-element.13), channel_id=1, source_target_pairs={{2,0},{132,2},{6,4},{136,6},{10,8},{140,10},{14,12},{144,14},{18,1... | collective-permute-start | bytes 3145736 | tf_op jit(solution)/shard_map/ppermute | solution.py:43
  36.6 15.8 %collective-permute-start.2 = (bf16[5,7,64,128]{3,2,1,0:T(8,128)(2,1)}, bf16[5,7,64,128]{3,2,1,0:T(8,128)(2,1)S(1)}, u32[]{:S(2)}, u32[]{:S(2)}) collective-permute-start(bf16[5,7,64,128]{3,2,1,0:T(8,128)(2,1)} %collective-permute-done.1), channel_id=1, source_target_pairs={{0,1},{1,0},{2,3},{3,2},{4,5},{5,4},{6,7},{7,6},{8,9},{9,8},{10,11... | collective-permute-start | bytes 1720328 | tf_op jit(solution)/shard_map/ppermute | solution.py:222
  37.6 14.7 %copy-start.1 = (bf16[10,7,64,128]{3,2,1,0:T(8,128)(2,1)S(1)}, bf16[10,7,64,128]{3,2,1,0:T(8,128)(2,1)}, u32[]{:S(2)}) copy-start(bf16[10,7,64,128]{3,2,1,0:T(8,128)(2,1)} %param.5) | copy-start | bytes 3440644
  66.4 24.3 %slice-start = ((s8[5242880]{0:T(1024)(128)(4,1)}), s8[1048576]{0:T(1024)(128)(4,1)S(1)}, s32[]{:S(2)}) async-start(s8[5242880]{0:T(1024)(128)(4,1)} %bitcast.20), calls=%async_computation | async-start | bytes 2097152
  77.5 13.2 %slice-start.1 = ((s8[5242880]{0:T(1024)(128)(4,1)}), s8[4194304]{0:T(1024)(128)(4,1)S(1)}, s32[]{:S(2)}) async-start(s8[5242880]{0:T(1024)(128)(4,1)} %bitcast.20), calls=%async_computation.1 | async-start | bytes 8388608
  86.5 4.1 %copy-start = (bf16[1280,1024]{1,0:T(8,128)(2,1)S(1)}, bf16[1280,1024]{1,0:T(8,128)(2,1)}, u32[]{:S(2)}) copy-start(bf16[1280,1024]{1,0:T(8,128)(2,1)} %shard_map.46) | copy-start | bytes 7864324
  245.6 5.7 %collective-permute-start.5 = (f32[32,1024]{1,0:T(8,128)S(1)}, f32[32,1024]{1,0:T(8,128)S(1)}, u32[]{:S(2)}, u32[]{:S(2)}) collective-permute-start(f32[32,1024]{1,0:T(8,128)S(1)} %dynamic-slice_bitcast_fusion.1), channel_id=1, source_target_pairs={{0,2},{2,0},{1,3},{3,1},{4,6},{6,4},{5,7},{7,5},{8,10},{10,8},{9,1... | collective-permute-start | bytes 393224 | tf_op jit(solution)/shard_map/ppermute | solution.py:155
  249.2 5.1 %collective-permute-start.6 = (f32[32,1024]{1,0:T(8,128)S(1)}, f32[32,1024]{1,0:T(8,128)S(1)}, u32[]{:S(2)}, u32[]{:S(2)}) collective-permute-start(f32[32,1024]{1,0:T(8,128)S(1)} %dynamic-slice_bitcast_fusion), channel_id=1, source_target_pairs={{0,2},{2,0},{1,3},{3,1},{4,6},{6,4},{5,7},{7,5},{8,10},{10,8},{9,1... | collective-permute-start | bytes 393224 | tf_op jit(solution)/shard_map/ppermute | solution.py:155
where the time goes:
time: 258 us; the launch traced here: 256 us
  Pallas kernels  168 us (65%)
  waiting for transfers between devices  33.6 us (13%)
  local copies, waits for them, and re-layouts  19.9 us (8%)
  matrix products  17.3 us (7%)
  starting transfers between devices  11.6 us (4%)
  other arithmetic  5.65 us (2%)
    pallas_call x2, Pallas kernels, multi_ring_reduce(): pl.pallas_call(functools.partial(multi_ring_kernel, tuple(plan)), out_sha...  146 us
    pallas_call x2, Pallas kernels, apply_operator(): pl.pallas_call(applied_kernel, grid_spec=grid_spec, out_shape=jax.ShapeDt...  22.1 us
    ppermute x1, waiting for transfers between devices, per_device(): from_sec = lax.ppermute(mine, 'sec', [(0, 1), (1, 0)])  21.6 us
    dot_general x2, matrix products, per_device(): lax.dot_general(left_projector, applied, (((0,), (0,)), ((), ())), prefer...  17.3 us
    ppermute x1, waiting for transfers between devices, halo(): after = lax.ppermute(shard[:width], axes, after_pairs)  7.88 us
    unnamed x15, local copies, waits for them, and re-layouts  6.95 us
  transfers between devices with their start and end apart: 7, of which 4 were waited for; matrix products, arithmetic and copies ran while one was open for 7% of the time, Pallas kernels for 9%

commit v1 on v0

--- a/solution.py
+++ b/solution.py
@@ -14,7 +14,7 @@
 ROW_PARTS = (("z", 8), ("x", 4), ("y", 2))
 ROW = tuple(name for name, _ in ROW_PARTS)
 UNIT = 256
-ORDERS = ((("z", "x", "y"), 4), (("x", "z", "y"), 4))
+ORDERS = ((("x", "z", "y"), 5), (("z", "x", "y"), 3))
 TILE_COLUMNS = 1024
 STATIC_OFFSETS = (0, -1, 1, -2, 2)
 WINDOW_SLOTS = tuple(range(len(STATIC_OFFSETS)))
@@ -184,7 +184,11 @@
 def apply_operator(offsets, mask, full_ops, extended, column_start, column_count):
     block_count, slot_count, block_rows, _ = full_ops.shape
     ext_rows = extended.shape[0]
-    tile = min(TILE_COLUMNS, column_count)
+    tile = max(
+        size
+        for size in range(128, TILE_COLUMNS + 1, 128)
+        if column_count % size == 0 and column_start % size == 0
+    )
     skip = column_start // tile
     grid_spec = pltpu.PrefetchScalarGridSpec(
         num_scalar_prefetch=2,

time: 258 us -> 285 us (1.10); the launches traced: 256 us -> 280 us
  Pallas kernels: 168 us -> 187 us
    pallas_call x2, Pallas kernels: 22.1 us -> 39.9 us  [apply_operator(): pl.pallas_call(applied_kernel, grid_spec=grid_spec, out_shape=jax.ShapeDt...]
    unnamed x15 -> x11, local copies, waits for them, and re-layouts: 6.95 us -> 6.92 us
  transfers between devices with their start and end apart: 7 -> 7, of which waited for: 4 -> 4; matrix products, arithmetic and copies ran while one was open for 7% -> 7% of each run, Pallas kernels for 9% -> 14%
where the time goes in v1:
time: 285 us; the launch traced here: 280 us
  Pallas kernels  187 us (66%)
  waiting for transfers between devices  33.9 us (12%)
  local copies, waits for them, and re-layouts  20.5 us (7%)
  matrix products  20 us (7%)
  starting transfers between devices  12.6 us (4%)
  other arithmetic  5.67 us (2%)
    pallas_call x2, Pallas kernels, multi_ring_reduce(): pl.pallas_call(functools.partial(multi_ring_kernel, tuple(plan)), out_sha...  147 us
    pallas_call x2, Pallas kernels, apply_operator(): pl.pallas_call(applied_kernel, grid_spec=grid_spec, out_shape=jax.ShapeDt...  39.9 us
    ppermute x1, waiting for transfers between devices, per_device(): from_sec = lax.ppermute(mine, 'sec', [(0, 1), (1, 0)])  21.6 us
    dot_general x2, matrix products, per_device(): lax.dot_general(left_projector, applied, (((0,), (0,)), ((), ())), prefer...  20 us
    ppermute x1, waiting for transfers between devices, halo(): after = lax.ppermute(shard[:width], axes, after_pairs)  7.9 us
    unnamed x11, local copies, waits for them, and re-layouts  6.92 us
  transfers between devices with their start and end apart: 7, of which 4 were waited for; matrix products, arithmetic and copies ran while one was open for 7% of the time, Pallas kernels for 14%

profile of v1, /device:TPU:8, one launch (start us, length us, event | category | flops | bytes accessed | tf_op | source)
XLA Modules:
  0.0 279.7 jit_solution(3633908630672545373)
XLA Ops:
  0.0 0.0 copy-start.3
  0.0 0.0 copy-start.2
  0.0 0.0 collective-permute-start
  0.0 2.7 fusion
  2.7 4.4 %collective-permute-start.3 = (bf16[256,2048]{1,0:T(8,128)(2,1)}, bf16[256,2048]{1,0:T(8,128)(2,1)S(1)}, u32[]{:S(2)}, u32[]{:S(2)}) collective-permute-start(bf16[256,2048]{1,0:T(8,128)(2,1)} %get-tuple-element.14), channel_id=1, source_target_pairs={{0,2},{130,4},{4,6},{134,8},{8,10},{138,12},{12,14},{142,16},{16,1... | collective-permute-start | bytes 3145736 | tf_op jit(solution)/shard_map/ppermute | solution.py:42
  7.2 1.9 constant_dynamic-slice_fusion
  9.1 0.9 collective-permute-start.1
  10.0 3.4 %collective-permute-start.4 = (bf16[256,2048]{1,0:T(8,128)(2,1)S(1)}, bf16[256,2048]{1,0:T(8,128)(2,1)S(1)}, u32[]{:S(2)}, u32[]{:S(2)}) collective-permute-start(bf16[256,2048]{1,0:T(8,128)(2,1)S(1)} %get-tuple-element.13), channel_id=1, source_target_pairs={{2,0},{132,2},{6,4},{136,6},{10,8},{140,10},{14,12},{144,14},{18,1... | collective-permute-start | bytes 3145736 | tf_op jit(solution)/shard_map/ppermute | solution.py:43
  13.5 0.0 copy-done.3
  13.5 0.1 copy.8
  13.6 0.6 reshape.20.offsets_ref
  14.2 0.0 copy-done.2
  14.2 0.1 copy.9
  14.3 0.6 reshape.21.mask_ref
  14.9 21.6 %collective-permute-done.1 = bf16[5,7,64,128]{3,2,1,0:T(8,128)(2,1)} collective-permute-done((bf16[5,7,64,128]{3,2,1,0:T(8,128)(2,1)}, bf16[5,7,64,128]{3,2,1,0:T(8,128)(2,1)}, u32[]{:S(2)}, u32[]{:S(2)}) %collective-permute-start.1) | collective-permute-done | bytes 573472 | tf_op jit(solution)/shard_map/ppermute | solution.py:225
  36.6 0.0 collective-permute-start.2
  36.6 0.0 collective-permute-done.3
  36.6 1.1 constant_dynamic-update-slice_fusion.2
  37.6 0.0 copy-start
  37.6 5.8 %constant_dynamic-update-slice_fusion.1 = bf16[1792,2048]{1,0:T(8,128)(2,1)} fusion(bf16[1792,2048]{1,0:T(8,128)(2,1)} %constant_dynamic-update-slice_fusion.2, bf16[1280,2048]{1,0:T(8,128)(2,1)} %param.4), kind=kLoop, calls=%fused_computation.13 | loop fusion | bytes 10485760
  43.4 7.9 %collective-permute-done.4 = bf16[256,2048]{1,0:T(8,128)(2,1)S(1)} collective-permute-done((bf16[256,2048]{1,0:T(8,128)(2,1)S(1)}, bf16[256,2048]{1,0:T(8,128)(2,1)S(1)}, u32[]{:S(2)}, u32[]{:S(2)}) %collective-permute-start.4) | collective-permute-done | bytes 1048608 | tf_op jit(solution)/shard_map/ppermute | solution.py:43
  51.3 1.1 constant_dynamic-update-slice_fusion.ext_ref
  52.4 0.0 collective-permute-done.2
  52.4 0.0 copy-done
  52.4 1.5 broadcast_select_fusion.4
  53.8 1.6 pad_maximum_fusion.ops_ref
  55.5 21.8 %shard_map.47 = bf16[1280,768]{1,0:T(8,128)(2,1)} custom-call(s32[70]{0:T(128)} %reshape.20.offsets_ref, s32[70]{0:T(128)} %reshape.21.mask_ref, bf16[10,7,128,128]{3,2,1,0:T(8,128)(2,1)} %pad_maximum_fusion.ops_ref, bf16[1792,2048]{1,0:T(8,128)(2,1)} %constant_dynamic-update-slice_fusion.ext_ref), custom_call_target="tpu_custom_call" | custom-call | flops 1761607680 | bytes 8257536 | tf_op jit(solution)/shard_map/pallas_call | solution.py:203
  77.2 18.2 %shard_map.46 = bf16[1280,1280]{1,0:T(8,128)(2,1)} custom-call(s32[70]{0:T(128)} %reshape.20.offsets_ref, s32[70]{0:T(128)} %reshape.21.mask_ref, bf16[10,7,128,128]{3,2,1,0:T(8,128)(2,1)} %pad_maximum_fusion.ops_ref, bf16[1792,2048]{1,0:T(8,128)(2,1)} %constant_dynamic-update-slice_fusion.ext_ref), custom_call_target="tpu_custom_call" | custom-call | flops 2936012800 | bytes 13762560 | tf_op jit(solution)/shard_map/pallas_call | solution.py:203
  95.4 0.0 collective-permute-done
  95.4 10.3 %convolution_multiply_fusion = f32[2048,1280]{1,0:T(8,128)S(1)} fusion(bf16[1280,1280]{1,0:T(8,128)(2,1)} %shard_map.46, bf16[1280,2048]{1,0:T(8,128)(2,1)} %param.4, bf16[1280,2048]{1,0:T(8,128)(2,1)} %collective-permute-done, pred[]{:T(512)S(6)} %eq.10), kind=kOutput, calls=%fused_computation | convolution fusion | flops 6716129280 | bytes 24248320 | tf_op jit(solution)/shard_map/dot_general | solution.py:254
  105.7 0.0 copy-start.1
  105.7 4.7 %copy.10 = f32[8,4,2,32,1280]{4,3,2,0,1:T(8,128)} copy(f32[8,4,2,32,1280]{4,3,2,1,0:T(8,128)S(1)} %bitcast.20) | data formatting | bytes 20971520 | tf_op jit(solution)/shard_map/reshape | solution.py:257
  110.4 0.0 copy-done.1
  110.4 9.7 %convolution_multiply_fusion.1 = f32[2048,768]{1,0:T(8,128)} fusion(bf16[1280,768]{1,0:T(8,128)(2,1)S(1)} %copy-done.1, bf16[1280,2048]{1,0:T(8,128)(2,1)} %param.4, bf16[1280,2048]{1,0:T(8,128)(2,1)} %collective-permute-done, pred[]{:T(512)S(6)} %eq.10), kind=kOutput, calls=%fused_computation.2 | convolution fusion | flops 4030726144 | bytes 18743296 | tf_op jit(solution)/shard_map/dot_general | solution.py:254
  120.1 101.4 %shard_map.48 = (f32[512,1280]{1,0:T(8,128)}, f32[256,768]{1,0:T(8,128)}) custom-call(f32[4,512,1280]{2,1,0:T(8,128)} %bitcast.19, f32[8,256,768]{2,1,0:T(8,128)} %bitcast.21), custom_call_target="tpu_custom_call" | custom-call | tf_op jit(solution)/shard_map/pallas_call | solution.py:140
  221.5 45.5 %shard_map.49 = (f32[64,1280]{1,0:T(8,128)}, f32[64,768]{1,0:T(8,128)}) custom-call(f32[8,64,1280]{2,1,0:T(8,128)} %bitcast.22, f32[4,64,768]{2,1,0:T(8,128)} %bitcast.23), custom_call_target="tpu_custom_call" | custom-call | tf_op jit(solution)/shard_map/pallas_call | solution.py:140
  267.0 0.9 dynamic-slice_bitcast_fusion.1
  268.0 3.7 %collective-permute-start.6 = (f32[32,768]{1,0:T(8,128)S(1)}, f32[32,768]{1,0:T(8,128)S(1)}, u32[]{:S(2)}, u32[]{:S(2)}) collective-permute-start(f32[32,768]{1,0:T(8,128)S(1)} %dynamic-slice_bitcast_fusion.1), channel_id=1, source_target_pairs={{0,2},{2,0},{1,3},{3,1},{4,6},{6,4},{5,7},{7,5},{8,10},{10,8},{9,1... | collective-permute-start | bytes 294920 | tf_op jit(solution)/shard_map/ppermute | solution.py:155
  271.7 0.9 dynamic-slice_bitcast_fusion
  272.6 0.1 collective-permute-start.5
  272.7 1.6 collective-permute-done.6
  274.3 0.9 bitcast_add_fusion.1
  275.2 2.8 %collective-permute-done.5 = f32[32,1280]{1,0:T(8,128)S(1)} collective-permute-done((f32[32,1280]{1,0:T(8,128)S(1)}, f32[32,1280]{1,0:T(8,128)S(1)}, u32[]{:S(2)}, u32[]{:S(2)}) %collective-permute-start.5) | collective-permute-done | bytes 163872 | tf_op jit(solution)/shard_map/ppermute | solution.py:155
  278.0 0.9 bitcast_add_fusion
  279.0 0.7 pad_maximum_fusion.1
  (1 shorter events, 0.0 us)
Async XLA Ops:
  0.0 13.5 %copy-start.3 = (s32[10,7]{0,1:T(8,128)S(1)}, s32[10,7]{0,1:T(8,128)}, u32[]{:S(2)}) copy-start(s32[10,7]{0,1:T(8,128)} %param.6) | copy-start | bytes 844
  0.0 14.2 %copy-start.2 = (s32[10,7]{0,1:T(8,128)S(1)}, s32[10,7]{0,1:T(8,128)}, u32[]{:S(2)}) copy-start(s32[10,7]{0,1:T(8,128)} %param.7) | copy-start | bytes 844
  0.0 95.4 %collective-permute-start = (bf16[1280,2048]{1,0:T(8,128)(2,1)}, bf16[1280,2048]{1,0:T(8,128)(2,1)}, u32[]{:S(2)}, u32[]{:S(2)}) collective-permute-start(bf16[1280,2048]{1,0:T(8,128)(2,1)} %param.4), channel_id=1, source_target_pairs={{0,1},{1,0},{2,3},{3,2},{4,5},{5,4},{6,7},{7,6},{8,9},{9,8},{10,11... | collective-permute-start | bytes 15728648 | tf_op jit(solution)/shard_map/ppermute | solution.py:236
  2.7 33.8 %collective-permute-start.3 = (bf16[256,2048]{1,0:T(8,128)(2,1)}, bf16[256,2048]{1,0:T(8,128)(2,1)S(1)}, u32[]{:S(2)}, u32[]{:S(2)}) collective-permute-start(bf16[256,2048]{1,0:T(8,128)(2,1)} %get-tuple-element.14), channel_id=1, source_target_pairs={{0,2},{130,4},{4,6},{134,8},{8,10},{138,12},{12,14},{142,16},{16,1... | collective-permute-start | bytes 3145736 | tf_op jit(solution)/shard_map/ppermute | solution.py:42
  9.1 27.5 %collective-permute-start.1 = (bf16[5,7,64,128]{3,2,1,0:T(8,128)(2,1)}, bf16[5,7,64,128]{3,2,1,0:T(8,128)(2,1)}, u32[]{:S(2)}, u32[]{:S(2)}) collective-permute-start(bf16[5,7,64,128]{3,2,1,0:T(8,128)(2,1)} %constant_dynamic-slice_fusion), channel_id=1, source_target_pairs={{0,128},{128,0},{1,129},{129,1},{2,130},{130,2},{3,131},{131,3},{4... | collective-permute-start | bytes 1720328 | tf_op jit(solution)/shard_map/ppermute | solution.py:225
  10.0 41.2 %collective-permute-start.4 = (bf16[256,2048]{1,0:T(8,128)(2,1)S(1)}, bf16[256,2048]{1,0:T(8,128)(2,1)S(1)}, u32[]{:S(2)}, u32[]{:S(2)}) collective-permute-start(bf16[256,2048]{1,0:T(8,128)(2,1)S(1)} %get-tuple-element.13), channel_id=1, source_target_pairs={{2,0},{132,2},{6,4},{136,6},{10,8},{140,10},{14,12},{144,14},{18,1... | collective-permute-start | bytes 3145736 | tf_op jit(solution)/shard_map/ppermute | solution.py:43
  36.6 15.8 %collective-permute-start.2 = (bf16[5,7,64,128]{3,2,1,0:T(8,128)(2,1)}, bf16[5,7,64,128]{3,2,1,0:T(8,128)(2,1)S(1)}, u32[]{:S(2)}, u32[]{:S(2)}) collective-permute-start(bf16[5,7,64,128]{3,2,1,0:T(8,128)(2,1)} %collective-permute-done.1), channel_id=1, source_target_pairs={{0,1},{1,0},{2,3},{3,2},{4,5},{5,4},{6,7},{7,6},{8,9},{9,8},{10,11... | collective-permute-start | bytes 1720328 | tf_op jit(solution)/shard_map/ppermute | solution.py:226
  37.6 14.7 %copy-start = (bf16[10,7,64,128]{3,2,1,0:T(8,128)(2,1)S(1)}, bf16[10,7,64,128]{3,2,1,0:T(8,128)(2,1)}, u32[]{:S(2)}) copy-start(bf16[10,7,64,128]{3,2,1,0:T(8,128)(2,1)} %param.5) | copy-start | bytes 3440644
  105.7 4.7 %copy-start.1 = (bf16[1280,768]{1,0:T(8,128)(2,1)S(1)}, bf16[1280,768]{1,0:T(8,128)(2,1)}, u32[]{:S(2)}) copy-start(bf16[1280,768]{1,0:T(8,128)(2,1)} %shard_map.47) | copy-start | bytes 5898244
  268.0 6.3 %collective-permute-start.6 = (f32[32,768]{1,0:T(8,128)S(1)}, f32[32,768]{1,0:T(8,128)S(1)}, u32[]{:S(2)}, u32[]{:S(2)}) collective-permute-start(f32[32,768]{1,0:T(8,128)S(1)} %dynamic-slice_bitcast_fusion.1), channel_id=1, source_target_pairs={{0,2},{2,0},{1,3},{3,1},{4,6},{6,4},{5,7},{7,5},{8,10},{10,8},{9,1... | collective-permute-start | bytes 294920 | tf_op jit(solution)/shard_map/ppermute | solution.py:155
  272.6 5.4 %collective-permute-start.5 = (f32[32,1280]{1,0:T(8,128)S(1)}, f32[32,1280]{1,0:T(8,128)S(1)}, u32[]{:S(2)}, u32[]{:S(2)}) collective-permute-start(f32[32,1280]{1,0:T(8,128)S(1)} %dynamic-slice_bitcast_fusion), channel_id=1, source_target_pairs={{0,2},{2,0},{1,3},{3,1},{4,6},{6,4},{5,7},{7,5},{8,10},{10,8},{9,1... | collective-permute-start | bytes 491528 | tf_op jit(solution)/shard_map/ppermute | solution.py:155

commit v2 on v0

--- a/solution.py
+++ b/solution.py
@@ -48,10 +48,11 @@
     return lax.dynamic_index_in_dim(x, index, axis=dim, keepdims=False)
 
 
-def multi_ring_kernel(plan, *refs):
+def multi_ring_kernel(plan, pair_axis, *refs):
     count = len(plan)
     x_refs, o_refs = refs[:count], refs[count : 2 * count]
-    scratch = refs[2 * count :]
+    scratch = refs[2 * count : 2 * count + 7 * count]
+    pair_scratch = refs[2 * count + 7 * count :]
     mesh = pl.DeviceIdType.MESH
     rings = []
     for index, (axis, n) in enumerate(plan):
@@ -70,7 +71,12 @@
     for ring in rings:
         for neighbour in (ring["left"], ring["right"]):
             pl.semaphore_signal(barrier, 1, device_id={ring["axis"]: neighbour}, device_id_type=mesh)
-    pl.semaphore_wait(barrier, 2 * count)
+    signals = 2 * count
+    if pair_axis is not None:
+        partner = 1 - lax.axis_index(pair_axis)
+        pl.semaphore_signal(barrier, 1, device_id={pair_axis: partner}, device_id_type=mesh)
+        signals += 1
+    pl.semaphore_wait(barrier, signals)
 
     ticks = max(n - 1 for _, n in plan)
     for tick in range(ticks):
@@ -115,17 +121,39 @@
                 copy_f.start()
                 copy_b.start()
                 ring["copies"] = (copy_f, copy_b)
-    for ring in rings:
+    for index, ring in enumerate(rings):
         for copy in ring["copies"]:
             copy.wait()
         n, p, x = ring["n"], ring["p"], ring["x"]
         half = x.shape[-1] // 2
         last = (n - 2) % 2
-        ring["o"][:, :half] = ring["in_f"][last] + x[p, :, :half]
-        ring["o"][:, half:] = ring["in_b"][last] + x[p, :, half:]
-
-
-def multi_ring_reduce(inputs, plan, collective_id):
+        total = ring["o"] if pair_axis is None else pair_scratch[4 * index]
+        total[:, :half] = ring["in_f"][last] + x[p, :, :half]
+        total[:, half:] = ring["in_b"][last] + x[p, :, half:]
+    if pair_axis is None:
+        return
+    mine = lax.axis_index(pair_axis)
+    copies = []
+    for index, ring in enumerate(rings):
+        total, got, send_sem, recv_sem = pair_scratch[4 * index : 4 * index + 4]
+        rows = got.shape[0]
+        theirs = pl.multiple_of((1 - mine) * rows, rows)
+        copy = pltpu.make_async_remote_copy(
+            src_ref=total.at[pl.ds(theirs, rows)], dst_ref=got,
+            send_sem=send_sem, recv_sem=recv_sem,
+            device_id={pair_axis: 1 - mine}, device_id_type=mesh,
+        )
+        copy.start()
+        copies.append(copy)
+    for index, ring in enumerate(rings):
+        total, got = pair_scratch[4 * index : 4 * index + 2]
+        rows = got.shape[0]
+        copies[index].wait()
+        own = pl.multiple_of(mine * rows, rows)
+        ring["o"][...] = got[...] + total[pl.ds(own, rows), :]
+
+
+def multi_ring_reduce(inputs, plan, collective_id, pair_axis=None):
     vmem = pltpu.VMEM
     scratch = []
     for x in inputs:
@@ -137,9 +165,20 @@
             pltpu.SemaphoreType.DMA((2, 2)),
             pltpu.SemaphoreType.REGULAR((2,)),
         ]
+    out_shapes = [x.shape[1:] for x in inputs]
+    if pair_axis is not None:
+        for x in inputs:
+            _, rows, width = x.shape
+            scratch += [
+                vmem((rows, width), x.dtype),
+                vmem((rows // 2, width), x.dtype),
+                pltpu.SemaphoreType.DMA(()),
+                pltpu.SemaphoreType.DMA(()),
+            ]
+        out_shapes = [(x.shape[1] // 2, x.shape[2]) for x in inputs]
     return pl.pallas_call(
-        functools.partial(multi_ring_kernel, tuple(plan)),
-        out_shape=[jax.ShapeDtypeStruct(x.shape[1:], x.dtype) for x in inputs],
+        functools.partial(multi_ring_kernel, tuple(plan), pair_axis),
+        out_shape=[jax.ShapeDtypeStruct(shape, x.dtype) for shape, x in zip(out_shapes, inputs)],
         in_specs=[pl.BlockSpec(memory_space=vmem) for _ in inputs],
         out_specs=[pl.BlockSpec(memory_space=vmem) for _ in inputs],
         scratch_shapes=scratch,
@@ -252,23 +291,36 @@
         )
         parts.append(part.reshape(tuple(size for _, size in ROW_PARTS) + (chunk_rows, width)))
         names.append(list(ROW))
-    for stage in range(len(ROW_PARTS)):
+    stages = len(ROW_PARTS)
+    for stage in range(stages):
         axes = [order[stage] for order, _ in ORDERS]
         if sizes[axes[0]] == 2:
-            for index, axis in enumerate(axes):
-                dim = names[index].index(axis)
-                parts[index] = ring_sum(parts[index], dim, axis, 2)
-                names[index].remove(axis)
             continue
+        pair_axis = None
+        if stage + 1 < stages:
+            following = [order[stage + 1] for order, _ in ORDERS]
+            if sizes[following[0]] == 2 and len(set(following)) == 1 and stage + 2 == stages:
+                pair_axis = following[0]
         inputs, shapes = [], []
         for index, axis in enumerate(axes):
             dim = names[index].index(axis)
             x = parts[index]
-            shapes.append(x.shape[:dim] + x.shape[dim + 1 :])
+            shape = x.shape[:dim] + x.shape[dim + 1 :]
+            names[index].remove(axis)
+            if pair_axis is not None:
+                shape = shape[1:]
+                names[index].remove(pair_axis)
+            shapes.append(shape)
             inputs.append(jnp.moveaxis(x, dim, 0).reshape(sizes[axis], -1, x.shape[-1]))
+        outs = multi_ring_reduce(
+            inputs, [(axis, sizes[axis]) for axis in axes], stage, pair_axis
+        )
+        parts = [out.reshape(shape) for out, shape in zip(outs, shapes)]
+    for index in range(len(parts)):
+        for axis in list(names[index]):
+            dim = names[index].index(axis)
+            parts[index] = ring_sum(parts[index], dim, axis, sizes[axis])
             names[index].remove(axis)
-        outs = multi_ring_reduce(inputs, [(axis, sizes[axis]) for axis in axes], stage)
-        parts = [out.reshape(shape) for out, shape in zip(outs, shapes)]
     pieces = parts
     return jnp.concatenate(pieces, axis=-1)
 

time: 258 us -> 255 us (0.988)
  Pallas kernels: 168 us -> 176 us
  waiting for transfers between devices: 33.6 us -> 29.5 us
  starting transfers between devices: 11.6 us -> 8.79 us
    pallas_call x2, Pallas kernels: 146 us -> 154 us  [multi_ring_reduce(): pl.pallas_call(functools.partial(multi_ring_kernel, tuple(plan), pair_axi...]
    ppermute x2 -> x0, waiting for transfers between devices: 4.02 us -> none  [ring_sum(): got = lax.ppermute(take_chunk(x, 1 - p, dim), axis, partner)]
    ppermute x2 -> x0, starting transfers between devices: 2.81 us -> none  [ring_sum(): got = lax.ppermute(take_chunk(x, 1 - p, dim), axis, partner)]
  transfers between devices with their start and end apart: 7 -> 5, of which waited for: 4 -> 2; matrix products, arithmetic and copies ran while one was open for 7% -> 7% of each run, Pallas kernels for 9% -> 9%
where the time goes in v2:
time: 255 us
  Pallas kernels  176 us (69%)
  waiting for transfers between devices  29.5 us (12%)
  local copies, waits for them, and re-layouts  18.1 us (7%)
  matrix products  17.3 us (7%)
  starting transfers between devices  8.79 us (3%)
  other arithmetic  4.77 us (2%)
    pallas_call x2, Pallas kernels, multi_ring_reduce(): pl.pallas_call(functools.partial(multi_ring_kernel, tuple(plan), pair_axi...  154 us
    pallas_call x2, Pallas kernels, apply_operator(): pl.pallas_call(applied_kernel, grid_spec=grid_spec, out_shape=jax.ShapeDt...  22.1 us
    ppermute x1, waiting for transfers between devices, per_device(): from_sec = lax.ppermute(mine, 'sec', [(0, 1), (1, 0)])  21.6 us
    dot_general x2, matrix products, per_device(): lax.dot_general(left_projector, applied, (((0,), (0,)), ((), ())), prefer...  17.3 us
    ppermute x1, waiting for transfers between devices, halo(): after = lax.ppermute(shard[:width], axes, after_pairs)  7.88 us
    unnamed x15, local copies, waits for them, and re-layouts  6.95 us
  transfers between devices with their start and end apart: 5, of which 2 were waited for; matrix products, arithmetic and copies ran while one was open for 7% of the time, Pallas kernels for 9%

profile of v2, /device:TPU:8, one launch (start us, length us, event | category | flops | bytes accessed | tf_op | source)
XLA Modules:
  0.0 254.5 jit_solution(10763895235422404959)
XLA Ops:
  0.0 0.0 copy-start.3
  0.0 0.0 copy-start.2
  0.0 0.0 collective-permute-start
  0.0 2.7 %fusion = (bf16[256,2048]{1,0:T(8,128)(2,1)S(1)}, bf16[256,2048]{1,0:T(8,128)(2,1)}) fusion(bf16[1280,2048]{1,0:T(8,128)(2,1)} %param.4), kind=kLoop, calls=%fused_computation.13 | loop fusion | bytes 4194304 | tf_op jit(solution)/shard_map/slice | solution.py:43
  2.7 4.4 %collective-permute-start.3 = (bf16[256,2048]{1,0:T(8,128)(2,1)}, bf16[256,2048]{1,0:T(8,128)(2,1)S(1)}, u32[]{:S(2)}, u32[]{:S(2)}) collective-permute-start(bf16[256,2048]{1,0:T(8,128)(2,1)} %get-tuple-element.14), channel_id=1, source_target_pairs={{0,2},{130,4},{4,6},{134,8},{8,10},{138,12},{12,14},{142,16},{16,1... | collective-permute-start | bytes 3145736 | tf_op jit(solution)/shard_map/ppermute | solution.py:42
  7.2 1.9 constant_dynamic-slice_fusion
  9.1 0.9 collective-permute-start.1
  10.0 3.4 %collective-permute-start.4 = (bf16[256,2048]{1,0:T(8,128)(2,1)S(1)}, bf16[256,2048]{1,0:T(8,128)(2,1)S(1)}, u32[]{:S(2)}, u32[]{:S(2)}) collective-permute-start(bf16[256,2048]{1,0:T(8,128)(2,1)S(1)} %get-tuple-element.13), channel_id=1, source_target_pairs={{2,0},{132,2},{6,4},{136,6},{10,8},{140,10},{14,12},{144,14},{18,1... | collective-permute-start | bytes 3145736 | tf_op jit(solution)/shard_map/ppermute | solution.py:43
  13.5 0.0 copy-done.3
  13.5 0.1 copy.8
  13.6 0.6 reshape.14.offsets_ref
  14.2 0.0 copy-done.2
  14.2 0.1 copy.9
  14.3 0.6 reshape.15.mask_ref
  14.9 21.6 %collective-permute-done.1 = bf16[5,7,64,128]{3,2,1,0:T(8,128)(2,1)} collective-permute-done((bf16[5,7,64,128]{3,2,1,0:T(8,128)(2,1)}, bf16[5,7,64,128]{3,2,1,0:T(8,128)(2,1)}, u32[]{:S(2)}, u32[]{:S(2)}) %collective-permute-start.1) | collective-permute-done | bytes 573472 | tf_op jit(solution)/shard_map/ppermute | solution.py:260
  36.6 0.0 collective-permute-start.2
  36.6 0.0 collective-permute-done.3
  36.6 1.0 constant_dynamic-update-slice_fusion.2
  37.6 0.0 copy-start.1
  37.6 5.8 %constant_dynamic-update-slice_fusion.1 = bf16[1792,2048]{1,0:T(8,128)(2,1)} fusion(bf16[1792,2048]{1,0:T(8,128)(2,1)} %constant_dynamic-update-slice_fusion.2, bf16[1280,2048]{1,0:T(8,128)(2,1)} %param.4), kind=kLoop, calls=%fused_computation.9 | loop fusion | bytes 10485760
  43.4 7.9 %collective-permute-done.4 = bf16[256,2048]{1,0:T(8,128)(2,1)S(1)} collective-permute-done((bf16[256,2048]{1,0:T(8,128)(2,1)S(1)}, bf16[256,2048]{1,0:T(8,128)(2,1)S(1)}, u32[]{:S(2)}, u32[]{:S(2)}) %collective-permute-start.4) | collective-permute-done | bytes 1048608 | tf_op jit(solution)/shard_map/ppermute | solution.py:43
  51.3 1.1 constant_dynamic-update-slice_fusion.ext_ref
  52.3 0.0 collective-permute-done.2
  52.4 0.0 copy-done.1
  52.4 1.5 broadcast_select_fusion.4
  53.8 1.6 pad_maximum_fusion.ops_ref
  55.4 11.0 %shard_map.47 = bf16[1280,1024]{1,0:T(8,128)(2,1)} custom-call(s32[70]{0:T(128)} %reshape.14.offsets_ref, s32[70]{0:T(128)} %reshape.15.mask_ref, bf16[10,7,128,128]{3,2,1,0:T(8,128)(2,1)} %pad_maximum_fusion.ops_ref, bf16[1792,2048]{1,0:T(8,128)(2,1)} %constant_dynamic-update-slice_fusion.ext_ref), custom_call_target="tpu_custom_call" | custom-call | flops 2348810240 | bytes 11010048 | tf_op jit(solution)/shard_map/pallas_call | solution.py:238
  66.4 0.0 slice-start
  66.4 11.1 %shard_map.46 = bf16[1280,1024]{1,0:T(8,128)(2,1)} custom-call(s32[70]{0:T(128)} %reshape.14.offsets_ref, s32[70]{0:T(128)} %reshape.15.mask_ref, bf16[10,7,128,128]{3,2,1,0:T(8,128)(2,1)} %pad_maximum_fusion.ops_ref, bf16[1792,2048]{1,0:T(8,128)(2,1)} %constant_dynamic-update-slice_fusion.ext_ref), custom_call_target="tpu_custom_call" | custom-call | flops 2348810240 | bytes 11010048 | tf_op jit(solution)/shard_map/pallas_call | solution.py:238
  77.6 0.0 slice-start.1
  77.6 0.0 collective-permute-done
  77.6 9.0 %convolution_multiply_fusion = f32[2048,1024]{1,0:T(8,128)S(1)} fusion(bf16[1280,1024]{1,0:T(8,128)(2,1)} %shard_map.47, bf16[1280,2048]{1,0:T(8,128)(2,1)} %param.4, bf16[1280,2048]{1,0:T(8,128)(2,1)} %collective-permute-done, pred[]{:T(512)S(6)} %eq.10), kind=kOutput, calls=%fused_computation.1 | convolution fusion | flops 5373427712 | bytes 21495808 | tf_op jit(solution)/shard_map/dot_general | solution.py:289
  86.6 0.0 copy-start
  86.6 4.1 %copy.10 = f32[8,4,2,32,1024]{4,3,2,0,1:T(8,128)} copy(f32[8,4,2,32,1024]{4,3,2,1,0:T(8,128)S(1)} %bitcast.13) | data formatting | bytes 16777216 | tf_op jit(solution)/shard_map/reshape | solution.py:292
  90.7 0.0 slice-done
  90.7 0.0 slice-done.1
  90.7 0.0 copy-done
  90.7 8.3 %convolution_multiply_fusion.1 = f32[2048,1024]{1,0:T(8,128)} fusion(bf16[1280,1024]{1,0:T(8,128)(2,1)S(1)} %copy-done, bf16[1280,2048]{1,0:T(8,128)(2,1)S(1)} %bitcast.11, bf16[1280,2048]{1,0:T(8,128)(2,1)} %collective-permute-done, pred[]{:T(512)S(6)} %eq.10), kind=kOutput, calls=%fused_computation.2 | convolution fusion | flops 5373427712 | bytes 21495808 | tf_op jit(solution)/shard_map/dot_general | solution.py:289
  99.0 105.4 %shard_map.48 = (f32[256,1024]{1,0:T(8,128)}, f32[512,1024]{1,0:T(8,128)}) custom-call(f32[8,256,1024]{2,1,0:T(8,128)} %bitcast.12, f32[4,512,1024]{2,1,0:T(8,128)} %bitcast.9), custom_call_target="tpu_custom_call" | custom-call | tf_op jit(solution)/shard_map/pallas_call | solution.py:179
  204.5 48.4 %shard_map.49 = (f32[32,1024]{1,0:T(8,128)}, f32[32,1024]{1,0:T(8,128)}) custom-call(f32[4,64,1024]{2,1,0:T(8,128)} %bitcast.15, f32[8,64,1024]{2,1,0:T(8,128)} %bitcast.14), custom_call_target="tpu_custom_call" | custom-call | tf_op jit(solution)/shard_map/pallas_call | solution.py:179
  252.8 1.7 pad_maximum_fusion.1
  (2 shorter events, 0.0 us)
Async XLA Ops:
  0.0 13.5 %copy-start.3 = (s32[10,7]{0,1:T(8,128)S(1)}, s32[10,7]{0,1:T(8,128)}, u32[]{:S(2)}) copy-start(s32[10,7]{0,1:T(8,128)} %param.6) | copy-start | bytes 844
  0.0 14.2 %copy-start.2 = (s32[10,7]{0,1:T(8,128)S(1)}, s32[10,7]{0,1:T(8,128)}, u32[]{:S(2)}) copy-start(s32[10,7]{0,1:T(8,128)} %param.7) | copy-start | bytes 844
  0.0 77.6 %collective-permute-start = (bf16[1280,2048]{1,0:T(8,128)(2,1)}, bf16[1280,2048]{1,0:T(8,128)(2,1)}, u32[]{:S(2)}, u32[]{:S(2)}) collective-permute-start(bf16[1280,2048]{1,0:T(8,128)(2,1)} %param.4), channel_id=1, source_target_pairs={{0,1},{1,0},{2,3},{3,2},{4,5},{5,4},{6,7},{7,6},{8,9},{9,8},{10,11... | collective-permute-start | bytes 15728648 | tf_op jit(solution)/shard_map/ppermute | solution.py:271
  2.7 33.8 %collective-permute-start.3 = (bf16[256,2048]{1,0:T(8,128)(2,1)}, bf16[256,2048]{1,0:T(8,128)(2,1)S(1)}, u32[]{:S(2)}, u32[]{:S(2)}) collective-permute-start(bf16[256,2048]{1,0:T(8,128)(2,1)} %get-tuple-element.14), channel_id=1, source_target_pairs={{0,2},{130,4},{4,6},{134,8},{8,10},{138,12},{12,14},{142,16},{16,1... | collective-permute-start | bytes 3145736 | tf_op jit(solution)/shard_map/ppermute | solution.py:42
  9.1 27.5 %collective-permute-start.1 = (bf16[5,7,64,128]{3,2,1,0:T(8,128)(2,1)}, bf16[5,7,64,128]{3,2,1,0:T(8,128)(2,1)}, u32[]{:S(2)}, u32[]{:S(2)}) collective-permute-start(bf16[5,7,64,128]{3,2,1,0:T(8,128)(2,1)} %constant_dynamic-slice_fusion), channel_id=1, source_target_pairs={{0,128},{128,0},{1,129},{129,1},{2,130},{130,2},{3,131},{131,3},{4... | collective-permute-start | bytes 1720328 | tf_op jit(solution)/shard_map/ppermute | solution.py:260
  10.0 41.2 %collective-permute-start.4 = (bf16[256,2048]{1,0:T(8,128)(2,1)S(1)}, bf16[256,2048]{1,0:T(8,128)(2,1)S(1)}, u32[]{:S(2)}, u32[]{:S(2)}) collective-permute-start(bf16[256,2048]{1,0:T(8,128)(2,1)S(1)} %get-tuple-element.13), channel_id=1, source_target_pairs={{2,0},{132,2},{6,4},{136,6},{10,8},{140,10},{14,12},{144,14},{18,1... | collective-permute-start | bytes 3145736 | tf_op jit(solution)/shard_map/ppermute | solution.py:43
  36.6 15.8 %collective-permute-start.2 = (bf16[5,7,64,128]{3,2,1,0:T(8,128)(2,1)}, bf16[5,7,64,128]{3,2,1,0:T(8,128)(2,1)S(1)}, u32[]{:S(2)}, u32[]{:S(2)}) collective-permute-start(bf16[5,7,64,128]{3,2,1,0:T(8,128)(2,1)} %collective-permute-done.1), channel_id=1, source_target_pairs={{0,1},{1,0},{2,3},{3,2},{4,5},{5,4},{6,7},{7,6},{8,9},{9,8},{10,11... | collective-permute-start | bytes 1720328 | tf_op jit(solution)/shard_map/ppermute | solution.py:261
  37.6 14.7 %copy-start.1 = (bf16[10,7,64,128]{3,2,1,0:T(8,128)(2,1)S(1)}, bf16[10,7,64,128]{3,2,1,0:T(8,128)(2,1)}, u32[]{:S(2)}) copy-start(bf16[10,7,64,128]{3,2,1,0:T(8,128)(2,1)} %param.5) | copy-start | bytes 3440644
  66.4 24.3 %slice-start = ((s8[5242880]{0:T(1024)(128)(4,1)}), s8[1048576]{0:T(1024)(128)(4,1)S(1)}, s32[]{:S(2)}) async-start(s8[5242880]{0:T(1024)(128)(4,1)} %bitcast.10), calls=%async_computation | async-start | bytes 2097152
  77.6 13.2 %slice-start.1 = ((s8[5242880]{0:T(1024)(128)(4,1)}), s8[4194304]{0:T(1024)(128)(4,1)S(1)}, s32[]{:S(2)}) async-start(s8[5242880]{0:T(1024)(128)(4,1)} %bitcast.10), calls=%async_computation.1 | async-start | bytes 8388608
  86.6 4.1 %copy-start = (bf16[1280,1024]{1,0:T(8,128)(2,1)S(1)}, bf16[1280,1024]{1,0:T(8,128)(2,1)}, u32[]{:S(2)}) copy-start(bf16[1280,1024]{1,0:T(8,128)(2,1)} %shard_map.46) | copy-start | bytes 7864324

commit v3 on v2

--- a/solution.py
+++ b/solution.py
@@ -268,10 +268,11 @@
     second = jnp.where(sec == 0, other_half, operator_blocks)
     full_ops = jnp.concatenate([first, second], axis=2)
 
-    other_basis = lax.ppermute(basis_matrix, "col", [(0, 1), (1, 0)])
+    extended = halo(basis_matrix, REACH * block_rows)
+
+    outgoing, _, _ = lax.optimization_barrier((basis_matrix, from_col, extended))
+    other_basis = lax.ppermute(outgoing, "col", [(0, 1), (1, 0)])
     left_projector = jnp.where(sec == col, basis_matrix, other_basis)
-
-    extended = halo(basis_matrix, REACH * block_rows)
     offsets = jnp.clip(neighbours - row * block_count + REACH, 0, block_count + 2 * REACH - 1)
     row_count = 1
     for _, size in ROW_PARTS:

time: 255 us -> 257 us (level)
  the two profiles are of different devices: /device:TPU:8 before, /device:TPU:24 now
where the time goes in v3:
time: 257 us; the launch traced here: 256 us
  Pallas kernels  174 us (68%)
  waiting for transfers between devices  33.4 us (13%)
  matrix products  18.8 us (7%)
  local copies, waits for them, and re-layouts  17.2 us (7%)
  starting transfers between devices  7.65 us (3%)
  other arithmetic  5.2 us (2%)
    pallas_call x2, Pallas kernels, multi_ring_reduce(): pl.pallas_call(functools.partial(multi_ring_kernel, tuple(plan), pair_axi...  152 us
    pallas_call x2, Pallas kernels, apply_operator(): pl.pallas_call(applied_kernel, grid_spec=grid_spec, out_shape=jax.ShapeDt...  22.1 us
    ppermute x1, waiting for transfers between devices, per_device(): from_sec = lax.ppermute(mine, 'sec', [(0, 1), (1, 0)])  19.4 us
    dot_general x2, matrix products, per_device(): lax.dot_general(left_projector, applied, (((0,), (0,)), ((), ())), prefer...  18.8 us
    ppermute x1, waiting for transfers between devices, halo(): after = lax.ppermute(shard[:width], axes, after_pairs)  14.1 us
    unnamed x17, local copies, waits for them, and re-layouts  7.91 us
  transfers between devices with their start and end apart: 5, of which 2 were waited for; matrix products, arithmetic and copies ran while one was open for 5% of the time, Pallas kernels for 9%

profile of v3, /device:TPU:24, one launch (start us, length us, event | category | flops | bytes accessed | tf_op | source)
XLA Modules:
  0.0 256.2 jit_solution(2856074576560017289)
XLA Ops:
  0.0 1.7 fusion
  1.7 3.1 %collective-permute-start.2 = (bf16[256,2048]{1,0:T(8,128)(2,1)S(1)}, bf16[256,2048]{1,0:T(8,128)(2,1)S(1)}, u32[]{:S(2)}, u32[]{:S(2)}) collective-permute-start(bf16[256,2048]{1,0:T(8,128)(2,1)S(1)} %get-tuple-element.16), channel_id=1, source_target_pairs={{0,2},{130,4},{4,6},{134,8},{8,10},{138,12},{12,14},{142,16},{16,1... | collective-permute-start | bytes 3145736 | tf_op jit(solution)/shard_map/ppermute | solution.py:42
  4.8 1.1 constant_dynamic-slice_fusion
  5.9 2.7 %collective-permute-start = (bf16[5,7,64,128]{3,2,1,0:T(8,128)(2,1)S(1)}, bf16[5,7,64,128]{3,2,1,0:T(8,128)(2,1)S(1)}, u32[]{:S(2)}, u32[]{:S(2)}) collective-permute-start(bf16[5,7,64,128]{3,2,1,0:T(8,128)(2,1)S(1)} %constant_dynamic-slice_fusion), channel_id=1, source_target_pairs={{0,128},{128,0},{1,129},{129,1},{2,130},{130,2},{3,131},{131,3},{4... | collective-permute-start | bytes 1720328 | tf_op jit(solution)/shard_map/ppermute | solution.py:260
  8.5 1.9 collective-permute-start.3
  10.4 19.4 %collective-permute-done = bf16[5,7,64,128]{3,2,1,0:T(8,128)(2,1)S(1)} collective-permute-done((bf16[5,7,64,128]{3,2,1,0:T(8,128)(2,1)S(1)}, bf16[5,7,64,128]{3,2,1,0:T(8,128)(2,1)S(1)}, u32[]{:S(2)}, u32[]{:S(2)}) %collective-permute-start) | collective-permute-done | bytes 573472 | tf_op jit(solution)/shard_map/ppermute | solution.py:260
  29.8 0.0 copy-start.3
  29.8 0.0 collective-permute-start.1
  29.8 0.0 collective-permute-done.2
  29.8 1.1 constant_dynamic-update-slice_fusion.2
  31.0 0.0 copy-start.6
  31.0 0.0 copy-start.5
  31.0 0.0 copy-start.2
  31.0 5.8 %constant_dynamic-update-slice_fusion.1 = bf16[1792,2048]{1,0:T(8,128)(2,1)} fusion(bf16[1792,2048]{1,0:T(8,128)(2,1)} %constant_dynamic-update-slice_fusion.2, bf16[1280,2048]{1,0:T(8,128)(2,1)} %param.4), kind=kLoop, calls=%fused_computation.9 | loop fusion | bytes 10485760
  36.8 0.0 copy-done.3
  36.8 14.1 %collective-permute-done.3 = bf16[256,2048]{1,0:T(8,128)(2,1)S(1)} collective-permute-done((bf16[256,2048]{1,0:T(8,128)(2,1)S(1)}, bf16[256,2048]{1,0:T(8,128)(2,1)S(1)}, u32[]{:S(2)}, u32[]{:S(2)}) %collective-permute-start.3) | collective-permute-done | bytes 1048608 | tf_op jit(solution)/shard_map/ppermute | solution.py:43
  50.8 1.1 constant_dynamic-update-slice_fusion.ext_ref
  51.9 0.0 collective-permute-done.1
  51.9 0.0 copy-start.4
  52.0 0.9 copy-done.4
  52.8 0.0 collective-permute-start.4
  52.8 0.0 copy-done.6
  52.8 0.1 copy.8
  52.9 0.6 reshape.14.offsets_ref
  53.5 0.0 copy-done.5
  53.5 0.1 copy.9
  53.6 0.6 reshape.15.mask_ref
  54.3 0.0 copy-done.2
  54.3 1.9 broadcast_select_fusion.4
  56.2 1.6 pad_maximum_fusion.ops_ref
  57.8 11.0 %shard_map.47 = bf16[1280,1024]{1,0:T(8,128)(2,1)} custom-call(s32[70]{0:T(128)} %reshape.14.offsets_ref, s32[70]{0:T(128)} %reshape.15.mask_ref, bf16[10,7,128,128]{3,2,1,0:T(8,128)(2,1)} %pad_maximum_fusion.ops_ref, bf16[1792,2048]{1,0:T(8,128)(2,1)} %constant_dynamic-update-slice_fusion.ext_ref), custom_call_target="tpu_custom_call" | custom-call | flops 2348810240 | bytes 11010048 | tf_op jit(solution)/shard_map/pallas_call | solution.py:238
  68.7 0.0 copy-start.1
  68.7 11.1 %shard_map.46 = bf16[1280,1024]{1,0:T(8,128)(2,1)} custom-call(s32[70]{0:T(128)} %reshape.14.offsets_ref, s32[70]{0:T(128)} %reshape.15.mask_ref, bf16[10,7,128,128]{3,2,1,0:T(8,128)(2,1)} %pad_maximum_fusion.ops_ref, bf16[1792,2048]{1,0:T(8,128)(2,1)} %constant_dynamic-update-slice_fusion.ext_ref), custom_call_target="tpu_custom_call" | custom-call | flops 2348810240 | bytes 11010048 | tf_op jit(solution)/shard_map/pallas_call | solution.py:238
  79.9 0.0 collective-permute-done.4
  79.9 0.0 copy-done.1
  79.9 8.0 %convolution_multiply_fusion = f32[2048,1024]{1,0:T(8,128)S(1)} fusion(bf16[1280,1024]{1,0:T(8,128)(2,1)S(1)} %copy-done.1, bf16[1280,2048]{1,0:T(8,128)(2,1)} %param.4, bf16[1280,2048]{1,0:T(8,128)(2,1)} %collective-permute-done.4, pred[]{:T(512)S(6)} %eq.10), kind=kOutput, calls=%fused_computation.1 | convolution fusion | flops 5373427712 | bytes 21495808 | tf_op jit(solution)/shard_map/dot_general | solution.py:290
  87.9 0.0 copy-start
  87.9 4.1 %copy.10 = f32[8,4,2,32,1024]{4,3,2,0,1:T(8,128)} copy(f32[8,4,2,32,1024]{4,3,2,1,0:T(8,128)S(1)} %bitcast.11) | data formatting | bytes 16777216 | tf_op jit(solution)/shard_map/reshape | solution.py:293
  92.0 0.0 copy-done
  92.0 10.7 %convolution_multiply_fusion.1 = f32[2048,1024]{1,0:T(8,128)} fusion(bf16[1280,1024]{1,0:T(8,128)(2,1)S(1)} %copy-done, bf16[1280,2048]{1,0:T(8,128)(2,1)} %param.4, bf16[1280,2048]{1,0:T(8,128)(2,1)} %collective-permute-done.4, pred[]{:T(512)S(6)} %eq.10), kind=kOutput, calls=%fused_computation.2 | convolution fusion | flops 5373427712 | bytes 21495808 | tf_op jit(solution)/shard_map/dot_general | solution.py:290
  102.8 103.0 %shard_map.48 = (f32[256,1024]{1,0:T(8,128)}, f32[512,1024]{1,0:T(8,128)}) custom-call(f32[8,256,1024]{2,1,0:T(8,128)} %bitcast.10, f32[4,512,1024]{2,1,0:T(8,128)} %bitcast.9), custom_call_target="tpu_custom_call" | custom-call | tf_op jit(solution)/shard_map/pallas_call | solution.py:179
  205.7 48.7 %shard_map.49 = (f32[32,1024]{1,0:T(8,128)}, f32[32,1024]{1,0:T(8,128)}) custom-call(f32[4,64,1024]{2,1,0:T(8,128)} %bitcast.13, f32[8,64,1024]{2,1,0:T(8,128)} %bitcast.12), custom_call_target="tpu_custom_call" | custom-call | tf_op jit(solution)/shard_map/pallas_call | solution.py:179
  254.5 1.7 pad_maximum_fusion.1
  (1 shorter events, 0.0 us)
Async XLA Ops:
  1.7 28.2 %collective-permute-start.2 = (bf16[256,2048]{1,0:T(8,128)(2,1)S(1)}, bf16[256,2048]{1,0:T(8,128)(2,1)S(1)}, u32[]{:S(2)}, u32[]{:S(2)}) collective-permute-start(bf16[256,2048]{1,0:T(8,128)(2,1)S(1)} %get-tuple-element.16), channel_id=1, source_target_pairs={{0,2},{130,4},{4,6},{134,8},{8,10},{138,12},{12,14},{142,16},{16,1... | collective-permute-start | bytes 3145736 | tf_op jit(solution)/shard_map/ppermute | solution.py:42
  5.9 24.0 %collective-permute-start = (bf16[5,7,64,128]{3,2,1,0:T(8,128)(2,1)S(1)}, bf16[5,7,64,128]{3,2,1,0:T(8,128)(2,1)S(1)}, u32[]{:S(2)}, u32[]{:S(2)}) collective-permute-start(bf16[5,7,64,128]{3,2,1,0:T(8,128)(2,1)S(1)} %constant_dynamic-slice_fusion), channel_id=1, source_target_pairs={{0,128},{128,0},{1,129},{129,1},{2,130},{130,2},{3,131},{131,3},{4... | collective-permute-start | bytes 1720328 | tf_op jit(solution)/shard_map/ppermute | solution.py:260
  8.5 42.3 %collective-permute-start.3 = (bf16[256,2048]{1,0:T(8,128)(2,1)S(1)}, bf16[256,2048]{1,0:T(8,128)(2,1)S(1)}, u32[]{:S(2)}, u32[]{:S(2)}) collective-permute-start(bf16[256,2048]{1,0:T(8,128)(2,1)S(1)} %get-tuple-element.15), channel_id=1, source_target_pairs={{2,0},{132,2},{6,4},{136,6},{10,8},{140,10},{14,12},{144,14},{18,1... | collective-permute-start | bytes 3145736 | tf_op jit(solution)/shard_map/ppermute | solution.py:43
  29.8 6.9 %copy-start.3 = (bf16[5,7,64,128]{3,2,1,0:T(8,128)(2,1)}, bf16[5,7,64,128]{3,2,1,0:T(8,128)(2,1)S(1)}, u32[]{:S(2)}) copy-start(bf16[5,7,64,128]{3,2,1,0:T(8,128)(2,1)S(1)} %collective-permute-done) | copy-start | bytes 1720324
  29.8 22.1 %collective-permute-start.1 = (bf16[5,7,64,128]{3,2,1,0:T(8,128)(2,1)S(1)}, bf16[5,7,64,128]{3,2,1,0:T(8,128)(2,1)S(1)}, u32[]{:S(2)}, u32[]{:S(2)}) collective-permute-start(bf16[5,7,64,128]{3,2,1,0:T(8,128)(2,1)S(1)} %collective-permute-done), channel_id=1, source_target_pairs={{0,1},{1,0},{2,3},{3,2},{4,5},{5,4},{6,7},{7,6},{8,9},{9,8},{10,11... | collective-permute-start | bytes 1720328 | tf_op jit(solution)/shard_map/ppermute | solution.py:261
  31.0 21.8 %copy-start.6 = (s32[10,7]{0,1:T(8,128)S(1)}, s32[10,7]{0,1:T(8,128)}, u32[]{:S(2)}) copy-start(s32[10,7]{0,1:T(8,128)} %param.6) | copy-start | bytes 844
  31.0 22.5 %copy-start.5 = (s32[10,7]{0,1:T(8,128)S(1)}, s32[10,7]{0,1:T(8,128)}, u32[]{:S(2)}) copy-start(s32[10,7]{0,1:T(8,128)} %param.7) | copy-start | bytes 844
  31.0 23.3 %copy-start.2 = (bf16[10,7,64,128]{3,2,1,0:T(8,128)(2,1)S(1)}, bf16[10,7,64,128]{3,2,1,0:T(8,128)(2,1)}, u32[]{:S(2)}) copy-start(bf16[10,7,64,128]{3,2,1,0:T(8,128)(2,1)} %param.5) | copy-start | bytes 3440644
  51.9 0.9 copy-start.4
  52.8 27.1 %collective-permute-start.4 = (bf16[1280,2048]{1,0:T(8,128)(2,1)}, bf16[1280,2048]{1,0:T(8,128)(2,1)}, u32[]{:S(2)}, u32[]{:S(2)}) collective-permute-start(bf16[1280,2048]{1,0:T(8,128)(2,1)} %param.4), channel_id=1, source_target_pairs={{0,1},{1,0},{2,3},{3,2},{4,5},{5,4},{6,7},{7,6},{8,9},{9,8},{10,11... | collective-permute-start | bytes 15728648 | tf_op jit(solution)/shard_map/ppermute | solution.py:274
  68.7 11.1 %copy-start.1 = (bf16[1280,1024]{1,0:T(8,128)(2,1)S(1)}, bf16[1280,1024]{1,0:T(8,128)(2,1)}, u32[]{:S(2)}) copy-start(bf16[1280,1024]{1,0:T(8,128)(2,1)} %shard_map.47) | copy-start | bytes 7864324
  87.9 4.1 %copy-start = (bf16[1280,1024]{1,0:T(8,128)(2,1)S(1)}, bf16[1280,1024]{1,0:T(8,128)(2,1)}, u32[]{:S(2)}) copy-start(bf16[1280,1024]{1,0:T(8,128)(2,1)} %shard_map.46) | copy-start | bytes 7864324

commit v4 on v2

--- a/solution.py
+++ b/solution.py
@@ -16,6 +16,7 @@
 UNIT = 256
 ORDERS = ((("z", "x", "y"), 4), (("x", "z", "y"), 4))
 TILE_COLUMNS = 1024
+STRIDE = 8
 STATIC_OFFSETS = (0, -1, 1, -2, 2)
 WINDOW_SLOTS = tuple(range(len(STATIC_OFFSETS)))
 
@@ -51,38 +52,84 @@
 def multi_ring_kernel(plan, pair_axis, *refs):
     count = len(plan)
     x_refs, o_refs = refs[:count], refs[count : 2 * count]
-    scratch = refs[2 * count : 2 * count + 7 * count]
-    pair_scratch = refs[2 * count + 7 * count :]
+    scratch = refs[2 * count : 2 * count + STRIDE * count]
+    pair_scratch = refs[2 * count + STRIDE * count :]
     mesh = pl.DeviceIdType.MESH
     rings = []
-    for index, (axis, n) in enumerate(plan):
-        out_f, in_f, out_b, in_b, send_sem, recv_sem, credit_sem = scratch[7 * index : 7 * index + 7]
+    for index, (axis, n, halving) in enumerate(plan):
         p = lax.axis_index(axis)
-        rings.append(
-            dict(
-                axis=axis, n=n, p=p, x=x_refs[index], o=o_refs[index],
+        ring = dict(axis=axis, n=n, p=p, x=x_refs[index], o=o_refs[index], halving=halving, copies=None)
+        if halving:
+            distances = []
+            d = n // 2
+            while d >= 1:
+                distances.append(d)
+                d //= 2
+            steps = len(distances)
+            ring.update(
+                distances=distances,
+                received=scratch[STRIDE * index : STRIDE * index + steps],
+                kept=scratch[STRIDE * index + steps : STRIDE * index + 2 * steps],
+                send=scratch[STRIDE * index + 2 * steps],
+                recv=scratch[STRIDE * index + 2 * steps + 1],
+                partners=[p + (1 - 2 * lax.rem(p // d, 2)) * d for d in distances],
+            )
+        else:
+            out_f, in_f, out_b, in_b, send_sem, recv_sem, credit_sem = scratch[STRIDE * index : STRIDE * index + 7]
+            ring.update(
                 right=lax.rem(p + 1, n), left=lax.rem(p + n - 1, n),
                 out_f=out_f, in_f=in_f, out_b=out_b, in_b=in_b,
-                send=send_sem, recv=recv_sem, credit=credit_sem, copies=None,
+                send=send_sem, recv=recv_sem, credit=credit_sem,
             )
-        )
+        rings.append(ring)
 
     barrier = pltpu.get_barrier_semaphore()
+    signals = 0
     for ring in rings:
-        for neighbour in (ring["left"], ring["right"]):
+        targets = ring["partners"] if ring["halving"] else (ring["left"], ring["right"])
+        for neighbour in targets:
             pl.semaphore_signal(barrier, 1, device_id={ring["axis"]: neighbour}, device_id_type=mesh)
-    signals = 2 * count
+            signals += 1
     if pair_axis is not None:
         partner = 1 - lax.axis_index(pair_axis)
         pl.semaphore_signal(barrier, 1, device_id={pair_axis: partner}, device_id_type=mesh)
         signals += 1
     pl.semaphore_wait(barrier, signals)
 
-    ticks = max(n - 1 for _, n in plan)
+    def halving_source(ring, step):
+        return ring["x"] if step == 0 else ring["kept"][step - 1]
+
+    def halving_finish(ring, step):
+        d = ring["distances"][step]
+        keep = pl.multiple_of(lax.rem(ring["p"] // d, 2) * d, d)
+        src = halving_source(ring, step)
+        ring["kept"][step][...] = src[pl.ds(keep, d)] + ring["received"][step][...]
+
+    def step_count(ring):
+        return len(ring["distances"]) if ring["halving"] else ring["n"] - 1
+
+    ticks = max(step_count(ring) for ring in rings)
     for tick in range(ticks):
         for ring in rings:
             n = ring["n"]
-            due = [step for step in range(n - 1) if (step * ticks) // (n - 1) == tick]
+            total_steps = step_count(ring)
+            due = [step for step in range(total_steps) if (step * ticks) // total_steps == tick]
+            if ring["halving"]:
+                for step in due:
+                    if step > 0:
+                        ring["copies"].wait()
+                        halving_finish(ring, step - 1)
+                    d = ring["distances"][step]
+                    away = pl.multiple_of((1 - lax.rem(ring["p"] // d, 2)) * d, d)
+                    copy = pltpu.make_async_remote_copy(
+                        src_ref=halving_source(ring, step).at[pl.ds(away, d)],
+                        dst_ref=ring["received"][step],
+                        send_sem=ring["send"].at[step], recv_sem=ring["recv"].at[step],
+                        device_id={ring["axis"]: ring["partners"][step]}, device_id_type=mesh,
+                    )
+                    copy.start()
+                    ring["copies"] = copy
+                continue
             for step in due:
                 if ring["copies"] is not None:
                     for copy in ring["copies"]:
@@ -122,6 +169,13 @@
                 copy_b.start()
                 ring["copies"] = (copy_f, copy_b)
     for index, ring in enumerate(rings):
+        if ring["halving"]:
+            ring["copies"].wait()
+            last = len(ring["distances"]) - 1
+            halving_finish(ring, last)
+            total = ring["o"] if pair_axis is None else pair_scratch[4 * index]
+            total[...] = ring["kept"][last][0]
+            continue
         for copy in ring["copies"]:
             copy.wait()
         n, p, x = ring["n"], ring["p"], ring["x"]
@@ -156,14 +210,27 @@
 def multi_ring_reduce(inputs, plan, collective_id, pair_axis=None):
     vmem = pltpu.VMEM
     scratch = []
-    for x in inputs:
+    for x, (_, n, halving) in zip(inputs, plan):
         _, rows, width = x.shape
         half = width // 2
+        if halving:
+            sizes = []
+            d = n // 2
+            while d >= 1:
+                sizes.append(d)
+                d //= 2
+            scratch += [vmem((d, rows, width), x.dtype) for d in sizes] * 2
+            scratch += [
+                pltpu.SemaphoreType.DMA((len(sizes),)),
+                pltpu.SemaphoreType.DMA((len(sizes),)),
+            ]
+            continue
         scratch += [vmem((2, rows, half), x.dtype) for _ in range(4)]
         scratch += [
             pltpu.SemaphoreType.DMA((2, 2)),
             pltpu.SemaphoreType.DMA((2, 2)),
             pltpu.SemaphoreType.REGULAR((2,)),
+            vmem((8, 128), x.dtype),
         ]
     out_shapes = [x.shape[1:] for x in inputs]
     if pair_axis is not None:
@@ -312,9 +379,8 @@
                 names[index].remove(pair_axis)
             shapes.append(shape)
             inputs.append(jnp.moveaxis(x, dim, 0).reshape(sizes[axis], -1, x.shape[-1]))
-        outs = multi_ring_reduce(
-            inputs, [(axis, sizes[axis]) for axis in axes], stage, pair_axis
-        )
+        plan = [(axis, sizes[axis], stage > 0 and sizes[axis] > 4) for axis in axes]
+        outs = multi_ring_reduce(inputs, plan, stage, pair_axis)
         parts = [out.reshape(shape) for out, shape in zip(outs, shapes)]
     for index in range(len(parts)):
         for axis in list(names[index]):

time: 255 us -> 301 us (1.18)
  Pallas kernels: 176 us -> 221 us
    pallas_call x2, Pallas kernels: 154 us -> 199 us  [multi_ring_reduce(): pl.pallas_call(functools.partial(multi_ring_kernel, tuple(plan), pair_axi...]
  transfers between devices with their start and end apart: 5 -> 5, of which waited for: 2 -> 2; matrix products, arithmetic and copies ran while one was open for 7% -> 6% of each run, Pallas kernels for 9% -> 7%
where the time goes in v4:
time: 301 us; the launch traced here: 300 us
  Pallas kernels  221 us (73%)
  waiting for transfers between devices  29.5 us (10%)
  local copies, waits for them, and re-layouts  18.1 us (6%)
  matrix products  17.3 us (6%)
  starting transfers between devices  8.79 us (3%)
  other arithmetic  4.77 us (2%)
    pallas_call x2, Pallas kernels, multi_ring_reduce(): pl.pallas_call(functools.partial(multi_ring_kernel, tuple(plan), pair_axi...  199 us
    pallas_call x2, Pallas kernels, apply_operator(): pl.pallas_call(applied_kernel, grid_spec=grid_spec, out_shape=jax.ShapeDt...  22.1 us
    ppermute x1, waiting for transfers between devices, per_device(): from_sec = lax.ppermute(mine, 'sec', [(0, 1), (1, 0)])  21.6 us
    dot_general x2, matrix products, per_device(): lax.dot_general(left_projector, applied, (((0,), (0,)), ((), ())), prefer...  17.3 us
    ppermute x1, waiting for transfers between devices, halo(): after = lax.ppermute(shard[:width], axes, after_pairs)  7.88 us
    unnamed x15, local copies, waits for them, and re-layouts  6.95 us
  transfers between devices with their start and end apart: 5, of which 2 were waited for; matrix products, arithmetic and copies ran while one was open for 6% of the time, Pallas kernels for 7%

profile of v4, /device:TPU:8, one launch (start us, length us, event | category | flops | bytes accessed | tf_op | source)
XLA Modules:
  0.0 299.6 jit_solution(7617678144424575084)
XLA Ops:
  0.0 0.0 copy-start.3
  0.0 0.0 copy-start.2
  0.0 0.0 collective-permute-start
  0.0 2.7 fusion
  2.7 4.4 %collective-permute-start.3 = (bf16[256,2048]{1,0:T(8,128)(2,1)}, bf16[256,2048]{1,0:T(8,128)(2,1)S(1)}, u32[]{:S(2)}, u32[]{:S(2)}) collective-permute-start(bf16[256,2048]{1,0:T(8,128)(2,1)} %get-tuple-element.14), channel_id=1, source_target_pairs={{0,2},{130,4},{4,6},{134,8},{8,10},{138,12},{12,14},{142,16},{16,1... | collective-permute-start | bytes 3145736 | tf_op jit(solution)/shard_map/ppermute | solution.py:43
  7.2 1.9 constant_dynamic-slice_fusion
  9.1 0.9 collective-permute-start.1
  10.0 3.4 %collective-permute-start.4 = (bf16[256,2048]{1,0:T(8,128)(2,1)S(1)}, bf16[256,2048]{1,0:T(8,128)(2,1)S(1)}, u32[]{:S(2)}, u32[]{:S(2)}) collective-permute-start(bf16[256,2048]{1,0:T(8,128)(2,1)S(1)} %get-tuple-element.13), channel_id=1, source_target_pairs={{2,0},{132,2},{6,4},{136,6},{10,8},{140,10},{14,12},{144,14},{18,1... | collective-permute-start | bytes 3145736 | tf_op jit(solution)/shard_map/ppermute | solution.py:44
  13.5 0.0 copy-done.3
  13.5 0.1 copy.8
  13.6 0.6 reshape.14.offsets_ref
  14.2 0.0 copy-done.2
  14.2 0.1 copy.9
  14.3 0.6 reshape.15.mask_ref
  14.9 21.6 %collective-permute-done.1 = bf16[5,7,64,128]{3,2,1,0:T(8,128)(2,1)} collective-permute-done((bf16[5,7,64,128]{3,2,1,0:T(8,128)(2,1)}, bf16[5,7,64,128]{3,2,1,0:T(8,128)(2,1)}, u32[]{:S(2)}, u32[]{:S(2)}) %collective-permute-start.1) | collective-permute-done | bytes 573472 | tf_op jit(solution)/shard_map/ppermute | solution.py:327
  36.6 0.0 collective-permute-start.2
  36.6 0.0 collective-permute-done.3
  36.6 1.0 constant_dynamic-update-slice_fusion.2
  37.6 0.0 copy-start.1
  37.6 5.8 %constant_dynamic-update-slice_fusion.1 = bf16[1792,2048]{1,0:T(8,128)(2,1)} fusion(bf16[1792,2048]{1,0:T(8,128)(2,1)} %constant_dynamic-update-slice_fusion.2, bf16[1280,2048]{1,0:T(8,128)(2,1)} %param.4), kind=kLoop, calls=%fused_computation.9 | loop fusion | bytes 10485760
  43.4 7.9 %collective-permute-done.4 = bf16[256,2048]{1,0:T(8,128)(2,1)S(1)} collective-permute-done((bf16[256,2048]{1,0:T(8,128)(2,1)S(1)}, bf16[256,2048]{1,0:T(8,128)(2,1)S(1)}, u32[]{:S(2)}, u32[]{:S(2)}) %collective-permute-start.4) | collective-permute-done | bytes 1048608 | tf_op jit(solution)/shard_map/ppermute | solution.py:44
  51.3 1.1 constant_dynamic-update-slice_fusion.ext_ref
  52.3 0.0 collective-permute-done.2
  52.4 0.0 copy-done.1
  52.4 1.5 broadcast_select_fusion.4
  53.8 1.6 pad_maximum_fusion.ops_ref
  55.4 11.0 %shard_map.47 = bf16[1280,1024]{1,0:T(8,128)(2,1)} custom-call(s32[70]{0:T(128)} %reshape.14.offsets_ref, s32[70]{0:T(128)} %reshape.15.mask_ref, bf16[10,7,128,128]{3,2,1,0:T(8,128)(2,1)} %pad_maximum_fusion.ops_ref, bf16[1792,2048]{1,0:T(8,128)(2,1)} %constant_dynamic-update-slice_fusion.ext_ref), custom_call_target="tpu_custom_call" | custom-call | flops 2348810240 | bytes 11010048 | tf_op jit(solution)/shard_map/pallas_call | solution.py:305
  66.4 0.0 slice-start
  66.4 11.1 %shard_map.46 = bf16[1280,1024]{1,0:T(8,128)(2,1)} custom-call(s32[70]{0:T(128)} %reshape.14.offsets_ref, s32[70]{0:T(128)} %reshape.15.mask_ref, bf16[10,7,128,128]{3,2,1,0:T(8,128)(2,1)} %pad_maximum_fusion.ops_ref, bf16[1792,2048]{1,0:T(8,128)(2,1)} %constant_dynamic-update-slice_fusion.ext_ref), custom_call_target="tpu_custom_call" | custom-call | flops 2348810240 | bytes 11010048 | tf_op jit(solution)/shard_map/pallas_call | solution.py:305
  77.6 0.0 slice-start.1
  77.6 0.0 collective-permute-done
  77.6 9.0 %convolution_multiply_fusion = f32[2048,1024]{1,0:T(8,128)S(1)} fusion(bf16[1280,1024]{1,0:T(8,128)(2,1)} %shard_map.47, bf16[1280,2048]{1,0:T(8,128)(2,1)} %param.4, bf16[1280,2048]{1,0:T(8,128)(2,1)} %collective-permute-done, pred[]{:T(512)S(6)} %eq.10), kind=kOutput, calls=%fused_computation.1 | convolution fusion | flops 5373427712 | bytes 21495808 | tf_op jit(solution)/shard_map/dot_general | solution.py:356
  86.6 0.0 copy-start
  86.6 4.1 %copy.10 = f32[8,4,2,32,1024]{4,3,2,0,1:T(8,128)} copy(f32[8,4,2,32,1024]{4,3,2,1,0:T(8,128)S(1)} %bitcast.13) | data formatting | bytes 16777216 | tf_op jit(solution)/shard_map/reshape | solution.py:359
  90.7 0.0 slice-done
  90.7 0.0 slice-done.1
  90.7 0.0 copy-done
  90.7 8.3 %convolution_multiply_fusion.1 = f32[2048,1024]{1,0:T(8,128)} fusion(bf16[1280,1024]{1,0:T(8,128)(2,1)S(1)} %copy-done, bf16[1280,2048]{1,0:T(8,128)(2,1)S(1)} %bitcast.11, bf16[1280,2048]{1,0:T(8,128)(2,1)} %collective-permute-done, pred[]{:T(512)S(6)} %eq.10), kind=kOutput, calls=%fused_computation.2 | convolution fusion | flops 5373427712 | bytes 21495808 | tf_op jit(solution)/shard_map/dot_general | solution.py:356
  99.0 105.4 %shard_map.48 = (f32[256,1024]{1,0:T(8,128)}, f32[512,1024]{1,0:T(8,128)}) custom-call(f32[8,256,1024]{2,1,0:T(8,128)} %bitcast.12, f32[4,512,1024]{2,1,0:T(8,128)} %bitcast.9), custom_call_target="tpu_custom_call" | custom-call | tf_op jit(solution)/shard_map/pallas_call | solution.py:246
  204.5 93.4 %shard_map.49 = (f32[32,1024]{1,0:T(8,128)}, f32[32,1024]{1,0:T(8,128)}) custom-call(f32[4,64,1024]{2,1,0:T(8,128)} %bitcast.15, f32[8,64,1024]{2,1,0:T(8,128)} %bitcast.14), custom_call_target="tpu_custom_call" | custom-call | tf_op jit(solution)/shard_map/pallas_call | solution.py:246
  297.9 1.7 pad_maximum_fusion.1
  (2 shorter events, 0.0 us)
Async XLA Ops:
  0.0 13.5 %copy-start.3 = (s32[10,7]{0,1:T(8,128)S(1)}, s32[10,7]{0,1:T(8,128)}, u32[]{:S(2)}) copy-start(s32[10,7]{0,1:T(8,128)} %param.6) | copy-start | bytes 844
  0.0 14.2 %copy-start.2 = (s32[10,7]{0,1:T(8,128)S(1)}, s32[10,7]{0,1:T(8,128)}, u32[]{:S(2)}) copy-start(s32[10,7]{0,1:T(8,128)} %param.7) | copy-start | bytes 844
  0.0 77.6 %collective-permute-start = (bf16[1280,2048]{1,0:T(8,128)(2,1)}, bf16[1280,2048]{1,0:T(8,128)(2,1)}, u32[]{:S(2)}, u32[]{:S(2)}) collective-permute-start(bf16[1280,2048]{1,0:T(8,128)(2,1)} %param.4), channel_id=1, source_target_pairs={{0,1},{1,0},{2,3},{3,2},{4,5},{5,4},{6,7},{7,6},{8,9},{9,8},{10,11... | collective-permute-start | bytes 15728648 | tf_op jit(solution)/shard_map/ppermute | solution.py:338
  2.7 33.8 %collective-permute-start.3 = (bf16[256,2048]{1,0:T(8,128)(2,1)}, bf16[256,2048]{1,0:T(8,128)(2,1)S(1)}, u32[]{:S(2)}, u32[]{:S(2)}) collective-permute-start(bf16[256,2048]{1,0:T(8,128)(2,1)} %get-tuple-element.14), channel_id=1, source_target_pairs={{0,2},{130,4},{4,6},{134,8},{8,10},{138,12},{12,14},{142,16},{16,1... | collective-permute-start | bytes 3145736 | tf_op jit(solution)/shard_map/ppermute | solution.py:43
  9.1 27.5 %collective-permute-start.1 = (bf16[5,7,64,128]{3,2,1,0:T(8,128)(2,1)}, bf16[5,7,64,128]{3,2,1,0:T(8,128)(2,1)}, u32[]{:S(2)}, u32[]{:S(2)}) collective-permute-start(bf16[5,7,64,128]{3,2,1,0:T(8,128)(2,1)} %constant_dynamic-slice_fusion), channel_id=1, source_target_pairs={{0,128},{128,0},{1,129},{129,1},{2,130},{130,2},{3,131},{131,3},{4... | collective-permute-start | bytes 1720328 | tf_op jit(solution)/shard_map/ppermute | solution.py:327
  10.0 41.2 %collective-permute-start.4 = (bf16[256,2048]{1,0:T(8,128)(2,1)S(1)}, bf16[256,2048]{1,0:T(8,128)(2,1)S(1)}, u32[]{:S(2)}, u32[]{:S(2)}) collective-permute-start(bf16[256,2048]{1,0:T(8,128)(2,1)S(1)} %get-tuple-element.13), channel_id=1, source_target_pairs={{2,0},{132,2},{6,4},{136,6},{10,8},{140,10},{14,12},{144,14},{18,1... | collective-permute-start | bytes 3145736 | tf_op jit(solution)/shard_map/ppermute | solution.py:44
  36.6 15.8 %collective-permute-start.2 = (bf16[5,7,64,128]{3,2,1,0:T(8,128)(2,1)}, bf16[5,7,64,128]{3,2,1,0:T(8,128)(2,1)S(1)}, u32[]{:S(2)}, u32[]{:S(2)}) collective-permute-start(bf16[5,7,64,128]{3,2,1,0:T(8,128)(2,1)} %collective-permute-done.1), channel_id=1, source_target_pairs={{0,1},{1,0},{2,3},{3,2},{4,5},{5,4},{6,7},{7,6},{8,9},{9,8},{10,11... | collective-permute-start | bytes 1720328 | tf_op jit(solution)/shard_map/ppermute | solution.py:328
  37.6 14.7 %copy-start.1 = (bf16[10,7,64,128]{3,2,1,0:T(8,128)(2,1)S(1)}, bf16[10,7,64,128]{3,2,1,0:T(8,128)(2,1)}, u32[]{:S(2)}) copy-start(bf16[10,7,64,128]{3,2,1,0:T(8,128)(2,1)} %param.5) | copy-start | bytes 3440644
  66.4 24.3 %slice-start = ((s8[5242880]{0:T(1024)(128)(4,1)}), s8[1048576]{0:T(1024)(128)(4,1)S(1)}, s32[]{:S(2)}) async-start(s8[5242880]{0:T(1024)(128)(4,1)} %bitcast.10), calls=%async_computation | async-start | bytes 2097152
  77.6 13.2 %slice-start.1 = ((s8[5242880]{0:T(1024)(128)(4,1)}), s8[4194304]{0:T(1024)(128)(4,1)S(1)}, s32[]{:S(2)}) async-start(s8[5242880]{0:T(1024)(128)(4,1)} %bitcast.10), calls=%async_computation.1 | async-start | bytes 8388608
  86.6 4.1 %copy-start = (bf16[1280,1024]{1,0:T(8,128)(2,1)S(1)}, bf16[1280,1024]{1,0:T(8,128)(2,1)}, u32[]{:S(2)}) copy-start(bf16[1280,1024]{1,0:T(8,128)(2,1)} %shard_map.46) | copy-start | bytes 7864324

commit v5 on v2

--- a/solution.py
+++ b/solution.py
@@ -46,6 +46,13 @@
 
 def take_chunk(x, index, dim):
     return lax.dynamic_index_in_dim(x, index, axis=dim, keepdims=False)
+
+
+def read_chunk(x, index, columns):
+    if len(x.shape) == 3:
+        return x[index, :, columns]
+    value = x[:, index, :, columns]
+    return value.reshape(value.shape[0] * value.shape[1], value.shape[2])
 
 
 def multi_ring_kernel(plan, pair_axis, *refs):
@@ -93,11 +100,11 @@
                 chunk_f = lax.rem(p - step - 1 + 2 * n, n)
                 chunk_b = lax.rem(p + step + 1, n)
                 if step == 0:
-                    ring["out_f"][slot] = x[chunk_f, :, :half]
-                    ring["out_b"][slot] = x[chunk_b, :, half:]
+                    ring["out_f"][slot] = read_chunk(x, chunk_f, slice(None, half))
+                    ring["out_b"][slot] = read_chunk(x, chunk_b, slice(half, None))
                 else:
-                    ring["out_f"][slot] = ring["in_f"][1 - slot] + x[chunk_f, :, :half]
-                    ring["out_b"][slot] = ring["in_b"][1 - slot] + x[chunk_b, :, half:]
+                    ring["out_f"][slot] = ring["in_f"][1 - slot] + read_chunk(x, chunk_f, slice(None, half))
+                    ring["out_b"][slot] = ring["in_b"][1 - slot] + read_chunk(x, chunk_b, slice(half, None))
                     if step <= n - 3:
                         pl.semaphore_signal(
                             ring["credit"].at[0], 1, device_id={ring["axis"]: ring["left"]}, device_id_type=mesh
@@ -128,8 +135,8 @@
         half = x.shape[-1] // 2
         last = (n - 2) % 2
         total = ring["o"] if pair_axis is None else pair_scratch[4 * index]
-        total[:, :half] = ring["in_f"][last] + x[p, :, :half]
-        total[:, half:] = ring["in_b"][last] + x[p, :, half:]
+        total[:, :half] = ring["in_f"][last] + read_chunk(x, p, slice(None, half))
+        total[:, half:] = ring["in_b"][last] + read_chunk(x, p, slice(half, None))
     if pair_axis is None:
         return
     mine = lax.axis_index(pair_axis)
@@ -156,8 +163,12 @@
 def multi_ring_reduce(inputs, plan, collective_id, pair_axis=None):
     vmem = pltpu.VMEM
     scratch = []
+    out_shapes = []
     for x in inputs:
-        _, rows, width = x.shape
+        rows, width = x.shape[-2], x.shape[-1]
+        if len(x.shape) == 4:
+            rows *= x.shape[0]
+        out_shapes.append((rows, width))
         half = width // 2
         scratch += [vmem((2, rows, half), x.dtype) for _ in range(4)]
         scratch += [
@@ -165,17 +176,16 @@
             pltpu.SemaphoreType.DMA((2, 2)),
             pltpu.SemaphoreType.REGULAR((2,)),
         ]
-    out_shapes = [x.shape[1:] for x in inputs]
     if pair_axis is not None:
-        for x in inputs:
-            _, rows, width = x.shape
+        for rows, width in list(out_shapes):
+            x = inputs[0]
             scratch += [
                 vmem((rows, width), x.dtype),
                 vmem((rows // 2, width), x.dtype),
                 pltpu.SemaphoreType.DMA(()),
                 pltpu.SemaphoreType.DMA(()),
             ]
-        out_shapes = [(x.shape[1] // 2, x.shape[2]) for x in inputs]
+        out_shapes = [(rows // 2, width) for rows, width in out_shapes]
     return pl.pallas_call(
         functools.partial(multi_ring_kernel, tuple(plan), pair_axis),
         out_shape=[jax.ShapeDtypeStruct(shape, x.dtype) for shape, x in zip(out_shapes, inputs)],
@@ -311,7 +321,11 @@
                 shape = shape[1:]
                 names[index].remove(pair_axis)
             shapes.append(shape)
-            inputs.append(jnp.moveaxis(x, dim, 0).reshape(sizes[axis], -1, x.shape[-1]))
+            if dim == 0:
+                inputs.append(x.reshape(sizes[axis], -1, x.shape[-1]))
+            else:
+                outer = math.prod(x.shape[:dim])
+                inputs.append(x.reshape(outer, sizes[axis], -1, x.shape[-1]))
         outs = multi_ring_reduce(
             inputs, [(axis, sizes[axis]) for axis in axes], stage, pair_axis
         )

time: 255 us -> 254 us (level)
  local copies, waits for them, and re-layouts: 18.1 us -> 13.4 us
    reshape x1 -> x0, local copies, waits for them, and re-layouts: 4.11 us -> none  [per_device(): part.reshape(tuple((size for _, size in ROW_PARTS)) + (chunk_rows, width))]
where the time goes in v5:
time: 254 us; the launch traced here: 253 us
  Pallas kernels  177 us (70%)
  waiting for transfers between devices  29.3 us (12%)
  matrix products  19.1 us (8%)
  local copies, waits for them, and re-layouts  13.4 us (5%)
  starting transfers between devices  8.88 us (3%)
  other arithmetic  4.79 us (2%)
    pallas_call x2, Pallas kernels, multi_ring_reduce(): pl.pallas_call(functools.partial(multi_ring_kernel, tuple(plan), pair_axi...  155 us
    pallas_call x2, Pallas kernels, apply_operator(): pl.pallas_call(applied_kernel, grid_spec=grid_spec, out_shape=jax.ShapeDt...  22.1 us
    ppermute x1, waiting for transfers between devices, per_device(): from_sec = lax.ppermute(mine, 'sec', [(0, 1), (1, 0)])  21.3 us
    dot_general x2, matrix products, per_device(): lax.dot_general(left_projector, applied, (((0,), (0,)), ((), ())), prefer...  19.1 us
    ppermute x1, waiting for transfers between devices, halo(): after = lax.ppermute(shard[:width], axes, after_pairs)  8.03 us
    unnamed x15, local copies, waits for them, and re-layouts  6.85 us
  transfers between devices with their start and end apart: 5, of which 2 were waited for; matrix products, arithmetic and copies ran while one was open for 7% of the time, Pallas kernels for 9%

profile of v5, /device:TPU:8, one launch (start us, length us, event | category | flops | bytes accessed | tf_op | source)
XLA Modules:
  0.0 252.6 jit_solution(17801260633947958681)
XLA Ops:
  0.0 0.0 copy-start.1
  0.0 0.0 copy-start.3
  0.0 0.0 copy-start.2
  0.0 0.1 collective-permute-start
  0.1 3.3 %fusion = (bf16[256,2048]{1,0:T(8,128)(2,1)}, bf16[256,2048]{1,0:T(8,128)(2,1)}) fusion(bf16[1280,2048]{1,0:T(8,128)(2,1)} %param.4), kind=kLoop, calls=%fused_computation.13 | loop fusion | bytes 4194304 | tf_op jit(solution)/shard_map/slice | solution.py:43
  3.4 4.4 %collective-permute-start.3 = (bf16[256,2048]{1,0:T(8,128)(2,1)}, bf16[256,2048]{1,0:T(8,128)(2,1)S(1)}, u32[]{:S(2)}, u32[]{:S(2)}) collective-permute-start(bf16[256,2048]{1,0:T(8,128)(2,1)} %get-tuple-element.14), channel_id=1, source_target_pairs={{0,2},{130,4},{4,6},{134,8},{8,10},{138,12},{12,14},{142,16},{16,1... | collective-permute-start | bytes 3145736 | tf_op jit(solution)/shard_map/ppermute | solution.py:42
  7.8 0.0 copy-done.1
  7.8 0.9 constant_dynamic-slice_fusion
  8.7 0.9 collective-permute-start.1
  9.6 3.4 %collective-permute-start.4 = (bf16[256,2048]{1,0:T(8,128)(2,1)}, bf16[256,2048]{1,0:T(8,128)(2,1)S(1)}, u32[]{:S(2)}, u32[]{:S(2)}) collective-permute-start(bf16[256,2048]{1,0:T(8,128)(2,1)} %get-tuple-element.13), channel_id=1, source_target_pairs={{2,0},{132,2},{6,4},{136,6},{10,8},{140,10},{14,12},{144,14},{18,1... | collective-permute-start | bytes 3145736 | tf_op jit(solution)/shard_map/ppermute | solution.py:43
  13.1 0.0 copy-done.3
  13.1 0.1 copy.7
  13.2 0.6 reshape.8.offsets_ref
  13.8 0.0 copy-done.2
  13.8 0.1 copy.8
  13.9 0.7 reshape.9.mask_ref
  14.6 21.3 %collective-permute-done.1 = bf16[5,7,64,128]{3,2,1,0:T(8,128)(2,1)} collective-permute-done((bf16[5,7,64,128]{3,2,1,0:T(8,128)(2,1)}, bf16[5,7,64,128]{3,2,1,0:T(8,128)(2,1)}, u32[]{:S(2)}, u32[]{:S(2)}) %collective-permute-start.1) | collective-permute-done | bytes 573472 | tf_op jit(solution)/shard_map/ppermute | solution.py:270
  35.9 0.0 collective-permute-start.2
  35.9 0.0 collective-permute-done.3
  35.9 1.0 constant_dynamic-update-slice_fusion.2
  36.9 5.7 %constant_dynamic-update-slice_fusion.1 = bf16[1792,2048]{1,0:T(8,128)(2,1)} fusion(bf16[1792,2048]{1,0:T(8,128)(2,1)} %constant_dynamic-update-slice_fusion.2, bf16[1280,2048]{1,0:T(8,128)(2,1)} %param.4), kind=kLoop, calls=%fused_computation.9 | loop fusion | bytes 10485760
  42.6 8.0 %collective-permute-done.4 = bf16[256,2048]{1,0:T(8,128)(2,1)S(1)} collective-permute-done((bf16[256,2048]{1,0:T(8,128)(2,1)}, bf16[256,2048]{1,0:T(8,128)(2,1)S(1)}, u32[]{:S(2)}, u32[]{:S(2)}) %collective-permute-start.4) | collective-permute-done | bytes 1048608 | tf_op jit(solution)/shard_map/ppermute | solution.py:43
  50.7 1.1 constant_dynamic-update-slice_fusion.ext_ref
  51.7 0.0 collective-permute-done.2
  51.7 1.5 broadcast_select_fusion.4
  53.2 1.6 pad_maximum_fusion.ops_ref
  54.8 11.0 %shard_map.47 = bf16[1280,1024]{1,0:T(8,128)(2,1)} custom-call(s32[70]{0:T(128)} %reshape.8.offsets_ref, s32[70]{0:T(128)} %reshape.9.mask_ref, bf16[10,7,128,128]{3,2,1,0:T(8,128)(2,1)} %pad_maximum_fusion.ops_ref, bf16[1792,2048]{1,0:T(8,128)(2,1)} %constant_dynamic-update-slice_fusion.ext_ref), custom_call_target="tpu_custom_call" | custom-call | flops 2348810240 | bytes 11010048 | tf_op jit(solution)/shard_map/pallas_call | solution.py:248
  65.8 0.0 slice-start
  65.8 11.1 %shard_map.46 = bf16[1280,1024]{1,0:T(8,128)(2,1)} custom-call(s32[70]{0:T(128)} %reshape.8.offsets_ref, s32[70]{0:T(128)} %reshape.9.mask_ref, bf16[10,7,128,128]{3,2,1,0:T(8,128)(2,1)} %pad_maximum_fusion.ops_ref, bf16[1792,2048]{1,0:T(8,128)(2,1)} %constant_dynamic-update-slice_fusion.ext_ref), custom_call_target="tpu_custom_call" | custom-call | flops 2348810240 | bytes 11010048 | tf_op jit(solution)/shard_map/pallas_call | solution.py:248
  76.9 0.0 slice-start.1
  76.9 0.0 copy-start
  76.9 0.0 collective-permute-done
  76.9 10.8 %convolution_multiply_fusion.1 = f32[2048,1024]{1,0:T(8,128)} fusion(bf16[1280,1024]{1,0:T(8,128)(2,1)} %shard_map.46, bf16[1280,2048]{1,0:T(8,128)(2,1)} %param.4, bf16[1280,2048]{1,0:T(8,128)(2,1)} %collective-permute-done, pred[]{:T(512)S(6)} %eq.10), kind=kOutput, calls=%fused_computation.2 | convolution fusion | flops 5373427712 | bytes 21495808 | tf_op jit(solution)/shard_map/dot_general | solution.py:299
  87.8 0.0 slice-done
  87.8 0.0 slice-done.1
  87.8 0.0 copy-done
  87.8 8.2 %convolution_multiply_fusion = f32[2048,1024]{1,0:T(8,128)} fusion(bf16[1280,1024]{1,0:T(8,128)(2,1)S(1)} %copy-done, bf16[1280,2048]{1,0:T(8,128)(2,1)S(1)} %bitcast.7, bf16[1280,2048]{1,0:T(8,128)(2,1)} %collective-permute-done, pred[]{:T(512)S(6)} %eq.10), kind=kOutput, calls=%fused_computation.1 | convolution fusion | flops 5373427712 | bytes 21495808 | tf_op jit(solution)/shard_map/dot_general | solution.py:299
  96.0 105.5 %shard_map.48 = (f32[256,1024]{1,0:T(8,128)}, f32[512,1024]{1,0:T(8,128)}) custom-call(f32[8,256,1024]{2,1,0:T(8,128)} %bitcast.8, f32[8,4,64,1024]{3,2,1,0:T(8,128)} %bitcast.9), custom_call_target="tpu_custom_call" | custom-call | tf_op jit(solution)/shard_map/pallas_call | solution.py:189
  201.6 49.4 %shard_map.49 = (f32[32,1024]{1,0:T(8,128)}, f32[32,1024]{1,0:T(8,128)}) custom-call(f32[4,64,1024]{2,1,0:T(8,128)} %bitcast.11, f32[8,64,1024]{2,1,0:T(8,128)} %bitcast.10), custom_call_target="tpu_custom_call" | custom-call | tf_op jit(solution)/shard_map/pallas_call | solution.py:189
  250.9 1.7 pad_maximum_fusion.1
  (2 shorter events, 0.0 us)
Async XLA Ops:
  0.0 7.8 %copy-start.1 = (bf16[10,7,64,128]{3,2,1,0:T(8,128)(2,1)S(1)}, bf16[10,7,64,128]{3,2,1,0:T(8,128)(2,1)}, u32[]{:S(2)}) copy-start(bf16[10,7,64,128]{3,2,1,0:T(8,128)(2,1)} %param.5) | copy-start | bytes 3440644
  0.0 13.1 %copy-start.3 = (s32[10,7]{0,1:T(8,128)S(1)}, s32[10,7]{0,1:T(8,128)}, u32[]{:S(2)}) copy-start(s32[10,7]{0,1:T(8,128)} %param.6) | copy-start | bytes 844
  0.0 13.8 %copy-start.2 = (s32[10,7]{0,1:T(8,128)S(1)}, s32[10,7]{0,1:T(8,128)}, u32[]{:S(2)}) copy-start(s32[10,7]{0,1:T(8,128)} %param.7) | copy-start | bytes 844
  0.0 76.9 %collective-permute-start = (bf16[1280,2048]{1,0:T(8,128)(2,1)}, bf16[1280,2048]{1,0:T(8,128)(2,1)}, u32[]{:S(2)}, u32[]{:S(2)}) collective-permute-start(bf16[1280,2048]{1,0:T(8,128)(2,1)} %param.4), channel_id=1, source_target_pairs={{0,1},{1,0},{2,3},{3,2},{4,5},{5,4},{6,7},{7,6},{8,9},{9,8},{10,11... | collective-permute-start | bytes 15728648 | tf_op jit(solution)/shard_map/ppermute | solution.py:281
  3.4 32.5 %collective-permute-start.3 = (bf16[256,2048]{1,0:T(8,128)(2,1)}, bf16[256,2048]{1,0:T(8,128)(2,1)S(1)}, u32[]{:S(2)}, u32[]{:S(2)}) collective-permute-start(bf16[256,2048]{1,0:T(8,128)(2,1)} %get-tuple-element.14), channel_id=1, source_target_pairs={{0,2},{130,4},{4,6},{134,8},{8,10},{138,12},{12,14},{142,16},{16,1... | collective-permute-start | bytes 3145736 | tf_op jit(solution)/shard_map/ppermute | solution.py:42
  8.7 27.2 %collective-permute-start.1 = (bf16[5,7,64,128]{3,2,1,0:T(8,128)(2,1)}, bf16[5,7,64,128]{3,2,1,0:T(8,128)(2,1)}, u32[]{:S(2)}, u32[]{:S(2)}) collective-permute-start(bf16[5,7,64,128]{3,2,1,0:T(8,128)(2,1)} %constant_dynamic-slice_fusion), channel_id=1, source_target_pairs={{0,128},{128,0},{1,129},{129,1},{2,130},{130,2},{3,131},{131,3},{4... | collective-permute-start | bytes 1720328 | tf_op jit(solution)/shard_map/ppermute | solution.py:270
  9.6 41.0 %collective-permute-start.4 = (bf16[256,2048]{1,0:T(8,128)(2,1)}, bf16[256,2048]{1,0:T(8,128)(2,1)S(1)}, u32[]{:S(2)}, u32[]{:S(2)}) collective-permute-start(bf16[256,2048]{1,0:T(8,128)(2,1)} %get-tuple-element.13), channel_id=1, source_target_pairs={{2,0},{132,2},{6,4},{136,6},{10,8},{140,10},{14,12},{144,14},{18,1... | collective-permute-start | bytes 3145736 | tf_op jit(solution)/shard_map/ppermute | solution.py:43
  35.9 15.8 %collective-permute-start.2 = (bf16[5,7,64,128]{3,2,1,0:T(8,128)(2,1)}, bf16[5,7,64,128]{3,2,1,0:T(8,128)(2,1)S(1)}, u32[]{:S(2)}, u32[]{:S(2)}) collective-permute-start(bf16[5,7,64,128]{3,2,1,0:T(8,128)(2,1)} %collective-permute-done.1), channel_id=1, source_target_pairs={{0,1},{1,0},{2,3},{3,2},{4,5},{5,4},{6,7},{7,6},{8,9},{9,8},{10,11... | collective-permute-start | bytes 1720328 | tf_op jit(solution)/shard_map/ppermute | solution.py:271
  65.8 22.0 %slice-start = ((s8[5242880]{0:T(1024)(128)(4,1)}), s8[1048576]{0:T(1024)(128)(4,1)S(1)}, s32[]{:S(2)}) async-start(s8[5242880]{0:T(1024)(128)(4,1)} %bitcast.6), calls=%async_computation | async-start | bytes 2097152
  76.9 10.9 %slice-start.1 = ((s8[5242880]{0:T(1024)(128)(4,1)}), s8[4194304]{0:T(1024)(128)(4,1)S(1)}, s32[]{:S(2)}) async-start(s8[5242880]{0:T(1024)(128)(4,1)} %bitcast.6), calls=%async_computation.1 | async-start | bytes 8388608
  76.9 10.9 %copy-start = (bf16[1280,1024]{1,0:T(8,128)(2,1)S(1)}, bf16[1280,1024]{1,0:T(8,128)(2,1)}, u32[]{:S(2)}) copy-start(bf16[1280,1024]{1,0:T(8,128)(2,1)} %shard_map.47) | copy-start | bytes 7864324

commit v6 on v5

--- a/solution.py
+++ b/solution.py
@@ -103,26 +103,16 @@
                     ring["out_f"][slot] = read_chunk(x, chunk_f, slice(None, half))
                     ring["out_b"][slot] = read_chunk(x, chunk_b, slice(half, None))
                 else:
-                    ring["out_f"][slot] = ring["in_f"][1 - slot] + read_chunk(x, chunk_f, slice(None, half))
-                    ring["out_b"][slot] = ring["in_b"][1 - slot] + read_chunk(x, chunk_b, slice(half, None))
-                    if step <= n - 3:
-                        pl.semaphore_signal(
-                            ring["credit"].at[0], 1, device_id={ring["axis"]: ring["left"]}, device_id_type=mesh
-                        )
-                        pl.semaphore_signal(
-                            ring["credit"].at[1], 1, device_id={ring["axis"]: ring["right"]}, device_id_type=mesh
-                        )
-                if step >= 2:
-                    pl.semaphore_wait(ring["credit"].at[0], 1)
-                    pl.semaphore_wait(ring["credit"].at[1], 1)
+                    ring["out_f"][slot] = ring["in_f"][step - 1] + read_chunk(x, chunk_f, slice(None, half))
+                    ring["out_b"][slot] = ring["in_b"][step - 1] + read_chunk(x, chunk_b, slice(half, None))
                 copy_f = pltpu.make_async_remote_copy(
-                    src_ref=ring["out_f"].at[slot], dst_ref=ring["in_f"].at[slot],
-                    send_sem=ring["send"].at[0, slot], recv_sem=ring["recv"].at[0, slot],
+                    src_ref=ring["out_f"].at[slot], dst_ref=ring["in_f"].at[step],
+                    send_sem=ring["send"].at[0, slot], recv_sem=ring["recv"].at[0, step],
                     device_id={ring["axis"]: ring["right"]}, device_id_type=mesh,
                 )
                 copy_b = pltpu.make_async_remote_copy(
-                    src_ref=ring["out_b"].at[slot], dst_ref=ring["in_b"].at[slot],
-                    send_sem=ring["send"].at[1, slot], recv_sem=ring["recv"].at[1, slot],
+                    src_ref=ring["out_b"].at[slot], dst_ref=ring["in_b"].at[step],
+                    send_sem=ring["send"].at[1, slot], recv_sem=ring["recv"].at[1, step],
                     device_id={ring["axis"]: ring["left"]}, device_id_type=mesh,
                 )
                 copy_f.start()
@@ -133,7 +123,7 @@
             copy.wait()
         n, p, x = ring["n"], ring["p"], ring["x"]
         half = x.shape[-1] // 2
-        last = (n - 2) % 2
+        last = n - 2
         total = ring["o"] if pair_axis is None else pair_scratch[4 * index]
         total[:, :half] = ring["in_f"][last] + read_chunk(x, p, slice(None, half))
         total[:, half:] = ring["in_b"][last] + read_chunk(x, p, slice(half, None))
@@ -164,16 +154,19 @@
     vmem = pltpu.VMEM
     scratch = []
     out_shapes = []
-    for x in inputs:
+    for x, (_, n) in zip(inputs, plan):
         rows, width = x.shape[-2], x.shape[-1]
         if len(x.shape) == 4:
             rows *= x.shape[0]
         out_shapes.append((rows, width))
         half = width // 2
-        scratch += [vmem((2, rows, half), x.dtype) for _ in range(4)]
         scratch += [
+            vmem((2, rows, half), x.dtype),
+            vmem((n - 1, rows, half), x.dtype),
+            vmem((2, rows, half), x.dtype),
+            vmem((n - 1, rows, half), x.dtype),
             pltpu.SemaphoreType.DMA((2, 2)),
-            pltpu.SemaphoreType.DMA((2, 2)),
+            pltpu.SemaphoreType.DMA((2, n - 1)),
             pltpu.SemaphoreType.REGULAR((2,)),
         ]
     if pair_axis is not None:

time: 254 us -> 254 us (level)
  no operation moved by 1% of the time
where the time goes in v6:
time: 254 us; the launch traced here: 253 us
  Pallas kernels  177 us (70%)
  waiting for transfers between devices  29.3 us (12%)
  matrix products  19.1 us (8%)
  local copies, waits for them, and re-layouts  13.4 us (5%)
  starting transfers between devices  8.88 us (3%)
  other arithmetic  4.79 us (2%)
    pallas_call x2, Pallas kernels, multi_ring_reduce(): pl.pallas_call(functools.partial(multi_ring_kernel, tuple(plan), pair_axi...  155 us
    pallas_call x2, Pallas kernels, apply_operator(): pl.pallas_call(applied_kernel, grid_spec=grid_spec, out_shape=jax.ShapeDt...  22.1 us
    ppermute x1, waiting for transfers between devices, per_device(): from_sec = lax.ppermute(mine, 'sec', [(0, 1), (1, 0)])  21.3 us
    dot_general x2, matrix products, per_device(): lax.dot_general(left_projector, applied, (((0,), (0,)), ((), ())), prefer...  19.1 us
    ppermute x1, waiting for transfers between devices, halo(): after = lax.ppermute(shard[:width], axes, after_pairs)  8.03 us
    unnamed x15, local copies, waits for them, and re-layouts  6.85 us
  transfers between devices with their start and end apart: 5, of which 2 were waited for; matrix products, arithmetic and copies ran while one was open for 7% of the time, Pallas kernels for 9%

profile of v6, /device:TPU:8, one launch (start us, length us, event | category | flops | bytes accessed | tf_op | source)
XLA Modules:
  0.0 252.8 jit_solution(9252858250517743400)
XLA Ops:
  0.0 0.0 copy-start.1
  0.0 0.0 copy-start.3
  0.0 0.0 copy-start.2
  0.0 0.1 collective-permute-start
  0.1 3.3 %fusion = (bf16[256,2048]{1,0:T(8,128)(2,1)}, bf16[256,2048]{1,0:T(8,128)(2,1)}) fusion(bf16[1280,2048]{1,0:T(8,128)(2,1)} %param.4), kind=kLoop, calls=%fused_computation.13 | loop fusion | bytes 4194304 | tf_op jit(solution)/shard_map/slice | solution.py:43
  3.4 4.4 %collective-permute-start.3 = (bf16[256,2048]{1,0:T(8,128)(2,1)}, bf16[256,2048]{1,0:T(8,128)(2,1)S(1)}, u32[]{:S(2)}, u32[]{:S(2)}) collective-permute-start(bf16[256,2048]{1,0:T(8,128)(2,1)} %get-tuple-element.14), channel_id=1, source_target_pairs={{0,2},{130,4},{4,6},{134,8},{8,10},{138,12},{12,14},{142,16},{16,1... | collective-permute-start | bytes 3145736 | tf_op jit(solution)/shard_map/ppermute | solution.py:42
  7.8 0.0 copy-done.1
  7.8 0.9 constant_dynamic-slice_fusion
  8.7 0.9 collective-permute-start.1
  9.6 3.4 %collective-permute-start.4 = (bf16[256,2048]{1,0:T(8,128)(2,1)}, bf16[256,2048]{1,0:T(8,128)(2,1)S(1)}, u32[]{:S(2)}, u32[]{:S(2)}) collective-permute-start(bf16[256,2048]{1,0:T(8,128)(2,1)} %get-tuple-element.13), channel_id=1, source_target_pairs={{2,0},{132,2},{6,4},{136,6},{10,8},{140,10},{14,12},{144,14},{18,1... | collective-permute-start | bytes 3145736 | tf_op jit(solution)/shard_map/ppermute | solution.py:43
  13.1 0.0 copy-done.3
  13.1 0.1 copy.7
  13.2 0.6 reshape.8.offsets_ref
  13.8 0.0 copy-done.2
  13.8 0.1 copy.8
  13.9 0.7 reshape.9.mask_ref
  14.6 21.3 %collective-permute-done.1 = bf16[5,7,64,128]{3,2,1,0:T(8,128)(2,1)} collective-permute-done((bf16[5,7,64,128]{3,2,1,0:T(8,128)(2,1)}, bf16[5,7,64,128]{3,2,1,0:T(8,128)(2,1)}, u32[]{:S(2)}, u32[]{:S(2)}) %collective-permute-start.1) | collective-permute-done | bytes 573472 | tf_op jit(solution)/shard_map/ppermute | solution.py:263
  35.9 0.0 collective-permute-start.2
  35.9 0.0 collective-permute-done.3
  35.9 1.0 constant_dynamic-update-slice_fusion.2
  36.9 5.7 %constant_dynamic-update-slice_fusion.1 = bf16[1792,2048]{1,0:T(8,128)(2,1)} fusion(bf16[1792,2048]{1,0:T(8,128)(2,1)} %constant_dynamic-update-slice_fusion.2, bf16[1280,2048]{1,0:T(8,128)(2,1)} %param.4), kind=kLoop, calls=%fused_computation.9 | loop fusion | bytes 10485760
  42.6 8.0 %collective-permute-done.4 = bf16[256,2048]{1,0:T(8,128)(2,1)S(1)} collective-permute-done((bf16[256,2048]{1,0:T(8,128)(2,1)}, bf16[256,2048]{1,0:T(8,128)(2,1)S(1)}, u32[]{:S(2)}, u32[]{:S(2)}) %collective-permute-start.4) | collective-permute-done | bytes 1048608 | tf_op jit(solution)/shard_map/ppermute | solution.py:43
  50.7 1.1 constant_dynamic-update-slice_fusion.ext_ref
  51.7 0.0 collective-permute-done.2
  51.7 1.5 broadcast_select_fusion.4
  53.2 1.6 pad_maximum_fusion.ops_ref
  54.8 11.0 %shard_map.47 = bf16[1280,1024]{1,0:T(8,128)(2,1)} custom-call(s32[70]{0:T(128)} %reshape.8.offsets_ref, s32[70]{0:T(128)} %reshape.9.mask_ref, bf16[10,7,128,128]{3,2,1,0:T(8,128)(2,1)} %pad_maximum_fusion.ops_ref, bf16[1792,2048]{1,0:T(8,128)(2,1)} %constant_dynamic-update-slice_fusion.ext_ref), custom_call_target="tpu_custom_call" | custom-call | flops 2348810240 | bytes 11010048 | tf_op jit(solution)/shard_map/pallas_call | solution.py:241
  65.8 0.0 slice-start
  65.8 11.1 %shard_map.46 = bf16[1280,1024]{1,0:T(8,128)(2,1)} custom-call(s32[70]{0:T(128)} %reshape.8.offsets_ref, s32[70]{0:T(128)} %reshape.9.mask_ref, bf16[10,7,128,128]{3,2,1,0:T(8,128)(2,1)} %pad_maximum_fusion.ops_ref, bf16[1792,2048]{1,0:T(8,128)(2,1)} %constant_dynamic-update-slice_fusion.ext_ref), custom_call_target="tpu_custom_call" | custom-call | flops 2348810240 | bytes 11010048 | tf_op jit(solution)/shard_map/pallas_call | solution.py:241
  76.9 0.0 slice-start.1
  76.9 0.0 copy-start
  76.9 0.0 collective-permute-done
  76.9 10.8 %convolution_multiply_fusion.1 = f32[2048,1024]{1,0:T(8,128)} fusion(bf16[1280,1024]{1,0:T(8,128)(2,1)} %shard_map.46, bf16[1280,2048]{1,0:T(8,128)(2,1)} %param.4, bf16[1280,2048]{1,0:T(8,128)(2,1)} %collective-permute-done, pred[]{:T(512)S(6)} %eq.10), kind=kOutput, calls=%fused_computation.2 | convolution fusion | flops 5373427712 | bytes 21495808 | tf_op jit(solution)/shard_map/dot_general | solution.py:292
  87.8 0.0 slice-done
  87.8 0.0 slice-done.1
  87.8 0.0 copy-done
  87.8 8.2 %convolution_multiply_fusion = f32[2048,1024]{1,0:T(8,128)} fusion(bf16[1280,1024]{1,0:T(8,128)(2,1)S(1)} %copy-done, bf16[1280,2048]{1,0:T(8,128)(2,1)S(1)} %bitcast.7, bf16[1280,2048]{1,0:T(8,128)(2,1)} %collective-permute-done, pred[]{:T(512)S(6)} %eq.10), kind=kOutput, calls=%fused_computation.1 | convolution fusion | flops 5373427712 | bytes 21495808 | tf_op jit(solution)/shard_map/dot_general | solution.py:292
  96.0 105.6 %shard_map.48 = (f32[256,1024]{1,0:T(8,128)}, f32[512,1024]{1,0:T(8,128)}) custom-call(f32[8,256,1024]{2,1,0:T(8,128)} %bitcast.8, f32[8,4,64,1024]{3,2,1,0:T(8,128)} %bitcast.9), custom_call_target="tpu_custom_call" | custom-call | tf_op jit(solution)/shard_map/pallas_call | solution.py:182
  201.6 49.5 %shard_map.49 = (f32[32,1024]{1,0:T(8,128)}, f32[32,1024]{1,0:T(8,128)}) custom-call(f32[4,64,1024]{2,1,0:T(8,128)} %bitcast.11, f32[8,64,1024]{2,1,0:T(8,128)} %bitcast.10), custom_call_target="tpu_custom_call" | custom-call | tf_op jit(solution)/shard_map/pallas_call | solution.py:182
  251.2 1.7 pad_maximum_fusion.1
  (2 shorter events, 0.0 us)
Async XLA Ops:
  0.0 7.8 %copy-start.1 = (bf16[10,7,64,128]{3,2,1,0:T(8,128)(2,1)S(1)}, bf16[10,7,64,128]{3,2,1,0:T(8,128)(2,1)}, u32[]{:S(2)}) copy-start(bf16[10,7,64,128]{3,2,1,0:T(8,128)(2,1)} %param.5) | copy-start | bytes 3440644
  0.0 13.1 %copy-start.3 = (s32[10,7]{0,1:T(8,128)S(1)}, s32[10,7]{0,1:T(8,128)}, u32[]{:S(2)}) copy-start(s32[10,7]{0,1:T(8,128)} %param.6) | copy-start | bytes 844
  0.0 13.8 %copy-start.2 = (s32[10,7]{0,1:T(8,128)S(1)}, s32[10,7]{0,1:T(8,128)}, u32[]{:S(2)}) copy-start(s32[10,7]{0,1:T(8,128)} %param.7) | copy-start | bytes 844
  0.0 76.9 %collective-permute-start = (bf16[1280,2048]{1,0:T(8,128)(2,1)}, bf16[1280,2048]{1,0:T(8,128)(2,1)}, u32[]{:S(2)}, u32[]{:S(2)}) collective-permute-start(bf16[1280,2048]{1,0:T(8,128)(2,1)} %param.4), channel_id=1, source_target_pairs={{0,1},{1,0},{2,3},{3,2},{4,5},{5,4},{6,7},{7,6},{8,9},{9,8},{10,11... | collective-permute-start | bytes 15728648 | tf_op jit(solution)/shard_map/ppermute | solution.py:274
  3.4 32.5 %collective-permute-start.3 = (bf16[256,2048]{1,0:T(8,128)(2,1)}, bf16[256,2048]{1,0:T(8,128)(2,1)S(1)}, u32[]{:S(2)}, u32[]{:S(2)}) collective-permute-start(bf16[256,2048]{1,0:T(8,128)(2,1)} %get-tuple-element.14), channel_id=1, source_target_pairs={{0,2},{130,4},{4,6},{134,8},{8,10},{138,12},{12,14},{142,16},{16,1... | collective-permute-start | bytes 3145736 | tf_op jit(solution)/shard_map/ppermute | solution.py:42
  8.7 27.2 %collective-permute-start.1 = (bf16[5,7,64,128]{3,2,1,0:T(8,128)(2,1)}, bf16[5,7,64,128]{3,2,1,0:T(8,128)(2,1)}, u32[]{:S(2)}, u32[]{:S(2)}) collective-permute-start(bf16[5,7,64,128]{3,2,1,0:T(8,128)(2,1)} %constant_dynamic-slice_fusion), channel_id=1, source_target_pairs={{0,128},{128,0},{1,129},{129,1},{2,130},{130,2},{3,131},{131,3},{4... | collective-permute-start | bytes 1720328 | tf_op jit(solution)/shard_map/ppermute | solution.py:263
  9.6 41.0 %collective-permute-start.4 = (bf16[256,2048]{1,0:T(8,128)(2,1)}, bf16[256,2048]{1,0:T(8,128)(2,1)S(1)}, u32[]{:S(2)}, u32[]{:S(2)}) collective-permute-start(bf16[256,2048]{1,0:T(8,128)(2,1)} %get-tuple-element.13), channel_id=1, source_target_pairs={{2,0},{132,2},{6,4},{136,6},{10,8},{140,10},{14,12},{144,14},{18,1... | collective-permute-start | bytes 3145736 | tf_op jit(solution)/shard_map/ppermute | solution.py:43
  35.9 15.8 %collective-permute-start.2 = (bf16[5,7,64,128]{3,2,1,0:T(8,128)(2,1)}, bf16[5,7,64,128]{3,2,1,0:T(8,128)(2,1)S(1)}, u32[]{:S(2)}, u32[]{:S(2)}) collective-permute-start(bf16[5,7,64,128]{3,2,1,0:T(8,128)(2,1)} %collective-permute-done.1), channel_id=1, source_target_pairs={{0,1},{1,0},{2,3},{3,2},{4,5},{5,4},{6,7},{7,6},{8,9},{9,8},{10,11... | collective-permute-start | bytes 1720328 | tf_op jit(solution)/shard_map/ppermute | solution.py:264
  65.8 22.0 %slice-start = ((s8[5242880]{0:T(1024)(128)(4,1)}), s8[1048576]{0:T(1024)(128)(4,1)S(1)}, s32[]{:S(2)}) async-start(s8[5242880]{0:T(1024)(128)(4,1)} %bitcast.6), calls=%async_computation | async-start | bytes 2097152
  76.9 10.9 %slice-start.1 = ((s8[5242880]{0:T(1024)(128)(4,1)}), s8[4194304]{0:T(1024)(128)(4,1)S(1)}, s32[]{:S(2)}) async-start(s8[5242880]{0:T(1024)(128)(4,1)} %bitcast.6), calls=%async_computation.1 | async-start | bytes 8388608
  76.9 10.9 %copy-start = (bf16[1280,1024]{1,0:T(8,128)(2,1)S(1)}, bf16[1280,1024]{1,0:T(8,128)(2,1)}, u32[]{:S(2)}) copy-start(bf16[1280,1024]{1,0:T(8,128)(2,1)} %shard_map.47) | copy-start | bytes 7864324

commit v7 on v0

--- a/solution.py
+++ b/solution.py
@@ -48,10 +48,18 @@
     return lax.dynamic_index_in_dim(x, index, axis=dim, keepdims=False)
 
 
-def multi_ring_kernel(plan, *refs):
+def read_chunk(x, index, columns):
+    if len(x.shape) == 3:
+        return x[index, :, columns]
+    value = x[:, index, :, columns]
+    return value.reshape(value.shape[0] * value.shape[1], value.shape[2])
+
+
+def multi_ring_kernel(plan, pairs, *refs):
     count = len(plan)
     x_refs, o_refs = refs[:count], refs[count : 2 * count]
-    scratch = refs[2 * count :]
+    scratch = refs[2 * count : 2 * count + 7 * count]
+    pair_scratch = refs[2 * count + 7 * count :]
     mesh = pl.DeviceIdType.MESH
     rings = []
     for index, (axis, n) in enumerate(plan):
@@ -70,7 +78,13 @@
     for ring in rings:
         for neighbour in (ring["left"], ring["right"]):
             pl.semaphore_signal(barrier, 1, device_id={ring["axis"]: neighbour}, device_id_type=mesh)
-    pl.semaphore_wait(barrier, 2 * count)
+    signals = 2 * count
+    pair_axes = sorted({pair[0] for pair in pairs if pair is not None})
+    for pair_axis in pair_axes:
+        partner = 1 - lax.axis_index(pair_axis)
+        pl.semaphore_signal(barrier, 1, device_id={pair_axis: partner}, device_id_type=mesh)
+        signals += 1
+    pl.semaphore_wait(barrier, signals)
 
     ticks = max(n - 1 for _, n in plan)
     for tick in range(ticks):
@@ -87,11 +101,11 @@
                 chunk_f = lax.rem(p - step - 1 + 2 * n, n)
                 chunk_b = lax.rem(p + step + 1, n)
                 if step == 0:
-                    ring["out_f"][slot] = x[chunk_f, :, :half]
-                    ring["out_b"][slot] = x[chunk_b, :, half:]
+                    ring["out_f"][slot] = read_chunk(x, chunk_f, slice(None, half))
+                    ring["out_b"][slot] = read_chunk(x, chunk_b, slice(half, None))
                 else:
-                    ring["out_f"][slot] = ring["in_f"][1 - slot] + x[chunk_f, :, :half]
-                    ring["out_b"][slot] = ring["in_b"][1 - slot] + x[chunk_b, :, half:]
+                    ring["out_f"][slot] = ring["in_f"][1 - slot] + read_chunk(x, chunk_f, slice(None, half))
+                    ring["out_b"][slot] = ring["in_b"][1 - slot] + read_chunk(x, chunk_b, slice(half, None))
                     if step <= n - 3:
                         pl.semaphore_signal(
                             ring["credit"].at[0], 1, device_id={ring["axis"]: ring["left"]}, device_id_type=mesh
@@ -115,21 +129,48 @@
                 copy_f.start()
                 copy_b.start()
                 ring["copies"] = (copy_f, copy_b)
-    for ring in rings:
+    pending = []
+    for index in sorted(range(count), key=lambda i: rings[i]["n"]):
+        ring = rings[index]
         for copy in ring["copies"]:
             copy.wait()
         n, p, x = ring["n"], ring["p"], ring["x"]
         half = x.shape[-1] // 2
         last = (n - 2) % 2
-        ring["o"][:, :half] = ring["in_f"][last] + x[p, :, :half]
-        ring["o"][:, half:] = ring["in_b"][last] + x[p, :, half:]
-
-
-def multi_ring_reduce(inputs, plan, collective_id):
+        forward = ring["in_f"][last] + read_chunk(x, p, slice(None, half))
+        backward = ring["in_b"][last] + read_chunk(x, p, slice(half, None))
+        if pairs[index] is None:
+            ring["o"][:, :half] = forward
+            ring["o"][:, half:] = backward
+            continue
+        pair_axis, _ = pairs[index]
+        total, got, send_sem, recv_sem = pair_scratch[4 * index : 4 * index + 4]
+        outer, _, rows, _ = total.shape
+        total[:, :, :, :half] = forward.reshape(outer, 2, rows, half)
+        total[:, :, :, half:] = backward.reshape(outer, 2, rows, half)
+        mine = lax.axis_index(pair_axis)
+        copy = pltpu.make_async_remote_copy(
+            src_ref=total.at[:, pl.ds(1 - mine, 1)], dst_ref=got,
+            send_sem=send_sem, recv_sem=recv_sem,
+            device_id={pair_axis: 1 - mine}, device_id_type=mesh,
+        )
+        copy.start()
+        pending.append((index, copy, mine))
+    for index, copy, mine in pending:
+        total, got = pair_scratch[4 * index : 4 * index + 2]
+        outer, _, rows, width = total.shape
+        copy.wait()
+        summed = got[...] + total[:, pl.ds(mine, 1)]
+        rings[index]["o"][...] = summed.reshape(outer * rows, width)
+
+
+def multi_ring_reduce(inputs, plan, collective_id, pairs):
     vmem = pltpu.VMEM
-    scratch = []
-    for x in inputs:
-        _, rows, width = x.shape
+    scratch, pair_scratch, out_shapes = [], [], []
+    for x, pair in zip(inputs, pairs):
+        rows, width = x.shape[-2], x.shape[-1]
+        if len(x.shape) == 4:
+            rows *= x.shape[0]
         half = width // 2
         scratch += [vmem((2, rows, half), x.dtype) for _ in range(4)]
         scratch += [
@@ -137,9 +178,22 @@
             pltpu.SemaphoreType.DMA((2, 2)),
             pltpu.SemaphoreType.REGULAR((2,)),
         ]
+        if pair is None:
+            out_shapes.append((rows, width))
+            pair_scratch += [vmem((8, 128), x.dtype), vmem((8, 128), x.dtype)]
+        else:
+            outer = pair[1]
+            inner = rows // (2 * outer)
+            out_shapes.append((rows // 2, width))
+            pair_scratch += [
+                vmem((outer, 2, inner, width), x.dtype),
+                vmem((outer, 1, inner, width), x.dtype),
+            ]
+        pair_scratch += [pltpu.SemaphoreType.DMA(()), pltpu.SemaphoreType.DMA(())]
+    scratch += pair_scratch
     return pl.pallas_call(
-        functools.partial(multi_ring_kernel, tuple(plan)),
-        out_shape=[jax.ShapeDtypeStruct(x.shape[1:], x.dtype) for x in inputs],
+        functools.partial(multi_ring_kernel, tuple(plan), tuple(pairs)),
+        out_shape=[jax.ShapeDtypeStruct(shape, x.dtype) for shape, x in zip(out_shapes, inputs)],
         in_specs=[pl.BlockSpec(memory_space=vmem) for _ in inputs],
         out_specs=[pl.BlockSpec(memory_space=vmem) for _ in inputs],
         scratch_shapes=scratch,
@@ -252,23 +306,24 @@
         )
         parts.append(part.reshape(tuple(size for _, size in ROW_PARTS) + (chunk_rows, width)))
         names.append(list(ROW))
-    for stage in range(len(ROW_PARTS)):
-        axes = [order[stage] for order, _ in ORDERS]
-        if sizes[axes[0]] == 2:
-            for index, axis in enumerate(axes):
-                dim = names[index].index(axis)
-                parts[index] = ring_sum(parts[index], dim, axis, 2)
-                names[index].remove(axis)
-            continue
-        inputs, shapes = [], []
-        for index, axis in enumerate(axes):
-            dim = names[index].index(axis)
-            x = parts[index]
-            shapes.append(x.shape[:dim] + x.shape[dim + 1 :])
-            inputs.append(jnp.moveaxis(x, dim, 0).reshape(sizes[axis], -1, x.shape[-1]))
-            names[index].remove(axis)
-        outs = multi_ring_reduce(inputs, [(axis, sizes[axis]) for axis in axes], stage)
-        parts = [out.reshape(shape) for out, shape in zip(outs, shapes)]
+    (first_order, _), (second_order, _) = ORDERS
+    assert first_order == ("z", "x", "y") and second_order == ("x", "z", "y")
+    nz, nx, ny = sizes["z"], sizes["x"], sizes["y"]
+    a, b = parts
+    width_a, width_b = a.shape[-1], b.shape[-1]
+    a, b = multi_ring_reduce(
+        [a.reshape(nz, -1, width_a), b.reshape(nz, nx, -1, width_b)],
+        [("z", nz), ("x", nx)],
+        0,
+        [None, ("y", nz)],
+    )
+    a, b = multi_ring_reduce(
+        [a.reshape(nx, -1, width_a), b.reshape(nz, -1, width_b)],
+        [("x", nx), ("z", nz)],
+        1,
+        [("y", 1), None],
+    )
+    parts = [a, b]
     pieces = parts
     return jnp.concatenate(pieces, axis=-1)
 

time: 258 us -> 251 us (0.973)
  Pallas kernels: 168 us -> 174 us
  local copies, waits for them, and re-layouts: 19.9 us -> 14 us
  waiting for transfers between devices: 33.6 us -> 29.5 us
  starting transfers between devices: 11.6 us -> 8.79 us
    pallas_call x2, Pallas kernels: 146 us -> 152 us  [multi_ring_reduce(): pl.pallas_call(functools.partial(multi_ring_kernel, tuple(plan), tuple(pa...]
    reshape x1 -> x0, local copies, waits for them, and re-layouts: 4.11 us -> none  [per_device(): part.reshape(tuple((size for _, size in ROW_PARTS)) + (chunk_rows, width))]
    ppermute x2 -> x0, waiting for transfers between devices: 4.02 us -> none  [ring_sum(): got = lax.ppermute(take_chunk(x, 1 - p, dim), axis, partner)]
    ppermute x2 -> x0, starting transfers between devices: 2.81 us -> none  [ring_sum(): got = lax.ppermute(take_chunk(x, 1 - p, dim), axis, partner)]
  transfers between devices with their start and end apart: 7 -> 5, of which waited for: 4 -> 2; matrix products, arithmetic and copies ran while one was open for 7% -> 7% of each run, Pallas kernels for 9% -> 9%
where the time goes in v7:
time: 251 us; the launch traced here: 250 us
  Pallas kernels  174 us (69%)
  waiting for transfers between devices  29.5 us (12%)
  matrix products  19.1 us (8%)
  local copies, waits for them, and re-layouts  14 us (6%)
  starting transfers between devices  8.79 us (4%)
  other arithmetic  4.77 us (2%)
    pallas_call x2, Pallas kernels, multi_ring_reduce(): pl.pallas_call(functools.partial(multi_ring_kernel, tuple(plan), tuple(pa...  152 us
    pallas_call x2, Pallas kernels, apply_operator(): pl.pallas_call(applied_kernel, grid_spec=grid_spec, out_shape=jax.ShapeDt...  22.1 us
    ppermute x1, waiting for transfers between devices, per_device(): from_sec = lax.ppermute(mine, 'sec', [(0, 1), (1, 0)])  21.6 us
    dot_general x2, matrix products, per_device(): lax.dot_general(left_projector, applied, (((0,), (0,)), ((), ())), prefer...  19.1 us
    ppermute x1, waiting for transfers between devices, halo(): after = lax.ppermute(shard[:width], axes, after_pairs)  7.88 us
    unnamed x15, local copies, waits for them, and re-layouts  6.95 us
  transfers between devices with their start and end apart: 5, of which 2 were waited for; matrix products, arithmetic and copies ran while one was open for 7% of the time, Pallas kernels for 9%

profile of v7, /device:TPU:8, one launch (start us, length us, event | category | flops | bytes accessed | tf_op | source)
XLA Modules:
  0.0 250.1 jit_solution(188756554730444999)
XLA Ops:
  0.0 0.0 copy-start.3
  0.0 0.0 copy-start.2
  0.0 0.0 collective-permute-start
  0.0 2.7 %fusion = (bf16[256,2048]{1,0:T(8,128)(2,1)S(1)}, bf16[256,2048]{1,0:T(8,128)(2,1)}) fusion(bf16[1280,2048]{1,0:T(8,128)(2,1)} %param.4), kind=kLoop, calls=%fused_computation.13 | loop fusion | bytes 4194304 | tf_op jit(solution)/shard_map/slice | solution.py:43
  2.7 4.4 %collective-permute-start.3 = (bf16[256,2048]{1,0:T(8,128)(2,1)}, bf16[256,2048]{1,0:T(8,128)(2,1)S(1)}, u32[]{:S(2)}, u32[]{:S(2)}) collective-permute-start(bf16[256,2048]{1,0:T(8,128)(2,1)} %get-tuple-element.14), channel_id=1, source_target_pairs={{0,2},{130,4},{4,6},{134,8},{8,10},{138,12},{12,14},{142,16},{16,1... | collective-permute-start | bytes 3145736 | tf_op jit(solution)/shard_map/ppermute | solution.py:42
  7.2 1.9 constant_dynamic-slice_fusion
  9.1 0.9 collective-permute-start.1
  10.0 3.4 %collective-permute-start.4 = (bf16[256,2048]{1,0:T(8,128)(2,1)S(1)}, bf16[256,2048]{1,0:T(8,128)(2,1)S(1)}, u32[]{:S(2)}, u32[]{:S(2)}) collective-permute-start(bf16[256,2048]{1,0:T(8,128)(2,1)S(1)} %get-tuple-element.13), channel_id=1, source_target_pairs={{2,0},{132,2},{6,4},{136,6},{10,8},{140,10},{14,12},{144,14},{18,1... | collective-permute-start | bytes 3145736 | tf_op jit(solution)/shard_map/ppermute | solution.py:43
  13.5 0.0 copy-done.3
  13.5 0.1 copy.7
  13.6 0.6 reshape.14.offsets_ref
  14.2 0.0 copy-done.2
  14.2 0.1 copy.8
  14.3 0.6 reshape.15.mask_ref
  14.9 21.6 %collective-permute-done.1 = bf16[5,7,64,128]{3,2,1,0:T(8,128)(2,1)} collective-permute-done((bf16[5,7,64,128]{3,2,1,0:T(8,128)(2,1)}, bf16[5,7,64,128]{3,2,1,0:T(8,128)(2,1)}, u32[]{:S(2)}, u32[]{:S(2)}) %collective-permute-start.1) | collective-permute-done | bytes 573472 | tf_op jit(solution)/shard_map/ppermute | solution.py:275
  36.6 0.0 collective-permute-start.2
  36.6 0.0 collective-permute-done.3
  36.6 1.0 constant_dynamic-update-slice_fusion.2
  37.6 0.0 copy-start.1
  37.6 5.8 %constant_dynamic-update-slice_fusion.1 = bf16[1792,2048]{1,0:T(8,128)(2,1)} fusion(bf16[1792,2048]{1,0:T(8,128)(2,1)} %constant_dynamic-update-slice_fusion.2, bf16[1280,2048]{1,0:T(8,128)(2,1)} %param.4), kind=kLoop, calls=%fused_computation.9 | loop fusion | bytes 10485760
  43.4 7.9 %collective-permute-done.4 = bf16[256,2048]{1,0:T(8,128)(2,1)S(1)} collective-permute-done((bf16[256,2048]{1,0:T(8,128)(2,1)S(1)}, bf16[256,2048]{1,0:T(8,128)(2,1)S(1)}, u32[]{:S(2)}, u32[]{:S(2)}) %collective-permute-start.4) | collective-permute-done | bytes 1048608 | tf_op jit(solution)/shard_map/ppermute | solution.py:43
  51.3 1.1 constant_dynamic-update-slice_fusion.ext_ref
  52.3 0.0 collective-permute-done.2
  52.4 0.0 copy-done.1
  52.4 1.5 broadcast_select_fusion.4
  53.8 1.6 pad_maximum_fusion.ops_ref
  55.4 11.0 %shard_map.47 = bf16[1280,1024]{1,0:T(8,128)(2,1)} custom-call(s32[70]{0:T(128)} %reshape.14.offsets_ref, s32[70]{0:T(128)} %reshape.15.mask_ref, bf16[10,7,128,128]{3,2,1,0:T(8,128)(2,1)} %pad_maximum_fusion.ops_ref, bf16[1792,2048]{1,0:T(8,128)(2,1)} %constant_dynamic-update-slice_fusion.ext_ref), custom_call_target="tpu_custom_call" | custom-call | flops 2348810240 | bytes 11010048 | tf_op jit(solution)/shard_map/pallas_call | solution.py:253
  66.4 0.0 slice-start
  66.4 11.1 %shard_map.46 = bf16[1280,1024]{1,0:T(8,128)(2,1)} custom-call(s32[70]{0:T(128)} %reshape.14.offsets_ref, s32[70]{0:T(128)} %reshape.15.mask_ref, bf16[10,7,128,128]{3,2,1,0:T(8,128)(2,1)} %pad_maximum_fusion.ops_ref, bf16[1792,2048]{1,0:T(8,128)(2,1)} %constant_dynamic-update-slice_fusion.ext_ref), custom_call_target="tpu_custom_call" | custom-call | flops 2348810240 | bytes 11010048 | tf_op jit(solution)/shard_map/pallas_call | solution.py:253
  77.5 0.0 slice-start.1
  77.5 0.0 copy-start
  77.5 0.0 collective-permute-done
  77.5 10.8 %convolution_multiply_fusion.1 = f32[2048,1024]{1,0:T(8,128)} fusion(bf16[1280,1024]{1,0:T(8,128)(2,1)} %shard_map.46, bf16[1280,2048]{1,0:T(8,128)(2,1)} %param.4, bf16[1280,2048]{1,0:T(8,128)(2,1)} %collective-permute-done, pred[]{:T(512)S(6)} %eq.10), kind=kOutput, calls=%fused_computation.2 | convolution fusion | flops 5373427712 | bytes 21495808 | tf_op jit(solution)/shard_map/dot_general | solution.py:304
  88.4 0.0 slice-done
  88.4 0.0 slice-done.1
  88.4 0.0 copy-done
  88.4 8.2 %convolution_multiply_fusion = f32[2048,1024]{1,0:T(8,128)} fusion(bf16[1280,1024]{1,0:T(8,128)(2,1)S(1)} %copy-done, bf16[1280,2048]{1,0:T(8,128)(2,1)S(1)} %bitcast.7, bf16[1280,2048]{1,0:T(8,128)(2,1)} %collective-permute-done, pred[]{:T(512)S(6)} %eq.10), kind=kOutput, calls=%fused_computation.1 | convolution fusion | flops 5373427712 | bytes 21495808 | tf_op jit(solution)/shard_map/dot_general | solution.py:304
  96.6 118.0 %shard_map.48 = (f32[256,1024]{1,0:T(8,128)}, f32[256,1024]{1,0:T(8,128)}) custom-call(f32[8,256,1024]{2,1,0:T(8,128)} %bitcast.8, f32[8,4,64,1024]{3,2,1,0:T(8,128)} %bitcast.9), custom_call_target="tpu_custom_call" | custom-call | tf_op jit(solution)/shard_map/pallas_call | solution.py:194
  214.6 33.9 %shard_map.49 = (f32[32,1024]{1,0:T(8,128)}, f32[32,1024]{1,0:T(8,128)}) custom-call(f32[4,64,1024]{2,1,0:T(8,128)} %bitcast.10, f32[8,32,1024]{2,1,0:T(8,128)} %bitcast.11), custom_call_target="tpu_custom_call" | custom-call | tf_op jit(solution)/shard_map/pallas_call | solution.py:194
  248.5 1.7 pad_maximum_fusion.1
  (2 shorter events, 0.0 us)
Async XLA Ops:
  0.0 13.5 %copy-start.3 = (s32[10,7]{0,1:T(8,128)S(1)}, s32[10,7]{0,1:T(8,128)}, u32[]{:S(2)}) copy-start(s32[10,7]{0,1:T(8,128)} %param.6) | copy-start | bytes 844
  0.0 14.2 %copy-start.2 = (s32[10,7]{0,1:T(8,128)S(1)}, s32[10,7]{0,1:T(8,128)}, u32[]{:S(2)}) copy-start(s32[10,7]{0,1:T(8,128)} %param.7) | copy-start | bytes 844
  0.0 77.5 %collective-permute-start = (bf16[1280,2048]{1,0:T(8,128)(2,1)}, bf16[1280,2048]{1,0:T(8,128)(2,1)}, u32[]{:S(2)}, u32[]{:S(2)}) collective-permute-start(bf16[1280,2048]{1,0:T(8,128)(2,1)} %param.4), channel_id=1, source_target_pairs={{0,1},{1,0},{2,3},{3,2},{4,5},{5,4},{6,7},{7,6},{8,9},{9,8},{10,11... | collective-permute-start | bytes 15728648 | tf_op jit(solution)/shard_map/ppermute | solution.py:286
  2.7 33.8 %collective-permute-start.3 = (bf16[256,2048]{1,0:T(8,128)(2,1)}, bf16[256,2048]{1,0:T(8,128)(2,1)S(1)}, u32[]{:S(2)}, u32[]{:S(2)}) collective-permute-start(bf16[256,2048]{1,0:T(8,128)(2,1)} %get-tuple-element.14), channel_id=1, source_target_pairs={{0,2},{130,4},{4,6},{134,8},{8,10},{138,12},{12,14},{142,16},{16,1... | collective-permute-start | bytes 3145736 | tf_op jit(solution)/shard_map/ppermute | solution.py:42
  9.1 27.5 %collective-permute-start.1 = (bf16[5,7,64,128]{3,2,1,0:T(8,128)(2,1)}, bf16[5,7,64,128]{3,2,1,0:T(8,128)(2,1)}, u32[]{:S(2)}, u32[]{:S(2)}) collective-permute-start(bf16[5,7,64,128]{3,2,1,0:T(8,128)(2,1)} %constant_dynamic-slice_fusion), channel_id=1, source_target_pairs={{0,128},{128,0},{1,129},{129,1},{2,130},{130,2},{3,131},{131,3},{4... | collective-permute-start | bytes 1720328 | tf_op jit(solution)/shard_map/ppermute | solution.py:275
  10.0 41.2 %collective-permute-start.4 = (bf16[256,2048]{1,0:T(8,128)(2,1)S(1)}, bf16[256,2048]{1,0:T(8,128)(2,1)S(1)}, u32[]{:S(2)}, u32[]{:S(2)}) collective-permute-start(bf16[256,2048]{1,0:T(8,128)(2,1)S(1)} %get-tuple-element.13), channel_id=1, source_target_pairs={{2,0},{132,2},{6,4},{136,6},{10,8},{140,10},{14,12},{144,14},{18,1... | collective-permute-start | bytes 3145736 | tf_op jit(solution)/shard_map/ppermute | solution.py:43
  36.6 15.8 %collective-permute-start.2 = (bf16[5,7,64,128]{3,2,1,0:T(8,128)(2,1)}, bf16[5,7,64,128]{3,2,1,0:T(8,128)(2,1)S(1)}, u32[]{:S(2)}, u32[]{:S(2)}) collective-permute-start(bf16[5,7,64,128]{3,2,1,0:T(8,128)(2,1)} %collective-permute-done.1), channel_id=1, source_target_pairs={{0,1},{1,0},{2,3},{3,2},{4,5},{5,4},{6,7},{7,6},{8,9},{9,8},{10,11... | collective-permute-start | bytes 1720328 | tf_op jit(solution)/shard_map/ppermute | solution.py:276
  37.6 14.7 %copy-start.1 = (bf16[10,7,64,128]{3,2,1,0:T(8,128)(2,1)S(1)}, bf16[10,7,64,128]{3,2,1,0:T(8,128)(2,1)}, u32[]{:S(2)}) copy-start(bf16[10,7,64,128]{3,2,1,0:T(8,128)(2,1)} %param.5) | copy-start | bytes 3440644
  66.4 21.9 %slice-start = ((s8[5242880]{0:T(1024)(128)(4,1)}), s8[1048576]{0:T(1024)(128)(4,1)S(1)}, s32[]{:S(2)}) async-start(s8[5242880]{0:T(1024)(128)(4,1)} %bitcast.6), calls=%async_computation | async-start | bytes 2097152
  77.5 10.9 %slice-start.1 = ((s8[5242880]{0:T(1024)(128)(4,1)}), s8[4194304]{0:T(1024)(128)(4,1)S(1)}, s32[]{:S(2)}) async-start(s8[5242880]{0:T(1024)(128)(4,1)} %bitcast.6), calls=%async_computation.1 | async-start | bytes 8388608
  77.5 10.9 %copy-start = (bf16[1280,1024]{1,0:T(8,128)(2,1)S(1)}, bf16[1280,1024]{1,0:T(8,128)(2,1)}, u32[]{:S(2)}) copy-start(bf16[1280,1024]{1,0:T(8,128)(2,1)} %shard_map.47) | copy-start | bytes 7864324

commit v8 on v7

--- a/solution.py
+++ b/solution.py
@@ -86,6 +86,36 @@
         signals += 1
     pl.semaphore_wait(barrier, signals)
 
+    pending = []
+
+    def finish(index):
+        ring = rings[index]
+        for copy in ring["copies"]:
+            copy.wait()
+        n, p, x = ring["n"], ring["p"], ring["x"]
+        half = x.shape[-1] // 2
+        last = (n - 2) % 2
+        forward = ring["in_f"][last] + read_chunk(x, p, slice(None, half))
+        backward = ring["in_b"][last] + read_chunk(x, p, slice(half, None))
+        if pairs[index] is None:
+            ring["o"][:, :half] = forward
+            ring["o"][:, half:] = backward
+            return
+        pair_axis, _ = pairs[index]
+        total, got, send_sem, recv_sem = pair_scratch[4 * index : 4 * index + 4]
+        outer, _, rows, _ = total.shape
+        total[:, :, :, :half] = forward.reshape(outer, 2, rows, half)
+        total[:, :, :, half:] = backward.reshape(outer, 2, rows, half)
+        mine = lax.axis_index(pair_axis)
+        copy = pltpu.make_async_remote_copy(
+            src_ref=total.at[:, pl.ds(1 - mine, 1)], dst_ref=got,
+            send_sem=send_sem, recv_sem=recv_sem,
+            device_id={pair_axis: 1 - mine}, device_id_type=mesh,
+        )
+        copy.start()
+        pending.append((index, copy, mine))
+
+    done = set()
     ticks = max(n - 1 for _, n in plan)
     for tick in range(ticks):
         for ring in rings:
@@ -129,33 +159,14 @@
                 copy_f.start()
                 copy_b.start()
                 ring["copies"] = (copy_f, copy_b)
-    pending = []
+        for index, ring in enumerate(rings):
+            last_tick = ((ring["n"] - 2) * ticks) // (ring["n"] - 1)
+            if pairs[index] is not None and last_tick + 1 == tick:
+                finish(index)
+                done.add(index)
     for index in sorted(range(count), key=lambda i: rings[i]["n"]):
-        ring = rings[index]
-        for copy in ring["copies"]:
-            copy.wait()
-        n, p, x = ring["n"], ring["p"], ring["x"]
-        half = x.shape[-1] // 2
-        last = (n - 2) % 2
-        forward = ring["in_f"][last] + read_chunk(x, p, slice(None, half))
-        backward = ring["in_b"][last] + read_chunk(x, p, slice(half, None))
-        if pairs[index] is None:
-            ring["o"][:, :half] = forward
-            ring["o"][:, half:] = backward
-            continue
-        pair_axis, _ = pairs[index]
-        total, got, send_sem, recv_sem = pair_scratch[4 * index : 4 * index + 4]
-        outer, _, rows, _ = total.shape
-        total[:, :, :, :half] = forward.reshape(outer, 2, rows, half)
-        total[:, :, :, half:] = backward.reshape(outer, 2, rows, half)
-        mine = lax.axis_index(pair_axis)
-        copy = pltpu.make_async_remote_copy(
-            src_ref=total.at[:, pl.ds(1 - mine, 1)], dst_ref=got,
-            send_sem=send_sem, recv_sem=recv_sem,
-            device_id={pair_axis: 1 - mine}, device_id_type=mesh,
-        )
-        copy.start()
-        pending.append((index, copy, mine))
+        if index not in done:
+            finish(index)
     for index, copy, mine in pending:
         total, got = pair_scratch[4 * index : 4 * index + 2]
         outer, _, rows, width = total.shape

time: 251 us -> 249 us (level)
  no operation moved by 1% of the time
where the time goes in v8:
time: 249 us; the launch traced here: 248 us
  Pallas kernels  172 us (69%)
  waiting for transfers between devices  29.5 us (12%)
  matrix products  19.1 us (8%)
  local copies, waits for them, and re-layouts  14 us (6%)
  starting transfers between devices  8.79 us (4%)
  other arithmetic  4.77 us (2%)
    pallas_call x2, Pallas kernels, multi_ring_reduce(): pl.pallas_call(functools.partial(multi_ring_kernel, tuple(plan), tuple(pa...  150 us
    pallas_call x2, Pallas kernels, apply_operator(): pl.pallas_call(applied_kernel, grid_spec=grid_spec, out_shape=jax.ShapeDt...  22.1 us
    ppermute x1, waiting for transfers between devices, per_device(): from_sec = lax.ppermute(mine, 'sec', [(0, 1), (1, 0)])  21.6 us
    dot_general x2, matrix products, per_device(): lax.dot_general(left_projector, applied, (((0,), (0,)), ((), ())), prefer...  19.1 us
    ppermute x1, waiting for transfers between devices, halo(): after = lax.ppermute(shard[:width], axes, after_pairs)  7.88 us
    unnamed x15, local copies, waits for them, and re-layouts  6.95 us
  transfers between devices with their start and end apart: 5, of which 2 were waited for; matrix products, arithmetic and copies ran while one was open for 7% of the time, Pallas kernels for 9%

profile of v8, /device:TPU:8, one launch (start us, length us, event | category | flops | bytes accessed | tf_op | source)
XLA Modules:
  0.0 248.0 jit_solution(2120770119744823740)
XLA Ops:
  0.0 0.0 copy-start.3
  0.0 0.0 copy-start.2
  0.0 0.0 collective-permute-start
  0.0 2.7 %fusion = (bf16[256,2048]{1,0:T(8,128)(2,1)S(1)}, bf16[256,2048]{1,0:T(8,128)(2,1)}) fusion(bf16[1280,2048]{1,0:T(8,128)(2,1)} %param.4), kind=kLoop, calls=%fused_computation.13 | loop fusion | bytes 4194304 | tf_op jit(solution)/shard_map/slice | solution.py:43
  2.7 4.4 %collective-permute-start.3 = (bf16[256,2048]{1,0:T(8,128)(2,1)}, bf16[256,2048]{1,0:T(8,128)(2,1)S(1)}, u32[]{:S(2)}, u32[]{:S(2)}) collective-permute-start(bf16[256,2048]{1,0:T(8,128)(2,1)} %get-tuple-element.14), channel_id=1, source_target_pairs={{0,2},{130,4},{4,6},{134,8},{8,10},{138,12},{12,14},{142,16},{16,1... | collective-permute-start | bytes 3145736 | tf_op jit(solution)/shard_map/ppermute | solution.py:42
  7.2 1.9 constant_dynamic-slice_fusion
  9.1 0.9 collective-permute-start.1
  10.0 3.4 %collective-permute-start.4 = (bf16[256,2048]{1,0:T(8,128)(2,1)S(1)}, bf16[256,2048]{1,0:T(8,128)(2,1)S(1)}, u32[]{:S(2)}, u32[]{:S(2)}) collective-permute-start(bf16[256,2048]{1,0:T(8,128)(2,1)S(1)} %get-tuple-element.13), channel_id=1, source_target_pairs={{2,0},{132,2},{6,4},{136,6},{10,8},{140,10},{14,12},{144,14},{18,1... | collective-permute-start | bytes 3145736 | tf_op jit(solution)/shard_map/ppermute | solution.py:43
  13.5 0.0 copy-done.3
  13.5 0.1 copy.7
  13.6 0.6 reshape.14.offsets_ref
  14.2 0.0 copy-done.2
  14.2 0.1 copy.8
  14.3 0.6 reshape.15.mask_ref
  14.9 21.6 %collective-permute-done.1 = bf16[5,7,64,128]{3,2,1,0:T(8,128)(2,1)} collective-permute-done((bf16[5,7,64,128]{3,2,1,0:T(8,128)(2,1)}, bf16[5,7,64,128]{3,2,1,0:T(8,128)(2,1)}, u32[]{:S(2)}, u32[]{:S(2)}) %collective-permute-start.1) | collective-permute-done | bytes 573472 | tf_op jit(solution)/shard_map/ppermute | solution.py:286
  36.6 0.0 collective-permute-start.2
  36.6 0.0 collective-permute-done.3
  36.6 1.0 constant_dynamic-update-slice_fusion.2
  37.6 0.0 copy-start.1
  37.6 5.8 %constant_dynamic-update-slice_fusion.1 = bf16[1792,2048]{1,0:T(8,128)(2,1)} fusion(bf16[1792,2048]{1,0:T(8,128)(2,1)} %constant_dynamic-update-slice_fusion.2, bf16[1280,2048]{1,0:T(8,128)(2,1)} %param.4), kind=kLoop, calls=%fused_computation.9 | loop fusion | bytes 10485760
  43.4 7.9 %collective-permute-done.4 = bf16[256,2048]{1,0:T(8,128)(2,1)S(1)} collective-permute-done((bf16[256,2048]{1,0:T(8,128)(2,1)S(1)}, bf16[256,2048]{1,0:T(8,128)(2,1)S(1)}, u32[]{:S(2)}, u32[]{:S(2)}) %collective-permute-start.4) | collective-permute-done | bytes 1048608 | tf_op jit(solution)/shard_map/ppermute | solution.py:43
  51.3 1.1 constant_dynamic-update-slice_fusion.ext_ref
  52.3 0.0 collective-permute-done.2
  52.4 0.0 copy-done.1
  52.4 1.5 broadcast_select_fusion.4
  53.8 1.6 pad_maximum_fusion.ops_ref
  55.4 11.0 %shard_map.47 = bf16[1280,1024]{1,0:T(8,128)(2,1)} custom-call(s32[70]{0:T(128)} %reshape.14.offsets_ref, s32[70]{0:T(128)} %reshape.15.mask_ref, bf16[10,7,128,128]{3,2,1,0:T(8,128)(2,1)} %pad_maximum_fusion.ops_ref, bf16[1792,2048]{1,0:T(8,128)(2,1)} %constant_dynamic-update-slice_fusion.ext_ref), custom_call_target="tpu_custom_call" | custom-call | flops 2348810240 | bytes 11010048 | tf_op jit(solution)/shard_map/pallas_call | solution.py:264
  66.4 0.0 slice-start
  66.4 11.1 %shard_map.46 = bf16[1280,1024]{1,0:T(8,128)(2,1)} custom-call(s32[70]{0:T(128)} %reshape.14.offsets_ref, s32[70]{0:T(128)} %reshape.15.mask_ref, bf16[10,7,128,128]{3,2,1,0:T(8,128)(2,1)} %pad_maximum_fusion.ops_ref, bf16[1792,2048]{1,0:T(8,128)(2,1)} %constant_dynamic-update-slice_fusion.ext_ref), custom_call_target="tpu_custom_call" | custom-call | flops 2348810240 | bytes 11010048 | tf_op jit(solution)/shard_map/pallas_call | solution.py:264
  77.5 0.0 slice-start.1
  77.5 0.0 copy-start
  77.5 0.0 collective-permute-done
  77.5 10.8 %convolution_multiply_fusion.1 = f32[2048,1024]{1,0:T(8,128)} fusion(bf16[1280,1024]{1,0:T(8,128)(2,1)} %shard_map.46, bf16[1280,2048]{1,0:T(8,128)(2,1)} %param.4, bf16[1280,2048]{1,0:T(8,128)(2,1)} %collective-permute-done, pred[]{:T(512)S(6)} %eq.10), kind=kOutput, calls=%fused_computation.2 | convolution fusion | flops 5373427712 | bytes 21495808 | tf_op jit(solution)/shard_map/dot_general | solution.py:315
  88.4 0.0 slice-done
  88.4 0.0 slice-done.1
  88.4 0.0 copy-done
  88.4 8.2 %convolution_multiply_fusion = f32[2048,1024]{1,0:T(8,128)} fusion(bf16[1280,1024]{1,0:T(8,128)(2,1)S(1)} %copy-done, bf16[1280,2048]{1,0:T(8,128)(2,1)S(1)} %bitcast.7, bf16[1280,2048]{1,0:T(8,128)(2,1)} %collective-permute-done, pred[]{:T(512)S(6)} %eq.10), kind=kOutput, calls=%fused_computation.1 | convolution fusion | flops 5373427712 | bytes 21495808 | tf_op jit(solution)/shard_map/dot_general | solution.py:315
  96.6 117.8 %shard_map.48 = (f32[256,1024]{1,0:T(8,128)}, f32[256,1024]{1,0:T(8,128)}) custom-call(f32[8,256,1024]{2,1,0:T(8,128)} %bitcast.8, f32[8,4,64,1024]{3,2,1,0:T(8,128)} %bitcast.9), custom_call_target="tpu_custom_call" | custom-call | tf_op jit(solution)/shard_map/pallas_call | solution.py:205
  214.5 31.9 %shard_map.49 = (f32[32,1024]{1,0:T(8,128)}, f32[32,1024]{1,0:T(8,128)}) custom-call(f32[4,64,1024]{2,1,0:T(8,128)} %bitcast.10, f32[8,32,1024]{2,1,0:T(8,128)} %bitcast.11), custom_call_target="tpu_custom_call" | custom-call | tf_op jit(solution)/shard_map/pallas_call | solution.py:205
  246.3 1.7 pad_maximum_fusion.1
  (2 shorter events, 0.0 us)
Async XLA Ops:
  0.0 13.5 %copy-start.3 = (s32[10,7]{0,1:T(8,128)S(1)}, s32[10,7]{0,1:T(8,128)}, u32[]{:S(2)}) copy-start(s32[10,7]{0,1:T(8,128)} %param.6) | copy-start | bytes 844
  0.0 14.2 %copy-start.2 = (s32[10,7]{0,1:T(8,128)S(1)}, s32[10,7]{0,1:T(8,128)}, u32[]{:S(2)}) copy-start(s32[10,7]{0,1:T(8,128)} %param.7) | copy-start | bytes 844
  0.0 77.5 %collective-permute-start = (bf16[1280,2048]{1,0:T(8,128)(2,1)}, bf16[1280,2048]{1,0:T(8,128)(2,1)}, u32[]{:S(2)}, u32[]{:S(2)}) collective-permute-start(bf16[1280,2048]{1,0:T(8,128)(2,1)} %param.4), channel_id=1, source_target_pairs={{0,1},{1,0},{2,3},{3,2},{4,5},{5,4},{6,7},{7,6},{8,9},{9,8},{10,11... | collective-permute-start | bytes 15728648 | tf_op jit(solution)/shard_map/ppermute | solution.py:297
  2.7 33.8 %collective-permute-start.3 = (bf16[256,2048]{1,0:T(8,128)(2,1)}, bf16[256,2048]{1,0:T(8,128)(2,1)S(1)}, u32[]{:S(2)}, u32[]{:S(2)}) collective-permute-start(bf16[256,2048]{1,0:T(8,128)(2,1)} %get-tuple-element.14), channel_id=1, source_target_pairs={{0,2},{130,4},{4,6},{134,8},{8,10},{138,12},{12,14},{142,16},{16,1... | collective-permute-start | bytes 3145736 | tf_op jit(solution)/shard_map/ppermute | solution.py:42
  9.1 27.5 %collective-permute-start.1 = (bf16[5,7,64,128]{3,2,1,0:T(8,128)(2,1)}, bf16[5,7,64,128]{3,2,1,0:T(8,128)(2,1)}, u32[]{:S(2)}, u32[]{:S(2)}) collective-permute-start(bf16[5,7,64,128]{3,2,1,0:T(8,128)(2,1)} %constant_dynamic-slice_fusion), channel_id=1, source_target_pairs={{0,128},{128,0},{1,129},{129,1},{2,130},{130,2},{3,131},{131,3},{4... | collective-permute-start | bytes 1720328 | tf_op jit(solution)/shard_map/ppermute | solution.py:286
  10.0 41.2 %collective-permute-start.4 = (bf16[256,2048]{1,0:T(8,128)(2,1)S(1)}, bf16[256,2048]{1,0:T(8,128)(2,1)S(1)}, u32[]{:S(2)}, u32[]{:S(2)}) collective-permute-start(bf16[256,2048]{1,0:T(8,128)(2,1)S(1)} %get-tuple-element.13), channel_id=1, source_target_pairs={{2,0},{132,2},{6,4},{136,6},{10,8},{140,10},{14,12},{144,14},{18,1... | collective-permute-start | bytes 3145736 | tf_op jit(solution)/shard_map/ppermute | solution.py:43
  36.6 15.8 %collective-permute-start.2 = (bf16[5,7,64,128]{3,2,1,0:T(8,128)(2,1)}, bf16[5,7,64,128]{3,2,1,0:T(8,128)(2,1)S(1)}, u32[]{:S(2)}, u32[]{:S(2)}) collective-permute-start(bf16[5,7,64,128]{3,2,1,0:T(8,128)(2,1)} %collective-permute-done.1), channel_id=1, source_target_pairs={{0,1},{1,0},{2,3},{3,2},{4,5},{5,4},{6,7},{7,6},{8,9},{9,8},{10,11... | collective-permute-start | bytes 1720328 | tf_op jit(solution)/shard_map/ppermute | solution.py:287
  37.6 14.7 %copy-start.1 = (bf16[10,7,64,128]{3,2,1,0:T(8,128)(2,1)S(1)}, bf16[10,7,64,128]{3,2,1,0:T(8,128)(2,1)}, u32[]{:S(2)}) copy-start(bf16[10,7,64,128]{3,2,1,0:T(8,128)(2,1)} %param.5) | copy-start | bytes 3440644
  66.4 21.9 %slice-start = ((s8[5242880]{0:T(1024)(128)(4,1)}), s8[1048576]{0:T(1024)(128)(4,1)S(1)}, s32[]{:S(2)}) async-start(s8[5242880]{0:T(1024)(128)(4,1)} %bitcast.6), calls=%async_computation | async-start | bytes 2097152
  77.5 10.9 %slice-start.1 = ((s8[5242880]{0:T(1024)(128)(4,1)}), s8[4194304]{0:T(1024)(128)(4,1)S(1)}, s32[]{:S(2)}) async-start(s8[5242880]{0:T(1024)(128)(4,1)} %bitcast.6), calls=%async_computation.1 | async-start | bytes 8388608
  77.5 10.9 %copy-start = (bf16[1280,1024]{1,0:T(8,128)(2,1)S(1)}, bf16[1280,1024]{1,0:T(8,128)(2,1)}, u32[]{:S(2)}) copy-start(bf16[1280,1024]{1,0:T(8,128)(2,1)} %shard_map.47) | copy-start | bytes 7864324

commit v9 on v8

--- a/solution.py
+++ b/solution.py
@@ -117,10 +117,17 @@
 
     done = set()
     ticks = max(n - 1 for _, n in plan)
+
+    def step_tick(index, step):
+        n = rings[index]["n"]
+        if pairs[index] is not None and 2 < n - 1 + 2 < ticks:
+            return (step * (ticks - 4)) // (n - 2)
+        return (step * ticks) // (n - 1)
+
     for tick in range(ticks):
-        for ring in rings:
+        for ring_index, ring in enumerate(rings):
             n = ring["n"]
-            due = [step for step in range(n - 1) if (step * ticks) // (n - 1) == tick]
+            due = [step for step in range(n - 1) if step_tick(ring_index, step) == tick]
             for step in due:
                 if ring["copies"] is not None:
                     for copy in ring["copies"]:
@@ -160,7 +167,7 @@
                 copy_b.start()
                 ring["copies"] = (copy_f, copy_b)
         for index, ring in enumerate(rings):
-            last_tick = ((ring["n"] - 2) * ticks) // (ring["n"] - 1)
+            last_tick = step_tick(index, ring["n"] - 2)
             if pairs[index] is not None and last_tick + 1 == tick:
                 finish(index)
                 done.add(index)

time: 249 us -> 249 us (level)
  no operation moved by 1% of the time
where the time goes in v9:
time: 249 us; the launch traced here: 248 us
  Pallas kernels  172 us (69%)
  waiting for transfers between devices  29.5 us (12%)
  matrix products  19.1 us (8%)
  local copies, waits for them, and re-layouts  14 us (6%)
  starting transfers between devices  8.79 us (4%)
  other arithmetic  4.77 us (2%)
    pallas_call x2, Pallas kernels, multi_ring_reduce(): pl.pallas_call(functools.partial(multi_ring_kernel, tuple(plan), tuple(pa...  150 us
    pallas_call x2, Pallas kernels, apply_operator(): pl.pallas_call(applied_kernel, grid_spec=grid_spec, out_shape=jax.ShapeDt...  22.1 us
    ppermute x1, waiting for transfers between devices, per_device(): from_sec = lax.ppermute(mine, 'sec', [(0, 1), (1, 0)])  21.6 us
    dot_general x2, matrix products, per_device(): lax.dot_general(left_projector, applied, (((0,), (0,)), ((), ())), prefer...  19.1 us
    ppermute x1, waiting for transfers between devices, halo(): after = lax.ppermute(shard[:width], axes, after_pairs)  7.88 us
    unnamed x15, local copies, waits for them, and re-layouts  6.95 us
  transfers between devices with their start and end apart: 5, of which 2 were waited for; matrix products, arithmetic and copies ran while one was open for 7% of the time, Pallas kernels for 9%

profile of v9, /device:TPU:8, one launch (start us, length us, event | category | flops | bytes accessed | tf_op | source)
XLA Modules:
  0.0 248.5 jit_solution(10419430695619432854)
XLA Ops:
  0.0 0.0 copy-start.3
  0.0 0.0 copy-start.2
  0.0 0.0 collective-permute-start
  0.0 2.7 %fusion = (bf16[256,2048]{1,0:T(8,128)(2,1)S(1)}, bf16[256,2048]{1,0:T(8,128)(2,1)}) fusion(bf16[1280,2048]{1,0:T(8,128)(2,1)} %param.4), kind=kLoop, calls=%fused_computation.13 | loop fusion | bytes 4194304 | tf_op jit(solution)/shard_map/slice | solution.py:43
  2.7 4.4 %collective-permute-start.3 = (bf16[256,2048]{1,0:T(8,128)(2,1)}, bf16[256,2048]{1,0:T(8,128)(2,1)S(1)}, u32[]{:S(2)}, u32[]{:S(2)}) collective-permute-start(bf16[256,2048]{1,0:T(8,128)(2,1)} %get-tuple-element.14), channel_id=1, source_target_pairs={{0,2},{130,4},{4,6},{134,8},{8,10},{138,12},{12,14},{142,16},{16,1... | collective-permute-start | bytes 3145736 | tf_op jit(solution)/shard_map/ppermute | solution.py:42
  7.2 1.9 constant_dynamic-slice_fusion
  9.1 0.9 collective-permute-start.1
  10.0 3.4 %collective-permute-start.4 = (bf16[256,2048]{1,0:T(8,128)(2,1)S(1)}, bf16[256,2048]{1,0:T(8,128)(2,1)S(1)}, u32[]{:S(2)}, u32[]{:S(2)}) collective-permute-start(bf16[256,2048]{1,0:T(8,128)(2,1)S(1)} %get-tuple-element.13), channel_id=1, source_target_pairs={{2,0},{132,2},{6,4},{136,6},{10,8},{140,10},{14,12},{144,14},{18,1... | collective-permute-start | bytes 3145736 | tf_op jit(solution)/shard_map/ppermute | solution.py:43
  13.5 0.0 copy-done.3
  13.5 0.1 copy.7
  13.6 0.6 reshape.14.offsets_ref
  14.2 0.0 copy-done.2
  14.2 0.1 copy.8
  14.3 0.6 reshape.15.mask_ref
  14.9 21.6 %collective-permute-done.1 = bf16[5,7,64,128]{3,2,1,0:T(8,128)(2,1)} collective-permute-done((bf16[5,7,64,128]{3,2,1,0:T(8,128)(2,1)}, bf16[5,7,64,128]{3,2,1,0:T(8,128)(2,1)}, u32[]{:S(2)}, u32[]{:S(2)}) %collective-permute-start.1) | collective-permute-done | bytes 573472 | tf_op jit(solution)/shard_map/ppermute | solution.py:293
  36.6 0.0 collective-permute-start.2
  36.6 0.0 collective-permute-done.3
  36.6 1.0 constant_dynamic-update-slice_fusion.2
  37.6 0.0 copy-start.1
  37.6 5.8 %constant_dynamic-update-slice_fusion.1 = bf16[1792,2048]{1,0:T(8,128)(2,1)} fusion(bf16[1792,2048]{1,0:T(8,128)(2,1)} %constant_dynamic-update-slice_fusion.2, bf16[1280,2048]{1,0:T(8,128)(2,1)} %param.4), kind=kLoop, calls=%fused_computation.9 | loop fusion | bytes 10485760
  43.4 7.9 %collective-permute-done.4 = bf16[256,2048]{1,0:T(8,128)(2,1)S(1)} collective-permute-done((bf16[256,2048]{1,0:T(8,128)(2,1)S(1)}, bf16[256,2048]{1,0:T(8,128)(2,1)S(1)}, u32[]{:S(2)}, u32[]{:S(2)}) %collective-permute-start.4) | collective-permute-done | bytes 1048608 | tf_op jit(solution)/shard_map/ppermute | solution.py:43
  51.3 1.1 constant_dynamic-update-slice_fusion.ext_ref
  52.3 0.0 collective-permute-done.2
  52.4 0.0 copy-done.1
  52.4 1.5 broadcast_select_fusion.4
  53.8 1.6 pad_maximum_fusion.ops_ref
  55.4 11.0 %shard_map.47 = bf16[1280,1024]{1,0:T(8,128)(2,1)} custom-call(s32[70]{0:T(128)} %reshape.14.offsets_ref, s32[70]{0:T(128)} %reshape.15.mask_ref, bf16[10,7,128,128]{3,2,1,0:T(8,128)(2,1)} %pad_maximum_fusion.ops_ref, bf16[1792,2048]{1,0:T(8,128)(2,1)} %constant_dynamic-update-slice_fusion.ext_ref), custom_call_target="tpu_custom_call" | custom-call | flops 2348810240 | bytes 11010048 | tf_op jit(solution)/shard_map/pallas_call | solution.py:271
  66.4 0.0 slice-start
  66.4 11.1 %shard_map.46 = bf16[1280,1024]{1,0:T(8,128)(2,1)} custom-call(s32[70]{0:T(128)} %reshape.14.offsets_ref, s32[70]{0:T(128)} %reshape.15.mask_ref, bf16[10,7,128,128]{3,2,1,0:T(8,128)(2,1)} %pad_maximum_fusion.ops_ref, bf16[1792,2048]{1,0:T(8,128)(2,1)} %constant_dynamic-update-slice_fusion.ext_ref), custom_call_target="tpu_custom_call" | custom-call | flops 2348810240 | bytes 11010048 | tf_op jit(solution)/shard_map/pallas_call | solution.py:271
  77.5 0.0 slice-start.1
  77.5 0.0 copy-start
  77.5 0.0 collective-permute-done
  77.5 10.8 %convolution_multiply_fusion.1 = f32[2048,1024]{1,0:T(8,128)} fusion(bf16[1280,1024]{1,0:T(8,128)(2,1)} %shard_map.46, bf16[1280,2048]{1,0:T(8,128)(2,1)} %param.4, bf16[1280,2048]{1,0:T(8,128)(2,1)} %collective-permute-done, pred[]{:T(512)S(6)} %eq.10), kind=kOutput, calls=%fused_computation.2 | convolution fusion | flops 5373427712 | bytes 21495808 | tf_op jit(solution)/shard_map/dot_general | solution.py:322
  88.4 0.0 slice-done
  88.4 0.0 slice-done.1
  88.4 0.0 copy-done
  88.4 8.2 %convolution_multiply_fusion = f32[2048,1024]{1,0:T(8,128)} fusion(bf16[1280,1024]{1,0:T(8,128)(2,1)S(1)} %copy-done, bf16[1280,2048]{1,0:T(8,128)(2,1)S(1)} %bitcast.7, bf16[1280,2048]{1,0:T(8,128)(2,1)} %collective-permute-done, pred[]{:T(512)S(6)} %eq.10), kind=kOutput, calls=%fused_computation.1 | convolution fusion | flops 5373427712 | bytes 21495808 | tf_op jit(solution)/shard_map/dot_general | solution.py:322
  96.6 117.2 %shard_map.48 = (f32[256,1024]{1,0:T(8,128)}, f32[256,1024]{1,0:T(8,128)}) custom-call(f32[8,256,1024]{2,1,0:T(8,128)} %bitcast.8, f32[8,4,64,1024]{3,2,1,0:T(8,128)} %bitcast.9), custom_call_target="tpu_custom_call" | custom-call | tf_op jit(solution)/shard_map/pallas_call | solution.py:212
  213.9 32.9 %shard_map.49 = (f32[32,1024]{1,0:T(8,128)}, f32[32,1024]{1,0:T(8,128)}) custom-call(f32[4,64,1024]{2,1,0:T(8,128)} %bitcast.10, f32[8,32,1024]{2,1,0:T(8,128)} %bitcast.11), custom_call_target="tpu_custom_call" | custom-call | tf_op jit(solution)/shard_map/pallas_call | solution.py:212
  246.8 1.7 pad_maximum_fusion.1
  (2 shorter events, 0.0 us)
Async XLA Ops:
  0.0 13.5 %copy-start.3 = (s32[10,7]{0,1:T(8,128)S(1)}, s32[10,7]{0,1:T(8,128)}, u32[]{:S(2)}) copy-start(s32[10,7]{0,1:T(8,128)} %param.6) | copy-start | bytes 844
  0.0 14.2 %copy-start.2 = (s32[10,7]{0,1:T(8,128)S(1)}, s32[10,7]{0,1:T(8,128)}, u32[]{:S(2)}) copy-start(s32[10,7]{0,1:T(8,128)} %param.7) | copy-start | bytes 844
  0.0 77.5 %collective-permute-start = (bf16[1280,2048]{1,0:T(8,128)(2,1)}, bf16[1280,2048]{1,0:T(8,128)(2,1)}, u32[]{:S(2)}, u32[]{:S(2)}) collective-permute-start(bf16[1280,2048]{1,0:T(8,128)(2,1)} %param.4), channel_id=1, source_target_pairs={{0,1},{1,0},{2,3},{3,2},{4,5},{5,4},{6,7},{7,6},{8,9},{9,8},{10,11... | collective-permute-start | bytes 15728648 | tf_op jit(solution)/shard_map/ppermute | solution.py:304
  2.7 33.8 %collective-permute-start.3 = (bf16[256,2048]{1,0:T(8,128)(2,1)}, bf16[256,2048]{1,0:T(8,128)(2,1)S(1)}, u32[]{:S(2)}, u32[]{:S(2)}) collective-permute-start(bf16[256,2048]{1,0:T(8,128)(2,1)} %get-tuple-element.14), channel_id=1, source_target_pairs={{0,2},{130,4},{4,6},{134,8},{8,10},{138,12},{12,14},{142,16},{16,1... | collective-permute-start | bytes 3145736 | tf_op jit(solution)/shard_map/ppermute | solution.py:42
  9.1 27.5 %collective-permute-start.1 = (bf16[5,7,64,128]{3,2,1,0:T(8,128)(2,1)}, bf16[5,7,64,128]{3,2,1,0:T(8,128)(2,1)}, u32[]{:S(2)}, u32[]{:S(2)}) collective-permute-start(bf16[5,7,64,128]{3,2,1,0:T(8,128)(2,1)} %constant_dynamic-slice_fusion), channel_id=1, source_target_pairs={{0,128},{128,0},{1,129},{129,1},{2,130},{130,2},{3,131},{131,3},{4... | collective-permute-start | bytes 1720328 | tf_op jit(solution)/shard_map/ppermute | solution.py:293
  10.0 41.2 %collective-permute-start.4 = (bf16[256,2048]{1,0:T(8,128)(2,1)S(1)}, bf16[256,2048]{1,0:T(8,128)(2,1)S(1)}, u32[]{:S(2)}, u32[]{:S(2)}) collective-permute-start(bf16[256,2048]{1,0:T(8,128)(2,1)S(1)} %get-tuple-element.13), channel_id=1, source_target_pairs={{2,0},{132,2},{6,4},{136,6},{10,8},{140,10},{14,12},{144,14},{18,1... | collective-permute-start | bytes 3145736 | tf_op jit(solution)/shard_map/ppermute | solution.py:43
  36.6 15.8 %collective-permute-start.2 = (bf16[5,7,64,128]{3,2,1,0:T(8,128)(2,1)}, bf16[5,7,64,128]{3,2,1,0:T(8,128)(2,1)S(1)}, u32[]{:S(2)}, u32[]{:S(2)}) collective-permute-start(bf16[5,7,64,128]{3,2,1,0:T(8,128)(2,1)} %collective-permute-done.1), channel_id=1, source_target_pairs={{0,1},{1,0},{2,3},{3,2},{4,5},{5,4},{6,7},{7,6},{8,9},{9,8},{10,11... | collective-permute-start | bytes 1720328 | tf_op jit(solution)/shard_map/ppermute | solution.py:294
  37.6 14.7 %copy-start.1 = (bf16[10,7,64,128]{3,2,1,0:T(8,128)(2,1)S(1)}, bf16[10,7,64,128]{3,2,1,0:T(8,128)(2,1)}, u32[]{:S(2)}) copy-start(bf16[10,7,64,128]{3,2,1,0:T(8,128)(2,1)} %param.5) | copy-start | bytes 3440644
  66.4 21.9 %slice-start = ((s8[5242880]{0:T(1024)(128)(4,1)}), s8[1048576]{0:T(1024)(128)(4,1)S(1)}, s32[]{:S(2)}) async-start(s8[5242880]{0:T(1024)(128)(4,1)} %bitcast.6), calls=%async_computation | async-start | bytes 2097152
  77.5 10.9 %slice-start.1 = ((s8[5242880]{0:T(1024)(128)(4,1)}), s8[4194304]{0:T(1024)(128)(4,1)S(1)}, s32[]{:S(2)}) async-start(s8[5242880]{0:T(1024)(128)(4,1)} %bitcast.6), calls=%async_computation.1 | async-start | bytes 8388608
  77.5 10.9 %copy-start = (bf16[1280,1024]{1,0:T(8,128)(2,1)S(1)}, bf16[1280,1024]{1,0:T(8,128)(2,1)}, u32[]{:S(2)}) copy-start(bf16[1280,1024]{1,0:T(8,128)(2,1)} %shard_map.47) | copy-start | bytes 7864324

commit v10 on v8

--- a/solution.py
+++ b/solution.py
@@ -41,7 +41,7 @@
                 before_pairs.append((index(other, row - 1), index(sec, row)))
     before = lax.ppermute(shard[length - width :], axes, before_pairs)
     after = lax.ppermute(shard[:width], axes, after_pairs)
-    return jnp.concatenate([before, shard, after], axis=0)
+    return before, shard, after
 
 
 def take_chunk(x, index, dim):
@@ -221,9 +221,17 @@
     return got + take_chunk(x, p, dim)
 
 
-def applied_kernel(offsets_ref, mask_ref, ops_ref, ext_ref, out_ref):
+def applied_kernel(offsets_ref, mask_ref, ops_ref, before_ref, basis_ref, after_ref, out_ref, ext_ref):
     block = pl.program_id(1)
     slot_count, block_rows = ops_ref.shape[1], ops_ref.shape[2]
+
+    @pl.when(block == 0)
+    def _():
+        width, local = before_ref.shape[0], basis_ref.shape[0]
+        ext_ref[pl.ds(0, width), :] = before_ref[...]
+        ext_ref[pl.ds(width, local), :] = basis_ref[...]
+        ext_ref[pl.ds(width + local, width), :] = after_ref[...]
+
     order = [slot for _, slot in sorted(zip(STATIC_OFFSETS, WINDOW_SLOTS))]
     lhs = jnp.concatenate(
         [
@@ -246,9 +254,10 @@
     out_ref[...] = acc.astype(out_ref.dtype)
 
 
-def apply_operator(offsets, mask, full_ops, extended, column_start, column_count):
+def apply_operator(offsets, mask, full_ops, sides, column_start, column_count):
+    before, basis, after = sides
     block_count, slot_count, block_rows, _ = full_ops.shape
-    ext_rows = extended.shape[0]
+    ext_rows = before.shape[0] + basis.shape[0] + after.shape[0]
     tile = min(TILE_COLUMNS, column_count)
     skip = column_start // tile
     grid_spec = pltpu.PrefetchScalarGridSpec(
@@ -256,9 +265,12 @@
         grid=(column_count // tile, block_count),
         in_specs=[
             pl.BlockSpec((1, slot_count, block_rows, block_rows), lambda j, b, *_: (b, 0, 0, 0)),
-            pl.BlockSpec((ext_rows, tile), lambda j, b, *_: (0, j + skip)),
+            pl.BlockSpec((before.shape[0], tile), lambda j, b, *_: (0, j + skip)),
+            pl.BlockSpec((basis.shape[0], tile), lambda j, b, *_: (0, j + skip)),
+            pl.BlockSpec((after.shape[0], tile), lambda j, b, *_: (0, j + skip)),
         ],
         out_specs=pl.BlockSpec((block_rows, tile), lambda j, b, *_: (b, j)),
+        scratch_shapes=[pltpu.VMEM((ext_rows, tile), basis.dtype)],
     )
     flops = 2 * block_count * slot_count * block_rows * block_rows * column_count
     return pl.pallas_call(
@@ -269,7 +281,7 @@
         cost_estimate=pl.CostEstimate(
             flops=flops, bytes_accessed=3 * ext_rows * column_count * 2, transcendentals=0
         ),
-    )(offsets, mask, full_ops, extended)
+    )(offsets, mask, full_ops, before, basis, after)
 
 
 def per_device(basis_matrix, operator_blocks, neighbours, neighbour_mask):
@@ -297,7 +309,7 @@
     other_basis = lax.ppermute(basis_matrix, "col", [(0, 1), (1, 0)])
     left_projector = jnp.where(sec == col, basis_matrix, other_basis)
 
-    extended = halo(basis_matrix, REACH * block_rows)
+    sides = halo(basis_matrix, REACH * block_rows)
     offsets = jnp.clip(neighbours - row * block_count + REACH, 0, block_count + 2 * REACH - 1)
     row_count = 1
     for _, size in ROW_PARTS:
@@ -309,7 +321,7 @@
     for order, units in ORDERS:
         width = units * UNIT
         applied = apply_operator(
-            offsets.reshape(-1), neighbour_mask.reshape(-1), full_ops, extended, start, width
+            offsets.reshape(-1), neighbour_mask.reshape(-1), full_ops, sides, start, width
         )
         start += width
         part = scaling * lax.dot_general(

time: 249 us -> 253 us (1.016)
  local copies, waits for them, and re-layouts: 14 us -> 6.72 us
  Pallas kernels: 172 us -> 178 us
  waiting for transfers between devices: 29.5 us -> 34.6 us
    ppermute x1, waiting for transfers between devices: 7.88 us -> 16.9 us  [halo(): after = lax.ppermute(shard[:width], axes, after_pairs)]
    ppermute x1, waiting for transfers between devices: 21.6 us -> 14.7 us  [per_device(): from_sec = lax.ppermute(mine, 'sec', [(0, 1), (1, 0)])]
    unnamed x15 -> x17, local copies, waits for them, and re-layouts: 6.95 us -> 1.1 us
    pallas_call x2, Pallas kernels: 150 us -> 155 us  [multi_ring_reduce(): pl.pallas_call(functools.partial(multi_ring_kernel, tuple(plan), tuple(pa...]
    ppermute x1, waiting for transfers between devices: 0.01 us -> 2.92 us  [halo(): before = lax.ppermute(shard[length - width:], axes, before_pairs)]
  transfers between devices with their start and end apart: 5 -> 5, of which waited for: 2 -> 3; matrix products, arithmetic and copies ran while one was open for 7% -> 4% of each run, Pallas kernels for 9% -> 9%
where the time goes in v10:
time: 253 us
  Pallas kernels  178 us (70%)
  waiting for transfers between devices  34.6 us (14%)
  matrix products  19.1 us (8%)
  starting transfers between devices  9.12 us (4%)
  local copies, waits for them, and re-layouts  6.72 us (3%)
  other arithmetic  5.12 us (2%)
    pallas_call x2, Pallas kernels, multi_ring_reduce(): pl.pallas_call(functools.partial(multi_ring_kernel, tuple(plan), tuple(pa...  155 us
    pallas_call x2, Pallas kernels, apply_operator(): pl.pallas_call(applied_kernel, grid_spec=grid_spec, out_shape=jax.ShapeDt...  22.5 us
    dot_general x2, matrix products, per_device(): lax.dot_general(left_projector, applied, (((0,), (0,)), ((), ())), prefer...  19.1 us
    ppermute x1, waiting for transfers between devices, halo(): after = lax.ppermute(shard[:width], axes, after_pairs)  16.9 us
    ppermute x1, waiting for transfers between devices, per_device(): from_sec = lax.ppermute(mine, 'sec', [(0, 1), (1, 0)])  14.7 us
  transfers between devices with their start and end apart: 5, of which 3 were waited for; matrix products, arithmetic and copies ran while one was open for 4% of the time, Pallas kernels for 9%

profile of v10, /device:TPU:8, one launch (start us, length us, event | category | flops | bytes accessed | tf_op | source)
XLA Modules:
  0.0 252.5 jit_solution(16068354231217070611)
XLA Ops:
  0.0 0.0 collective-permute-start
  0.0 0.0 copy-start.5
  0.0 0.0 copy-start.4
  0.0 0.0 copy-start.3
  0.0 1.2 constant_dynamic-slice_fusion
  1.2 2.4 collective-permute-start.1
  3.6 14.7 %collective-permute-done.1 = bf16[5,7,64,128]{3,2,1,0:T(8,128)(2,1)} collective-permute-done((bf16[5,7,64,128]{3,2,1,0:T(8,128)(2,1)S(1)}, bf16[5,7,64,128]{3,2,1,0:T(8,128)(2,1)}, u32[]{:S(2)}, u32[]{:S(2)}) %collective-permute-start.1) | collective-permute-done | bytes 573472 | tf_op jit(solution)/shard_map/ppermute | solution.py:298
  18.3 0.0 collective-permute-start.2
  18.3 3.1 %fusion = (bf16[256,2048]{1,0:T(8,128)(2,1)}, bf16[256,2048]{1,0:T(8,128)(2,1)}) fusion(bf16[1280,2048]{1,0:T(8,128)(2,1)} %basis_ref.3), kind=kLoop, calls=%fused_computation.10 | loop fusion | bytes 4194304 | tf_op jit(solution)/shard_map/slice | solution.py:43
  21.4 4.1 %collective-permute-start.4 = (bf16[256,2048]{1,0:T(8,128)(2,1)}, bf16[256,2048]{1,0:T(8,128)(2,1)S(1)}, u32[]{:S(2)}, u32[]{:S(2)}) collective-permute-start(bf16[256,2048]{1,0:T(8,128)(2,1)} %get-tuple-element.13), channel_id=1, source_target_pairs={{2,0},{132,2},{6,4},{136,6},{10,8},{140,10},{14,12},{144,14},{18,1... | collective-permute-start | bytes 3145736 | tf_op jit(solution)/shard_map/ppermute | solution.py:43
  25.5 2.6 %collective-permute-start.3 = (bf16[256,2048]{1,0:T(8,128)(2,1)}, bf16[256,2048]{1,0:T(8,128)(2,1)S(1)}, u32[]{:S(2)}, u32[]{:S(2)}) collective-permute-start(bf16[256,2048]{1,0:T(8,128)(2,1)} %get-tuple-element.14), channel_id=1, source_target_pairs={{0,2},{130,4},{4,6},{134,8},{8,10},{138,12},{12,14},{142,16},{16,1... | collective-permute-start | bytes 3145736 | tf_op jit(solution)/shard_map/ppermute | solution.py:42
  28.2 0.0 copy-done.5
  28.2 0.1 copy.7
  28.3 0.6 reshape.14.offsets_ref
  28.9 0.0 copy-done.4
  28.9 0.1 copy.8
  29.0 0.6 reshape.15.mask_ref
  29.6 0.0 collective-permute-done.2
  29.6 0.0 copy-done.3
  29.6 1.8 broadcast_select_fusion.4
  31.4 1.6 pad_maximum_fusion.ops_ref
  33.0 16.9 %collective-permute-done.4.after_ref = bf16[256,2048]{1,0:T(8,128)(2,1)S(1)} collective-permute-done((bf16[256,2048]{1,0:T(8,128)(2,1)}, bf16[256,2048]{1,0:T(8,128)(2,1)S(1)}, u32[]{:S(2)}, u32[]{:S(2)}) %collective-permute-start.4) | collective-permute-done | bytes 1048608 | tf_op jit(solution)/shard_map/ppermute | solution.py:43
  50.0 0.0 copy-start
  50.0 2.9 %collective-permute-done.3.before_ref = bf16[256,2048]{1,0:T(8,128)(2,1)S(1)} collective-permute-done((bf16[256,2048]{1,0:T(8,128)(2,1)}, bf16[256,2048]{1,0:T(8,128)(2,1)S(1)}, u32[]{:S(2)}, u32[]{:S(2)}) %collective-permute-start.3) | collective-permute-done | bytes 1048608 | tf_op jit(solution)/shard_map/ppermute | solution.py:42
  52.9 0.0 copy-done
  52.9 0.0 copy-start.1
  52.9 1.0 copy-done.1
  53.9 11.2 %shard_map.47 = bf16[1280,1024]{1,0:T(8,128)(2,1)} custom-call(s32[70]{0:T(128)} %reshape.14.offsets_ref, s32[70]{0:T(128)} %reshape.15.mask_ref, bf16[10,7,128,128]{3,2,1,0:T(8,128)(2,1)} %pad_maximum_fusion.ops_ref, bf16[256,2048]{1,0:T(8,128)(2,1)} %copy-done.1, bf16[1280,2048]{1,0:T(8,128)(2,1)} %basis_ref.3, bf16[256,2048]{1,0:T(8,128)(2,1)} %copy-done), custom_call_target="tpu_custom_call" | custom-call | flops 2348810240 | bytes 11010048 | tf_op jit(solution)/shard_map/pallas_call | solution.py:276
  65.1 0.0 slice-start
  65.1 11.3 %shard_map.46 = bf16[1280,1024]{1,0:T(8,128)(2,1)} custom-call(s32[70]{0:T(128)} %reshape.14.offsets_ref, s32[70]{0:T(128)} %reshape.15.mask_ref, bf16[10,7,128,128]{3,2,1,0:T(8,128)(2,1)} %pad_maximum_fusion.ops_ref, bf16[256,2048]{1,0:T(8,128)(2,1)} %copy-done.1, bf16[1280,2048]{1,0:T(8,128)(2,1)} %basis_ref.3, bf16[256,2048]{1,0:T(8,128)(2,1)} %copy-done), custom_call_target="tpu_custom_call" | custom-call | flops 2348810240 | bytes 11010048 | tf_op jit(solution)/shard_map/pallas_call | solution.py:276
  76.4 0.0 slice-start.1
  76.4 0.0 copy-start.2
  76.4 0.0 collective-permute-done
  76.4 10.9 %convolution_multiply_fusion = f32[2048,1024]{1,0:T(8,128)} fusion(bf16[1280,1024]{1,0:T(8,128)(2,1)} %shard_map.47, bf16[1280,2048]{1,0:T(8,128)(2,1)} %basis_ref.3, bf16[1280,2048]{1,0:T(8,128)(2,1)} %collective-permute-done, pred[]{:T(512)S(6)} %eq.10), kind=kOutput, calls=%fused_computation.1 | convolution fusion | flops 5373427712 | bytes 21495808 | tf_op jit(solution)/shard_map/dot_general | solution.py:327
  87.3 0.0 slice-done
  87.3 0.0 slice-done.1
  87.3 0.0 copy-done.2
  87.3 8.2 %convolution_multiply_fusion.1 = f32[2048,1024]{1,0:T(8,128)} fusion(bf16[1280,1024]{1,0:T(8,128)(2,1)S(1)} %copy-done.2, bf16[1280,2048]{1,0:T(8,128)(2,1)S(1)} %bitcast.7, bf16[1280,2048]{1,0:T(8,128)(2,1)} %collective-permute-done, pred[]{:T(512)S(6)} %eq.10), kind=kOutput, calls=%fused_computation.2 | convolution fusion | flops 5373427712 | bytes 21495808 | tf_op jit(solution)/shard_map/dot_general | solution.py:327
  95.5 122.1 %shard_map.48 = (f32[256,1024]{1,0:T(8,128)}, f32[256,1024]{1,0:T(8,128)}) custom-call(f32[8,256,1024]{2,1,0:T(8,128)} %bitcast.9, f32[8,4,64,1024]{3,2,1,0:T(8,128)} %bitcast.8), custom_call_target="tpu_custom_call" | custom-call | tf_op jit(solution)/shard_map/pallas_call | solution.py:205
  217.6 33.2 %shard_map.49 = (f32[32,1024]{1,0:T(8,128)}, f32[32,1024]{1,0:T(8,128)}) custom-call(f32[4,64,1024]{2,1,0:T(8,128)} %bitcast.10, f32[8,32,1024]{2,1,0:T(8,128)} %bitcast.11), custom_call_target="tpu_custom_call" | custom-call | tf_op jit(solution)/shard_map/pallas_call | solution.py:205
  250.8 1.7 pad_maximum_fusion.1
  (2 shorter events, 0.0 us)
Async XLA Ops:
  0.0 76.4 %collective-permute-start = (bf16[1280,2048]{1,0:T(8,128)(2,1)}, bf16[1280,2048]{1,0:T(8,128)(2,1)}, u32[]{:S(2)}, u32[]{:S(2)}) collective-permute-start(bf16[1280,2048]{1,0:T(8,128)(2,1)} %basis_ref.3), channel_id=1, source_target_pairs={{0,1},{1,0},{2,3},{3,2},{4,5},{5,4},{6,7},{7,6},{8,9},{9,8},{10,11... | collective-permute-start | bytes 15728648 | tf_op jit(solution)/shard_map/ppermute | solution.py:309
  0.0 28.2 %copy-start.5 = (s32[10,7]{0,1:T(8,128)S(1)}, s32[10,7]{0,1:T(8,128)}, u32[]{:S(2)}) copy-start(s32[10,7]{0,1:T(8,128)} %param.6) | copy-start | bytes 844
  0.0 28.9 %copy-start.4 = (s32[10,7]{0,1:T(8,128)S(1)}, s32[10,7]{0,1:T(8,128)}, u32[]{:S(2)}) copy-start(s32[10,7]{0,1:T(8,128)} %param.7) | copy-start | bytes 844
  0.0 29.6 %copy-start.3 = (bf16[10,7,64,128]{3,2,1,0:T(8,128)(2,1)S(1)}, bf16[10,7,64,128]{3,2,1,0:T(8,128)(2,1)}, u32[]{:S(2)}) copy-start(bf16[10,7,64,128]{3,2,1,0:T(8,128)(2,1)} %param.5) | copy-start | bytes 3440644
  1.2 17.1 %collective-permute-start.1 = (bf16[5,7,64,128]{3,2,1,0:T(8,128)(2,1)S(1)}, bf16[5,7,64,128]{3,2,1,0:T(8,128)(2,1)}, u32[]{:S(2)}, u32[]{:S(2)}) collective-permute-start(bf16[5,7,64,128]{3,2,1,0:T(8,128)(2,1)S(1)} %constant_dynamic-slice_fusion), channel_id=1, source_target_pairs={{0,128},{128,0},{1,129},{129,1},{2,130},{130,2},{3,131},{131,3},{4... | collective-permute-start | bytes 1720328 | tf_op jit(solution)/shard_map/ppermute | solution.py:298
  18.3 11.3 %collective-permute-start.2 = (bf16[5,7,64,128]{3,2,1,0:T(8,128)(2,1)}, bf16[5,7,64,128]{3,2,1,0:T(8,128)(2,1)}, u32[]{:S(2)}, u32[]{:S(2)}) collective-permute-start(bf16[5,7,64,128]{3,2,1,0:T(8,128)(2,1)} %collective-permute-done.1), channel_id=1, source_target_pairs={{0,1},{1,0},{2,3},{3,2},{4,5},{5,4},{6,7},{7,6},{8,9},{9,8},{10,11... | collective-permute-start | bytes 1720328 | tf_op jit(solution)/shard_map/ppermute | solution.py:299
  21.4 28.6 %collective-permute-start.4 = (bf16[256,2048]{1,0:T(8,128)(2,1)}, bf16[256,2048]{1,0:T(8,128)(2,1)S(1)}, u32[]{:S(2)}, u32[]{:S(2)}) collective-permute-start(bf16[256,2048]{1,0:T(8,128)(2,1)} %get-tuple-element.13), channel_id=1, source_target_pairs={{2,0},{132,2},{6,4},{136,6},{10,8},{140,10},{14,12},{144,14},{18,1... | collective-permute-start | bytes 3145736 | tf_op jit(solution)/shard_map/ppermute | solution.py:43
  25.5 27.4 %collective-permute-start.3 = (bf16[256,2048]{1,0:T(8,128)(2,1)}, bf16[256,2048]{1,0:T(8,128)(2,1)S(1)}, u32[]{:S(2)}, u32[]{:S(2)}) collective-permute-start(bf16[256,2048]{1,0:T(8,128)(2,1)} %get-tuple-element.14), channel_id=1, source_target_pairs={{0,2},{130,4},{4,6},{134,8},{8,10},{138,12},{12,14},{142,16},{16,1... | collective-permute-start | bytes 3145736 | tf_op jit(solution)/shard_map/ppermute | solution.py:42
  50.0 2.9 %copy-start = (bf16[256,2048]{1,0:T(8,128)(2,1)}, bf16[256,2048]{1,0:T(8,128)(2,1)S(1)}, u32[]{:S(2)}) copy-start(bf16[256,2048]{1,0:T(8,128)(2,1)S(1)} %collective-permute-done.4.after_ref) | copy-start | bytes 3145732
  52.9 1.0 copy-start.1
  65.1 22.2 %slice-start = ((s8[5242880]{0:T(1024)(128)(4,1)}), s8[1048576]{0:T(1024)(128)(4,1)S(1)}, s32[]{:S(2)}) async-start(s8[5242880]{0:T(1024)(128)(4,1)} %bitcast.6), calls=%async_computation | async-start | bytes 2097152
  76.4 10.9 %slice-start.1 = ((s8[5242880]{0:T(1024)(128)(4,1)}), s8[4194304]{0:T(1024)(128)(4,1)S(1)}, s32[]{:S(2)}) async-start(s8[5242880]{0:T(1024)(128)(4,1)} %bitcast.6), calls=%async_computation.1 | async-start | bytes 8388608
  76.4 10.9 %copy-start.2 = (bf16[1280,1024]{1,0:T(8,128)(2,1)S(1)}, bf16[1280,1024]{1,0:T(8,128)(2,1)}, u32[]{:S(2)}) copy-start(bf16[1280,1024]{1,0:T(8,128)(2,1)} %shard_map.46) | copy-start | bytes 7864324

commit v11 on v8

--- a/solution.py
+++ b/solution.py
@@ -222,28 +222,32 @@
 
 
 def applied_kernel(offsets_ref, mask_ref, ops_ref, ext_ref, out_ref):
-    block = pl.program_id(1)
-    slot_count, block_rows = ops_ref.shape[1], ops_ref.shape[2]
+    block_count, slot_count, block_rows = ops_ref.shape[0], ops_ref.shape[1], ops_ref.shape[2]
     order = [slot for _, slot in sorted(zip(STATIC_OFFSETS, WINDOW_SLOTS))]
-    lhs = jnp.concatenate(
-        [
-            jnp.where(mask_ref[block * slot_count + slot] != 0, ops_ref[0, slot], 0)
-            for slot in order
-        ],
-        axis=1,
-    )
-    first = pl.multiple_of(block * block_rows, block_rows)
-    acc = jnp.dot(
-        lhs, ext_ref[pl.ds(first, len(order) * block_rows), :], preferred_element_type=jnp.float32
-    )
-    for slot in range(len(WINDOW_SLOTS), slot_count):
-        tile_index = offsets_ref[block * slot_count + slot]
-        start = pl.multiple_of(tile_index * block_rows, block_rows)
-        tile = ext_ref[pl.ds(start, block_rows), :]
-        product = jnp.dot(ops_ref[0, slot], tile, preferred_element_type=jnp.float32)
-        live = mask_ref[block * slot_count + slot] != 0
-        acc = acc + jnp.where(live, product, 0.0)
-    out_ref[...] = acc.astype(out_ref.dtype)
+
+    def one_block(block, carry):
+        lhs = jnp.concatenate(
+            [
+                jnp.where(mask_ref[block * slot_count + slot] != 0, ops_ref[block, slot], 0)
+                for slot in order
+            ],
+            axis=1,
+        )
+        first = pl.multiple_of(block * block_rows, block_rows)
+        acc = jnp.dot(
+            lhs, ext_ref[pl.ds(first, len(order) * block_rows), :], preferred_element_type=jnp.float32
+        )
+        for slot in range(len(WINDOW_SLOTS), slot_count):
+            tile_index = offsets_ref[block * slot_count + slot]
+            start = pl.multiple_of(tile_index * block_rows, block_rows)
+            tile = ext_ref[pl.ds(start, block_rows), :]
+            product = jnp.dot(ops_ref[block, slot], tile, preferred_element_type=jnp.float32)
+            live = mask_ref[block * slot_count + slot] != 0
+            acc = acc + jnp.where(live, product, 0.0)
+        out_ref[pl.ds(first, block_rows), :] = acc.astype(out_ref.dtype)
+        return carry
+
+    lax.fori_loop(0, block_count, one_block, 0)
 
 
 def apply_operator(offsets, mask, full_ops, extended, column_start, column_count):
@@ -253,19 +257,19 @@
     skip = column_start // tile
     grid_spec = pltpu.PrefetchScalarGridSpec(
         num_scalar_prefetch=2,
-        grid=(column_count // tile, block_count),
+        grid=(column_count // tile,),
         in_specs=[
-            pl.BlockSpec((1, slot_count, block_rows, block_rows), lambda j, b, *_: (b, 0, 0, 0)),
-            pl.BlockSpec((ext_rows, tile), lambda j, b, *_: (0, j + skip)),
+            pl.BlockSpec((block_count, slot_count, block_rows, block_rows), lambda j, *_: (0, 0, 0, 0)),
+            pl.BlockSpec((ext_rows, tile), lambda j, *_: (0, j + skip)),
         ],
-        out_specs=pl.BlockSpec((block_rows, tile), lambda j, b, *_: (b, j)),
+        out_specs=pl.BlockSpec((block_count * block_rows, tile), lambda j, *_: (0, j)),
     )
     flops = 2 * block_count * slot_count * block_rows * block_rows * column_count
     return pl.pallas_call(
         applied_kernel,
         grid_spec=grid_spec,
         out_shape=jax.ShapeDtypeStruct((block_count * block_rows, column_count), jnp.bfloat16),
-        compiler_params=pltpu.CompilerParams(dimension_semantics=("arbitrary", "arbitrary")),
+        compiler_params=pltpu.CompilerParams(dimension_semantics=("arbitrary",)),
         cost_estimate=pl.CostEstimate(
             flops=flops, bytes_accessed=3 * ext_rows * column_count * 2, transcendentals=0
         ),

time: 249 us -> 247 us (level)
  transfers between devices with their start and end apart: 5 -> 5, of which waited for: 2 -> 2; matrix products, arithmetic and copies ran while one was open for 7% -> 7% of each run, Pallas kernels for 9% -> 8%
where the time goes in v11:
time: 247 us; the launch traced here: 246 us
  Pallas kernels  170 us (69%)
  waiting for transfers between devices  29.5 us (12%)
  matrix products  19.1 us (8%)
  local copies, waits for them, and re-layouts  14 us (6%)
  starting transfers between devices  8.79 us (4%)
  other arithmetic  4.77 us (2%)
    pallas_call x2, Pallas kernels, multi_ring_reduce(): pl.pallas_call(functools.partial(multi_ring_kernel, tuple(plan), tuple(pa...  150 us
    ppermute x1, waiting for transfers between devices, per_device(): from_sec = lax.ppermute(mine, 'sec', [(0, 1), (1, 0)])  21.6 us
    pallas_call x2, Pallas kernels, apply_operator(): pl.pallas_call(applied_kernel, grid_spec=grid_spec, out_shape=jax.ShapeDt...  20.4 us
    dot_general x2, matrix products, per_device(): lax.dot_general(left_projector, applied, (((0,), (0,)), ((), ())), prefer...  19.1 us
    ppermute x1, waiting for transfers between devices, halo(): after = lax.ppermute(shard[:width], axes, after_pairs)  7.88 us
    unnamed x15, local copies, waits for them, and re-layouts  6.95 us
  transfers between devices with their start and end apart: 5, of which 2 were waited for; matrix products, arithmetic and copies ran while one was open for 7% of the time, Pallas kernels for 8%

profile of v11, /device:TPU:8, one launch (start us, length us, event | category | flops | bytes accessed | tf_op | source)
XLA Modules:
  0.0 246.3 jit_solution(15006722645233558000)
XLA Ops:
  0.0 0.0 copy-start.3
  0.0 0.0 copy-start.2
  0.0 0.0 collective-permute-start
  0.0 2.7 %fusion = (bf16[256,2048]{1,0:T(8,128)(2,1)S(1)}, bf16[256,2048]{1,0:T(8,128)(2,1)}) fusion(bf16[1280,2048]{1,0:T(8,128)(2,1)} %param.4), kind=kLoop, calls=%fused_computation.13 | loop fusion | bytes 4194304 | tf_op jit(solution)/shard_map/slice | solution.py:43
  2.7 4.4 %collective-permute-start.3 = (bf16[256,2048]{1,0:T(8,128)(2,1)}, bf16[256,2048]{1,0:T(8,128)(2,1)S(1)}, u32[]{:S(2)}, u32[]{:S(2)}) collective-permute-start(bf16[256,2048]{1,0:T(8,128)(2,1)} %get-tuple-element.14), channel_id=1, source_target_pairs={{0,2},{130,4},{4,6},{134,8},{8,10},{138,12},{12,14},{142,16},{16,1... | collective-permute-start | bytes 3145736 | tf_op jit(solution)/shard_map/ppermute | solution.py:42
  7.2 1.9 constant_dynamic-slice_fusion
  9.1 0.9 collective-permute-start.1
  10.0 3.4 %collective-permute-start.4 = (bf16[256,2048]{1,0:T(8,128)(2,1)S(1)}, bf16[256,2048]{1,0:T(8,128)(2,1)S(1)}, u32[]{:S(2)}, u32[]{:S(2)}) collective-permute-start(bf16[256,2048]{1,0:T(8,128)(2,1)S(1)} %get-tuple-element.13), channel_id=1, source_target_pairs={{2,0},{132,2},{6,4},{136,6},{10,8},{140,10},{14,12},{144,14},{18,1... | collective-permute-start | bytes 3145736 | tf_op jit(solution)/shard_map/ppermute | solution.py:43
  13.5 0.0 copy-done.3
  13.5 0.1 copy.7
  13.6 0.6 reshape.14.offsets_ref
  14.2 0.0 copy-done.2
  14.2 0.1 copy.8
  14.3 0.6 reshape.15.mask_ref
  14.9 21.6 %collective-permute-done.1 = bf16[5,7,64,128]{3,2,1,0:T(8,128)(2,1)} collective-permute-done((bf16[5,7,64,128]{3,2,1,0:T(8,128)(2,1)}, bf16[5,7,64,128]{3,2,1,0:T(8,128)(2,1)}, u32[]{:S(2)}, u32[]{:S(2)}) %collective-permute-start.1) | collective-permute-done | bytes 573472 | tf_op jit(solution)/shard_map/ppermute | solution.py:290
  36.6 0.0 collective-permute-start.2
  36.6 0.0 collective-permute-done.3
  36.6 1.0 constant_dynamic-update-slice_fusion.2
  37.6 0.0 copy-start.1
  37.6 5.8 %constant_dynamic-update-slice_fusion.1 = bf16[1792,2048]{1,0:T(8,128)(2,1)} fusion(bf16[1792,2048]{1,0:T(8,128)(2,1)} %constant_dynamic-update-slice_fusion.2, bf16[1280,2048]{1,0:T(8,128)(2,1)} %param.4), kind=kLoop, calls=%fused_computation.9 | loop fusion | bytes 10485760
  43.4 7.9 %collective-permute-done.4 = bf16[256,2048]{1,0:T(8,128)(2,1)S(1)} collective-permute-done((bf16[256,2048]{1,0:T(8,128)(2,1)S(1)}, bf16[256,2048]{1,0:T(8,128)(2,1)S(1)}, u32[]{:S(2)}, u32[]{:S(2)}) %collective-permute-start.4) | collective-permute-done | bytes 1048608 | tf_op jit(solution)/shard_map/ppermute | solution.py:43
  51.3 1.1 constant_dynamic-update-slice_fusion.ext_ref
  52.3 0.0 collective-permute-done.2
  52.4 0.0 copy-done.1
  52.4 1.5 broadcast_select_fusion.4
  53.8 1.6 pad_maximum_fusion.ops_ref
  55.4 10.1 %shard_map.47 = bf16[1280,1024]{1,0:T(8,128)(2,1)} custom-call(s32[70]{0:T(128)} %reshape.14.offsets_ref, s32[70]{0:T(128)} %reshape.15.mask_ref, bf16[10,7,128,128]{3,2,1,0:T(8,128)(2,1)} %pad_maximum_fusion.ops_ref, bf16[1792,2048]{1,0:T(8,128)(2,1)} %constant_dynamic-update-slice_fusion.ext_ref), custom_call_target="tpu_custom_call" | custom-call | flops 2348810240 | bytes 11010048 | tf_op jit(solution)/shard_map/pallas_call | solution.py:268
  65.5 0.0 slice-start
  65.5 10.3 %shard_map.46 = bf16[1280,1024]{1,0:T(8,128)(2,1)} custom-call(s32[70]{0:T(128)} %reshape.14.offsets_ref, s32[70]{0:T(128)} %reshape.15.mask_ref, bf16[10,7,128,128]{3,2,1,0:T(8,128)(2,1)} %pad_maximum_fusion.ops_ref, bf16[1792,2048]{1,0:T(8,128)(2,1)} %constant_dynamic-update-slice_fusion.ext_ref), custom_call_target="tpu_custom_call" | custom-call | flops 2348810240 | bytes 11010048 | tf_op jit(solution)/shard_map/pallas_call | solution.py:268
  75.8 0.0 slice-start.1
  75.8 0.0 copy-start
  75.8 0.0 collective-permute-done
  75.8 10.9 %convolution_multiply_fusion.1 = f32[2048,1024]{1,0:T(8,128)} fusion(bf16[1280,1024]{1,0:T(8,128)(2,1)} %shard_map.46, bf16[1280,2048]{1,0:T(8,128)(2,1)} %param.4, bf16[1280,2048]{1,0:T(8,128)(2,1)} %collective-permute-done, pred[]{:T(512)S(6)} %eq.10), kind=kOutput, calls=%fused_computation.2 | convolution fusion | flops 5373427712 | bytes 21495808 | tf_op jit(solution)/shard_map/dot_general | solution.py:319
  86.7 0.0 slice-done
  86.7 0.0 slice-done.1
  86.7 0.0 copy-done
  86.7 8.2 %convolution_multiply_fusion = f32[2048,1024]{1,0:T(8,128)} fusion(bf16[1280,1024]{1,0:T(8,128)(2,1)S(1)} %copy-done, bf16[1280,2048]{1,0:T(8,128)(2,1)S(1)} %bitcast.7, bf16[1280,2048]{1,0:T(8,128)(2,1)} %collective-permute-done, pred[]{:T(512)S(6)} %eq.10), kind=kOutput, calls=%fused_computation.1 | convolution fusion | flops 5373427712 | bytes 21495808 | tf_op jit(solution)/shard_map/dot_general | solution.py:319
  94.9 117.8 %shard_map.48 = (f32[256,1024]{1,0:T(8,128)}, f32[256,1024]{1,0:T(8,128)}) custom-call(f32[8,256,1024]{2,1,0:T(8,128)} %bitcast.8, f32[8,4,64,1024]{3,2,1,0:T(8,128)} %bitcast.9), custom_call_target="tpu_custom_call" | custom-call | tf_op jit(solution)/shard_map/pallas_call | solution.py:205
  212.7 31.9 %shard_map.49 = (f32[32,1024]{1,0:T(8,128)}, f32[32,1024]{1,0:T(8,128)}) custom-call(f32[4,64,1024]{2,1,0:T(8,128)} %bitcast.10, f32[8,32,1024]{2,1,0:T(8,128)} %bitcast.11), custom_call_target="tpu_custom_call" | custom-call | tf_op jit(solution)/shard_map/pallas_call | solution.py:205
  244.6 1.7 pad_maximum_fusion.1
  (2 shorter events, 0.0 us)
Async XLA Ops:
  0.0 13.5 %copy-start.3 = (s32[10,7]{0,1:T(8,128)S(1)}, s32[10,7]{0,1:T(8,128)}, u32[]{:S(2)}) copy-start(s32[10,7]{0,1:T(8,128)} %param.6) | copy-start | bytes 844
  0.0 14.2 %copy-start.2 = (s32[10,7]{0,1:T(8,128)S(1)}, s32[10,7]{0,1:T(8,128)}, u32[]{:S(2)}) copy-start(s32[10,7]{0,1:T(8,128)} %param.7) | copy-start | bytes 844
  0.0 75.8 %collective-permute-start = (bf16[1280,2048]{1,0:T(8,128)(2,1)}, bf16[1280,2048]{1,0:T(8,128)(2,1)}, u32[]{:S(2)}, u32[]{:S(2)}) collective-permute-start(bf16[1280,2048]{1,0:T(8,128)(2,1)} %param.4), channel_id=1, source_target_pairs={{0,1},{1,0},{2,3},{3,2},{4,5},{5,4},{6,7},{7,6},{8,9},{9,8},{10,11... | collective-permute-start | bytes 15728648 | tf_op jit(solution)/shard_map/ppermute | solution.py:301
  2.7 33.8 %collective-permute-start.3 = (bf16[256,2048]{1,0:T(8,128)(2,1)}, bf16[256,2048]{1,0:T(8,128)(2,1)S(1)}, u32[]{:S(2)}, u32[]{:S(2)}) collective-permute-start(bf16[256,2048]{1,0:T(8,128)(2,1)} %get-tuple-element.14), channel_id=1, source_target_pairs={{0,2},{130,4},{4,6},{134,8},{8,10},{138,12},{12,14},{142,16},{16,1... | collective-permute-start | bytes 3145736 | tf_op jit(solution)/shard_map/ppermute | solution.py:42
  9.1 27.5 %collective-permute-start.1 = (bf16[5,7,64,128]{3,2,1,0:T(8,128)(2,1)}, bf16[5,7,64,128]{3,2,1,0:T(8,128)(2,1)}, u32[]{:S(2)}, u32[]{:S(2)}) collective-permute-start(bf16[5,7,64,128]{3,2,1,0:T(8,128)(2,1)} %constant_dynamic-slice_fusion), channel_id=1, source_target_pairs={{0,128},{128,0},{1,129},{129,1},{2,130},{130,2},{3,131},{131,3},{4... | collective-permute-start | bytes 1720328 | tf_op jit(solution)/shard_map/ppermute | solution.py:290
  10.0 41.2 %collective-permute-start.4 = (bf16[256,2048]{1,0:T(8,128)(2,1)S(1)}, bf16[256,2048]{1,0:T(8,128)(2,1)S(1)}, u32[]{:S(2)}, u32[]{:S(2)}) collective-permute-start(bf16[256,2048]{1,0:T(8,128)(2,1)S(1)} %get-tuple-element.13), channel_id=1, source_target_pairs={{2,0},{132,2},{6,4},{136,6},{10,8},{140,10},{14,12},{144,14},{18,1... | collective-permute-start | bytes 3145736 | tf_op jit(solution)/shard_map/ppermute | solution.py:43
  36.6 15.8 %collective-permute-start.2 = (bf16[5,7,64,128]{3,2,1,0:T(8,128)(2,1)}, bf16[5,7,64,128]{3,2,1,0:T(8,128)(2,1)S(1)}, u32[]{:S(2)}, u32[]{:S(2)}) collective-permute-start(bf16[5,7,64,128]{3,2,1,0:T(8,128)(2,1)} %collective-permute-done.1), channel_id=1, source_target_pairs={{0,1},{1,0},{2,3},{3,2},{4,5},{5,4},{6,7},{7,6},{8,9},{9,8},{10,11... | collective-permute-start | bytes 1720328 | tf_op jit(solution)/shard_map/ppermute | solution.py:291
  37.6 14.7 %copy-start.1 = (bf16[10,7,64,128]{3,2,1,0:T(8,128)(2,1)S(1)}, bf16[10,7,64,128]{3,2,1,0:T(8,128)(2,1)}, u32[]{:S(2)}) copy-start(bf16[10,7,64,128]{3,2,1,0:T(8,128)(2,1)} %param.5) | copy-start | bytes 3440644
  65.5 21.2 %slice-start = ((s8[5242880]{0:T(1024)(128)(4,1)}), s8[1048576]{0:T(1024)(128)(4,1)S(1)}, s32[]{:S(2)}) async-start(s8[5242880]{0:T(1024)(128)(4,1)} %bitcast.6), calls=%async_computation | async-start | bytes 2097152
  75.8 10.9 %slice-start.1 = ((s8[5242880]{0:T(1024)(128)(4,1)}), s8[4194304]{0:T(1024)(128)(4,1)S(1)}, s32[]{:S(2)}) async-start(s8[5242880]{0:T(1024)(128)(4,1)} %bitcast.6), calls=%async_computation.1 | async-start | bytes 8388608
  75.8 10.9 %copy-start = (bf16[1280,1024]{1,0:T(8,128)(2,1)S(1)}, bf16[1280,1024]{1,0:T(8,128)(2,1)}, u32[]{:S(2)}) copy-start(bf16[1280,1024]{1,0:T(8,128)(2,1)} %shard_map.47) | copy-start | bytes 7864324

commit v12 on v11

--- a/solution.py
+++ b/solution.py
@@ -247,7 +247,7 @@
         out_ref[pl.ds(first, block_rows), :] = acc.astype(out_ref.dtype)
         return carry
 
-    lax.fori_loop(0, block_count, one_block, 0)
+    lax.fori_loop(0, block_count, one_block, 0, unroll=True)
 
 
 def apply_operator(offsets, mask, full_ops, extended, column_start, column_count):

time: 247 us -> 244 us (0.988)
  Pallas kernels: 170 us -> 167 us
    pallas_call x2, Pallas kernels: 20.4 us -> 17.4 us  [apply_operator(): pl.pallas_call(applied_kernel, grid_spec=grid_spec, out_shape=jax.ShapeDt...]
  transfers between devices with their start and end apart: 5 -> 5, of which waited for: 2 -> 2; matrix products, arithmetic and copies ran while one was open for 7% -> 7% of each run, Pallas kernels for 8% -> 7%
where the time goes in v12:
time: 244 us
  Pallas kernels  167 us (68%)
  waiting for transfers between devices  29.5 us (12%)
  matrix products  19.3 us (8%)
  local copies, waits for them, and re-layouts  14 us (6%)
  starting transfers between devices  8.79 us (4%)
  other arithmetic  4.77 us (2%)
    pallas_call x2, Pallas kernels, multi_ring_reduce(): pl.pallas_call(functools.partial(multi_ring_kernel, tuple(plan), tuple(pa...  150 us
    ppermute x1, waiting for transfers between devices, per_device(): from_sec = lax.ppermute(mine, 'sec', [(0, 1), (1, 0)])  21.6 us
    dot_general x2, matrix products, per_device(): lax.dot_general(left_projector, applied, (((0,), (0,)), ((), ())), prefer...  19.3 us
    pallas_call x2, Pallas kernels, apply_operator(): pl.pallas_call(applied_kernel, grid_spec=grid_spec, out_shape=jax.ShapeDt...  17.4 us
    ppermute x1, waiting for transfers between devices, halo(): after = lax.ppermute(shard[:width], axes, after_pairs)  7.88 us
    unnamed x15, local copies, waits for them, and re-layouts  6.95 us
  transfers between devices with their start and end apart: 5, of which 2 were waited for; matrix products, arithmetic and copies ran while one was open for 7% of the time, Pallas kernels for 7%

profile of v12, /device:TPU:8, one launch (start us, length us, event | category | flops | bytes accessed | tf_op | source)
XLA Modules:
  0.0 243.6 jit_solution(14131507665622009851)
XLA Ops:
  0.0 0.0 copy-start.3
  0.0 0.0 copy-start.2
  0.0 0.0 collective-permute-start
  0.0 2.7 %fusion = (bf16[256,2048]{1,0:T(8,128)(2,1)S(1)}, bf16[256,2048]{1,0:T(8,128)(2,1)}) fusion(bf16[1280,2048]{1,0:T(8,128)(2,1)} %param.4), kind=kLoop, calls=%fused_computation.13 | loop fusion | bytes 4194304 | tf_op jit(solution)/shard_map/slice | solution.py:43
  2.7 4.4 %collective-permute-start.3 = (bf16[256,2048]{1,0:T(8,128)(2,1)}, bf16[256,2048]{1,0:T(8,128)(2,1)S(1)}, u32[]{:S(2)}, u32[]{:S(2)}) collective-permute-start(bf16[256,2048]{1,0:T(8,128)(2,1)} %get-tuple-element.14), channel_id=1, source_target_pairs={{0,2},{130,4},{4,6},{134,8},{8,10},{138,12},{12,14},{142,16},{16,1... | collective-permute-start | bytes 3145736 | tf_op jit(solution)/shard_map/ppermute | solution.py:42
  7.2 1.9 constant_dynamic-slice_fusion
  9.1 0.9 collective-permute-start.1
  10.0 3.4 %collective-permute-start.4 = (bf16[256,2048]{1,0:T(8,128)(2,1)S(1)}, bf16[256,2048]{1,0:T(8,128)(2,1)S(1)}, u32[]{:S(2)}, u32[]{:S(2)}) collective-permute-start(bf16[256,2048]{1,0:T(8,128)(2,1)S(1)} %get-tuple-element.13), channel_id=1, source_target_pairs={{2,0},{132,2},{6,4},{136,6},{10,8},{140,10},{14,12},{144,14},{18,1... | collective-permute-start | bytes 3145736 | tf_op jit(solution)/shard_map/ppermute | solution.py:43
  13.5 0.0 copy-done.3
  13.5 0.1 copy.7
  13.6 0.6 reshape.14.offsets_ref
  14.2 0.0 copy-done.2
  14.2 0.1 copy.8
  14.3 0.6 reshape.15.mask_ref
  14.9 21.6 %collective-permute-done.1 = bf16[5,7,64,128]{3,2,1,0:T(8,128)(2,1)} collective-permute-done((bf16[5,7,64,128]{3,2,1,0:T(8,128)(2,1)}, bf16[5,7,64,128]{3,2,1,0:T(8,128)(2,1)}, u32[]{:S(2)}, u32[]{:S(2)}) %collective-permute-start.1) | collective-permute-done | bytes 573472 | tf_op jit(solution)/shard_map/ppermute | solution.py:290
  36.6 0.0 collective-permute-start.2
  36.6 0.0 collective-permute-done.3
  36.6 1.0 constant_dynamic-update-slice_fusion.2
  37.6 0.0 copy-start.1
  37.6 5.8 %constant_dynamic-update-slice_fusion.1 = bf16[1792,2048]{1,0:T(8,128)(2,1)} fusion(bf16[1792,2048]{1,0:T(8,128)(2,1)} %constant_dynamic-update-slice_fusion.2, bf16[1280,2048]{1,0:T(8,128)(2,1)} %param.4), kind=kLoop, calls=%fused_computation.9 | loop fusion | bytes 10485760
  43.4 7.9 %collective-permute-done.4 = bf16[256,2048]{1,0:T(8,128)(2,1)S(1)} collective-permute-done((bf16[256,2048]{1,0:T(8,128)(2,1)S(1)}, bf16[256,2048]{1,0:T(8,128)(2,1)S(1)}, u32[]{:S(2)}, u32[]{:S(2)}) %collective-permute-start.4) | collective-permute-done | bytes 1048608 | tf_op jit(solution)/shard_map/ppermute | solution.py:43
  51.3 1.1 constant_dynamic-update-slice_fusion.ext_ref
  52.3 0.0 collective-permute-done.2
  52.4 0.0 copy-done.1
  52.4 1.5 broadcast_select_fusion.4
  53.8 1.6 pad_maximum_fusion.ops_ref
  55.4 8.6 %shard_map.47 = bf16[1280,1024]{1,0:T(8,128)(2,1)} custom-call(s32[70]{0:T(128)} %reshape.14.offsets_ref, s32[70]{0:T(128)} %reshape.15.mask_ref, bf16[10,7,128,128]{3,2,1,0:T(8,128)(2,1)} %pad_maximum_fusion.ops_ref, bf16[1792,2048]{1,0:T(8,128)(2,1)} %constant_dynamic-update-slice_fusion.ext_ref), custom_call_target="tpu_custom_call" | custom-call | flops 2348810240 | bytes 11010048 | tf_op jit(solution)/shard_map/pallas_call | solution.py:268
  64.0 0.0 slice-start
  64.0 8.8 %shard_map.46 = bf16[1280,1024]{1,0:T(8,128)(2,1)} custom-call(s32[70]{0:T(128)} %reshape.14.offsets_ref, s32[70]{0:T(128)} %reshape.15.mask_ref, bf16[10,7,128,128]{3,2,1,0:T(8,128)(2,1)} %pad_maximum_fusion.ops_ref, bf16[1792,2048]{1,0:T(8,128)(2,1)} %constant_dynamic-update-slice_fusion.ext_ref), custom_call_target="tpu_custom_call" | custom-call | flops 2348810240 | bytes 11010048 | tf_op jit(solution)/shard_map/pallas_call | solution.py:268
  72.8 0.0 slice-start.1
  72.8 0.0 copy-start
  72.8 0.0 collective-permute-done
  72.8 11.0 %convolution_multiply_fusion.1 = f32[2048,1024]{1,0:T(8,128)} fusion(bf16[1280,1024]{1,0:T(8,128)(2,1)} %shard_map.46, bf16[1280,2048]{1,0:T(8,128)(2,1)} %param.4, bf16[1280,2048]{1,0:T(8,128)(2,1)} %collective-permute-done, pred[]{:T(512)S(6)} %eq.10), kind=kOutput, calls=%fused_computation.2 | convolution fusion | flops 5373427712 | bytes 21495808 | tf_op jit(solution)/shard_map/dot_general | solution.py:319
  83.9 0.0 slice-done
  83.9 0.0 slice-done.1
  83.9 0.0 copy-done
  83.9 8.2 %convolution_multiply_fusion = f32[2048,1024]{1,0:T(8,128)} fusion(bf16[1280,1024]{1,0:T(8,128)(2,1)S(1)} %copy-done, bf16[1280,2048]{1,0:T(8,128)(2,1)S(1)} %bitcast.7, bf16[1280,2048]{1,0:T(8,128)(2,1)} %collective-permute-done, pred[]{:T(512)S(6)} %eq.10), kind=kOutput, calls=%fused_computation.1 | convolution fusion | flops 5373427712 | bytes 21495808 | tf_op jit(solution)/shard_map/dot_general | solution.py:319
  92.1 117.6 %shard_map.48 = (f32[256,1024]{1,0:T(8,128)}, f32[256,1024]{1,0:T(8,128)}) custom-call(f32[8,256,1024]{2,1,0:T(8,128)} %bitcast.8, f32[8,4,64,1024]{3,2,1,0:T(8,128)} %bitcast.9), custom_call_target="tpu_custom_call" | custom-call | tf_op jit(solution)/shard_map/pallas_call | solution.py:205
  209.7 32.1 %shard_map.49 = (f32[32,1024]{1,0:T(8,128)}, f32[32,1024]{1,0:T(8,128)}) custom-call(f32[4,64,1024]{2,1,0:T(8,128)} %bitcast.10, f32[8,32,1024]{2,1,0:T(8,128)} %bitcast.11), custom_call_target="tpu_custom_call" | custom-call | tf_op jit(solution)/shard_map/pallas_call | solution.py:205
  241.9 1.7 pad_maximum_fusion.1
  (2 shorter events, 0.0 us)
Async XLA Ops:
  0.0 13.5 %copy-start.3 = (s32[10,7]{0,1:T(8,128)S(1)}, s32[10,7]{0,1:T(8,128)}, u32[]{:S(2)}) copy-start(s32[10,7]{0,1:T(8,128)} %param.6) | copy-start | bytes 844
  0.0 14.2 %copy-start.2 = (s32[10,7]{0,1:T(8,128)S(1)}, s32[10,7]{0,1:T(8,128)}, u32[]{:S(2)}) copy-start(s32[10,7]{0,1:T(8,128)} %param.7) | copy-start | bytes 844
  0.0 72.8 %collective-permute-start = (bf16[1280,2048]{1,0:T(8,128)(2,1)}, bf16[1280,2048]{1,0:T(8,128)(2,1)}, u32[]{:S(2)}, u32[]{:S(2)}) collective-permute-start(bf16[1280,2048]{1,0:T(8,128)(2,1)} %param.4), channel_id=1, source_target_pairs={{0,1},{1,0},{2,3},{3,2},{4,5},{5,4},{6,7},{7,6},{8,9},{9,8},{10,11... | collective-permute-start | bytes 15728648 | tf_op jit(solution)/shard_map/ppermute | solution.py:301
  2.7 33.8 %collective-permute-start.3 = (bf16[256,2048]{1,0:T(8,128)(2,1)}, bf16[256,2048]{1,0:T(8,128)(2,1)S(1)}, u32[]{:S(2)}, u32[]{:S(2)}) collective-permute-start(bf16[256,2048]{1,0:T(8,128)(2,1)} %get-tuple-element.14), channel_id=1, source_target_pairs={{0,2},{130,4},{4,6},{134,8},{8,10},{138,12},{12,14},{142,16},{16,1... | collective-permute-start | bytes 3145736 | tf_op jit(solution)/shard_map/ppermute | solution.py:42
  9.1 27.5 %collective-permute-start.1 = (bf16[5,7,64,128]{3,2,1,0:T(8,128)(2,1)}, bf16[5,7,64,128]{3,2,1,0:T(8,128)(2,1)}, u32[]{:S(2)}, u32[]{:S(2)}) collective-permute-start(bf16[5,7,64,128]{3,2,1,0:T(8,128)(2,1)} %constant_dynamic-slice_fusion), channel_id=1, source_target_pairs={{0,128},{128,0},{1,129},{129,1},{2,130},{130,2},{3,131},{131,3},{4... | collective-permute-start | bytes 1720328 | tf_op jit(solution)/shard_map/ppermute | solution.py:290
  10.0 41.2 %collective-permute-start.4 = (bf16[256,2048]{1,0:T(8,128)(2,1)S(1)}, bf16[256,2048]{1,0:T(8,128)(2,1)S(1)}, u32[]{:S(2)}, u32[]{:S(2)}) collective-permute-start(bf16[256,2048]{1,0:T(8,128)(2,1)S(1)} %get-tuple-element.13), channel_id=1, source_target_pairs={{2,0},{132,2},{6,4},{136,6},{10,8},{140,10},{14,12},{144,14},{18,1... | collective-permute-start | bytes 3145736 | tf_op jit(solution)/shard_map/ppermute | solution.py:43
  36.6 15.8 %collective-permute-start.2 = (bf16[5,7,64,128]{3,2,1,0:T(8,128)(2,1)}, bf16[5,7,64,128]{3,2,1,0:T(8,128)(2,1)S(1)}, u32[]{:S(2)}, u32[]{:S(2)}) collective-permute-start(bf16[5,7,64,128]{3,2,1,0:T(8,128)(2,1)} %collective-permute-done.1), channel_id=1, source_target_pairs={{0,1},{1,0},{2,3},{3,2},{4,5},{5,4},{6,7},{7,6},{8,9},{9,8},{10,11... | collective-permute-start | bytes 1720328 | tf_op jit(solution)/shard_map/ppermute | solution.py:291
  37.6 14.7 %copy-start.1 = (bf16[10,7,64,128]{3,2,1,0:T(8,128)(2,1)S(1)}, bf16[10,7,64,128]{3,2,1,0:T(8,128)(2,1)}, u32[]{:S(2)}) copy-start(bf16[10,7,64,128]{3,2,1,0:T(8,128)(2,1)} %param.5) | copy-start | bytes 3440644
  64.0 19.8 %slice-start = ((s8[5242880]{0:T(1024)(128)(4,1)}), s8[1048576]{0:T(1024)(128)(4,1)S(1)}, s32[]{:S(2)}) async-start(s8[5242880]{0:T(1024)(128)(4,1)} %bitcast.6), calls=%async_computation | async-start | bytes 2097152
  72.8 11.0 %slice-start.1 = ((s8[5242880]{0:T(1024)(128)(4,1)}), s8[4194304]{0:T(1024)(128)(4,1)S(1)}, s32[]{:S(2)}) async-start(s8[5242880]{0:T(1024)(128)(4,1)} %bitcast.6), calls=%async_computation.1 | async-start | bytes 8388608
  72.8 11.0 %copy-start = (bf16[1280,1024]{1,0:T(8,128)(2,1)S(1)}, bf16[1280,1024]{1,0:T(8,128)(2,1)}, u32[]{:S(2)}) copy-start(bf16[1280,1024]{1,0:T(8,128)(2,1)} %shard_map.47) | copy-start | bytes 7864324
